TPU v7x, 512 devices: a whole 4x4x16 slice. The times are simulated.
512 devices in a mesh: grp: 16 (over z), seq: 32 (over x, y, core).
Axes of the slice: x: 4, y: 4, z: 16, core: 2. Of those that a mesh axis runs over, the one named last changes fastest.
Arguments:
- queries: bfloat16 [16, 8192, 2048], P('grp', 'seq'), may hold values from -24 to 24
- grad_out: bfloat16 [16, 8192, 2048], P('grp', 'seq'), may hold values from -6 to 6
- neighbour_keys: bfloat16 [16, 32, 128, 2048], P('grp', 'seq'), may hold values from -6 to 6
- neighbour_values: bfloat16 [16, 32, 128, 2048], P('grp', 'seq'), may hold values from -6 to 6
- neighbours: int32 [16, 128, 4], P('grp', 'seq'), may hold values from 0 to 15, all different within a row; in each aligned block of 4 rows (0 to 3, 4 to 7, ..., all dimensions but the last counted through in order) no two rows name the same one
Outputs:
- grad_windows: bfloat16 [16, 128, 64, 2048], P('grp', 'seq')
- grad_keys: bfloat16 [16, 32, 128, 2048], P('grp', 'seq')
- grad_values: bfloat16 [16, 32, 128, 2048], P('grp', 'seq')
Inputs may be any that keep to these rules, and one draw needn't show every extreme that they name: `neighbours`: the 4 groups of a span differ; among the 4 spans of one device no group is named more than 1 times, and that many is reached.
All inputs are finite; a program needn't handle non-finite values.
Results may differ from a plain program's by a relative error of at most 0.015.
The roundings to bfloat16 on the way count: a program that leaves them out, or rounds other values in their place, can miss the bound.
Values may be sent and summed in bfloat16 or wider, within the bound.
A program may use at most 64 MiB of HBM per device.

v0:
```python
import jax
import jax.numpy as jnp
from jax import lax
from jax.sharding import PartitionSpec as P

HEAD = 128
SPAN = 64
NBRS = 4


def from_behind(array, axis, by):
    length = lax.axis_size(axis)
    pairs = [(i, i + by) for i in range(length) if 0 <= i + by < length]
    return lax.ppermute(array, axis, pairs)


def split_heads(block_rows):
    return block_rows.reshape(block_rows.shape[:-1] + (block_rows.shape[-1] // HEAD, HEAD))


def owner_forward(query_block, grad_block, key_heads, value_heads):
    query_heads = split_heads(query_block)
    scores = jnp.einsum(
        "nqhd,khd->nqhk", query_heads, key_heads, preferred_element_type=jnp.float32
    ) * HEAD ** (-0.5)
    row_max = jnp.max(scores, axis=-1)
    exp_scores = jnp.exp(scores - row_max[..., None])
    row_total = jnp.sum(exp_scores, axis=-1)
    partial_value = (
        jnp.einsum(
            "nqhk,khd->nqhd",
            exp_scores.astype(jnp.bfloat16),
            value_heads,
            preferred_element_type=jnp.float32,
        )
        / row_total[..., None]
    )
    dotted = jnp.sum(split_heads(grad_block).astype(jnp.float32) * partial_value, axis=-1)
    return (row_max, row_total, dotted)


def owner_backward(query_block, grad_block, log_block, delta_block, key_heads, value_heads):
    query_heads = split_heads(query_block)
    grad_heads = split_heads(grad_block)
    scores = jnp.einsum(
        "nqhd,khd->nqhk", query_heads, key_heads, preferred_element_type=jnp.float32
    ) * HEAD ** (-0.5)
    probabilities = jnp.exp(scores - log_block[..., None])
    grad_probs = jnp.einsum(
        "nqhd,khd->nqhk", grad_heads, value_heads, preferred_element_type=jnp.float32
    )
    grad_scores = (probabilities * (grad_probs - delta_block[..., None])).astype(jnp.bfloat16)
    grad_query = (
        jnp.einsum("nqhk,khd->nqhd", grad_scores, key_heads, preferred_element_type=jnp.float32)
        * HEAD ** (-0.5)
    ).astype(jnp.bfloat16)
    value_term = jnp.einsum(
        "nqhk,nqhd->khd",
        probabilities.astype(jnp.bfloat16),
        grad_heads,
        preferred_element_type=jnp.float32,
    )
    key_term = jnp.einsum(
        "nqhk,nqhd->khd", grad_scores, query_heads, preferred_element_type=jnp.float32
    )
    return (grad_query.reshape(query_block.shape), key_term, value_term)


def shards(queries, grad_out, neighbour_keys, neighbour_values, neighbours):
    groups = lax.axis_size("grp")
    span_len = SPAN
    tok_rows = queries.shape[1]
    row_width = queries.shape[2]
    head_count = row_width // HEAD
    neighbour_len = neighbour_keys.shape[2]
    span_count = tok_rows // span_len
    pair_count = span_count * NBRS
    capacity = (pair_count + groups - 1) // groups
    slot_count = groups * capacity
    score_scale = HEAD ** (-0.5)
    next_query, next_grad = from_behind(
        (queries[0, : span_len - 1], grad_out[0, : span_len - 1]), "seq", -1
    )
    window_query = jnp.concatenate([queries[0, span_len - 1 :], next_query], axis=0).reshape(
        span_count, span_len, row_width
    )
    window_grad = jnp.concatenate([grad_out[0, span_len - 1 :], next_grad], axis=0).reshape(
        span_count, span_len, row_width
    )
    owner_ids = neighbours[0].reshape(pair_count)
    group_ids = jnp.arange(groups, dtype=jnp.int32)
    owner_hits = (owner_ids[:, None] == group_ids[None, :]).astype(jnp.int32)
    earlier = jnp.cumsum(owner_hits, axis=0) - owner_hits
    slot_rank = jnp.sum(earlier * owner_hits, axis=1)
    slot_of = owner_ids * capacity + slot_rank
    slot_ids = jnp.arange(slot_count, dtype=jnp.int32)
    placement = (slot_of[None, :] == slot_ids[:, None]).astype(jnp.int32)
    slot_live = jnp.sum(placement, axis=1)
    slot_span = (
        jnp.sum(placement * jnp.arange(pair_count, dtype=jnp.int32)[None, :], axis=1) // NBRS
    )
    live_rows = slot_live[:, None, None] > 0
    send_query = jnp.where(
        live_rows, window_query[slot_span], jnp.zeros((), queries.dtype)
    ).reshape(groups, capacity, span_len, row_width)
    send_grad = jnp.where(live_rows, window_grad[slot_span], jnp.zeros((), grad_out.dtype)).reshape(
        groups, capacity, span_len, row_width
    )
    send_flags = slot_live.reshape(groups, capacity)
    recv_query, recv_grad, recv_flags = (
        lax.all_to_all(send_query, "grp", split_axis=0, concat_axis=0, tiled=True),
        lax.all_to_all(send_grad, "grp", split_axis=0, concat_axis=0, tiled=True),
        lax.all_to_all(send_flags, "grp", split_axis=0, concat_axis=0, tiled=True),
    )
    key_heads = split_heads(neighbour_keys[0, 0])
    value_heads = split_heads(neighbour_values[0, 0])
    flat_query = recv_query.reshape(slot_count, span_len, row_width)
    flat_grad = recv_grad.reshape(slot_count, span_len, row_width)
    flat_flags = recv_flags.reshape(slot_count)
    block_size = 8
    block_count = slot_count // block_size

    def forward_block(pieces):
        return owner_forward(pieces[0], pieces[1], key_heads, value_heads)

    stat_max, stat_total, stat_dot = lax.map(
        forward_block,
        (
            flat_query.reshape(block_count, block_size, span_len, row_width),
            flat_grad.reshape(block_count, block_size, span_len, row_width),
        ),
    )
    stat_shape = (groups, capacity, span_len, head_count)
    back_max, back_total, back_dot = (
        lax.all_to_all(
            stat_max.reshape(stat_shape), "grp", split_axis=0, concat_axis=0, tiled=True
        ),
        lax.all_to_all(
            stat_total.reshape(stat_shape), "grp", split_axis=0, concat_axis=0, tiled=True
        ),
        lax.all_to_all(
            stat_dot.reshape(stat_shape), "grp", split_axis=0, concat_axis=0, tiled=True
        ),
    )
    pair_shape = (span_count, NBRS, span_len, head_count)
    pair_max = back_max.reshape(slot_count, span_len, head_count)[slot_of].reshape(pair_shape)
    pair_total = back_total.reshape(slot_count, span_len, head_count)[slot_of].reshape(pair_shape)
    pair_dot = back_dot.reshape(slot_count, span_len, head_count)[slot_of].reshape(pair_shape)
    top_max = jnp.max(pair_max, axis=1, keepdims=True)
    weights = pair_total * jnp.exp(pair_max - top_max)
    weight_sum = jnp.sum(weights, axis=1)
    log_total = top_max[:, 0] + jnp.log(weight_sum)
    delta_rows = jnp.sum(weights * pair_dot, axis=1) / weight_sum
    live_stats = slot_live[:, None, None] > 0
    send_log = jnp.where(live_stats, log_total[slot_span], 0.0).reshape(stat_shape)
    send_delta = jnp.where(live_stats, delta_rows[slot_span], 0.0).reshape(stat_shape)
    recv_log, recv_delta = (
        lax.all_to_all(send_log, "grp", split_axis=0, concat_axis=0, tiled=True),
        lax.all_to_all(send_delta, "grp", split_axis=0, concat_axis=0, tiled=True),
    )
    flat_log = recv_log.reshape(slot_count, span_len, head_count)
    flat_delta = recv_delta.reshape(slot_count, span_len, head_count)
    zero_sum = jnp.zeros((neighbour_len, head_count, HEAD), jnp.float32)

    def backward_block(carried, pieces):
        grad_query, key_term, value_term = owner_backward(
            pieces[0], pieces[1], pieces[2], pieces[3], key_heads, value_heads
        )
        return ((carried[0] + key_term, carried[1] + value_term), grad_query)

    block_inputs = (
        flat_query.reshape(block_count, block_size, span_len, row_width),
        flat_grad.reshape(block_count, block_size, span_len, row_width),
        flat_log.reshape(block_count, block_size, span_len, head_count),
        flat_delta.reshape(block_count, block_size, span_len, head_count),
    )
    sums, grad_blocks = lax.scan(backward_block, (zero_sum, zero_sum), block_inputs)
    key_sum, value_sum = sums
    slot_grads = grad_blocks.reshape(slot_count, span_len, row_width)
    grad_reply = jnp.where(flat_flags[:, None, None] > 0, slot_grads, jnp.zeros((), jnp.bfloat16))
    back_grad = lax.all_to_all(
        grad_reply.reshape(groups, capacity, span_len, row_width),
        "grp",
        split_axis=0,
        concat_axis=0,
        tiled=True,
    )
    pair_grad = back_grad.reshape(slot_count, span_len, row_width)[slot_of].reshape(
        span_count, NBRS, span_len, row_width
    )
    grad_windows = (
        jnp.sum(pair_grad.astype(jnp.float32), axis=1)
        .astype(jnp.bfloat16)
        .reshape(1, span_count, span_len, row_width)
    )
    grad_keys = (key_sum * score_scale).astype(jnp.bfloat16).reshape(1, 1, neighbour_len, row_width)
    grad_values = value_sum.astype(jnp.bfloat16).reshape(1, 1, neighbour_len, row_width)
    return (grad_windows, grad_keys, grad_values)


def solution(mesh):
    in_specs = (
        P("grp", "seq", None),
        P("grp", "seq", None),
        P("grp", "seq", None, None),
        P("grp", "seq", None, None),
        P("grp", "seq", None),
    )
    out_specs = (
        P("grp", "seq", None, None),
        P("grp", "seq", None, None),
        P("grp", "seq", None, None),
    )
    return jax.shard_map(shards, mesh=mesh, in_specs=in_specs, out_specs=out_specs, check_vma=False)
```

profile of v0, /device:TPU:6, one launch (start us, length us, event | category | flops | bytes accessed | tf_op | source)
XLA Modules:
  0.0 793.0 jit_solution(17074718106347072738)
XLA Ops:
  0.6 1.0 slice_bitcast_fusion.2
  1.6 4.6 collective-permute-start.1
  6.3 1.0 slice_bitcast_fusion.3
  7.2 2.6 collective-permute-start
  9.8 1.3 slice_bitcast_fusion.1
  11.2 1.3 slice_bitcast_fusion
  13.1 1.1 pad_maximum_fusion.1
  14.2 2.8 gather_fusion.1
  17.1 2.7 gather_fusion
  19.9 6.1 bitcast_select_fusion
  25.9 201.5 %all_to_all.49 = bf16[16,1,64,2048]{3,2,1,0:T(8,128)(2,1)} all-to-all(bf16[16,1,64,2048]{3,2,1,0:T(8,128)(2,1)S(1)} %get-tuple-element.254), channel_id=1, replica_groups=mesh['grp'=16,'seq'=32] {'grp'}, dimensions={0} | all-to-all | bytes 8388608 | tf_op jit(solution)/shard_map/all_to_all | solution.py:112
  227.4 6.5 all-to-all-start.1
  235.1 181.1 %all-to-all-done.1 = bf16[16,1,64,2048]{3,2,1,0:T(8,128)(2,1)} async-done(((bf16[16,1,64,2048]{3,2,1,0:T(8,128)(2,1)}), bf16[16,1,64,2048]{3,2,1,0:T(8,128)(2,1)}, u32[]{:S(2)}, u32[]{:S(2)}) %all-to-all-start.1) | async-done | bytes 4194336 | tf_op jit(solution)/shard_map/all_to_all | solution.py:111
  416.2 27.5 %while.29 = (s32[]{:T(128)}, f32[2,8,64,16]{2,3,1,0:T(8,128)S(1)}, f32[2,8,64,16]{2,3,1,0:T(8,128)S(1)}, f32[2,8,64,16]{2,3,1,0:T(8,128)S(1)}, bf16[2,8,64,2048]...) while((s32[]{:T(128)}, f32[2,8,64,16]{2,3,1,0:T(8,128)S(1)}, ...), condition=%wide.region_8.9_spmd, body=%wide.region_4.8_spmd.sunk | while | flops 549429248 | bytes 43581556 | solution.py:126
  416.2 2.8 dynamic-slice_convert_fusion.2
  419.7 0.9 copy.149
  420.6 1.5 bitcast_reduce_fusion.4
  422.1 2.4 fusion.78
  424.4 5.4 fusion.79
  430.0 2.8 dynamic-slice_convert_fusion.2
  433.4 0.9 copy.149
  434.3 1.5 bitcast_reduce_fusion.4
  435.8 2.4 fusion.78
  438.2 5.4 fusion.79
  443.7 0.8 reshape.321
  444.5 10.5 %all-to-all-start.6 = ((f32[16,1,1024]{2,1,0:T(1,128)}), f32[16,1,1024]{2,1,0:T(1,128)S(1)}, u32[]{:S(2)}, u32[]{:S(2)}) async-start(f32[16,1,1024]{2,1,0:T(1,128)} %reshape.321), calls=%async_computation.6 | async-start | bytes 131072 | tf_op jit(solution)/shard_map/all_to_all | solution.py:141
  455.0 0.8 reshape.317
  455.8 12.2 %all-to-all-done.6 = f32[16,1,1024]{2,1,0:T(1,128)S(1)} async-done(((f32[16,1,1024]{2,1,0:T(1,128)}), f32[16,1,1024]{2,1,0:T(1,128)S(1)}, u32[]{:S(2)}, u32[]{:S(2)}) %all-to-all-start.6) | async-done | bytes 65568 | tf_op jit(solution)/shard_map/all_to_all | solution.py:141
  468.0 3.5 all-to-all-start.3
  474.3 9.9 %all-to-all-done.3 = f32[16,1,1024]{2,1,0:T(1,128)S(1)} async-done(((f32[16,1,1024]{2,1,0:T(1,128)}), f32[16,1,1024]{2,1,0:T(1,128)S(1)}, u32[]{:S(2)}, u32[]{:S(2)}) %all-to-all-start.3) | async-done | bytes 65568 | tf_op jit(solution)/shard_map/all_to_all | solution.py:135
  484.3 3.5 all-to-all-start.4
  489.8 10.7 %all-to-all-done.4 = f32[16,1,1024]{2,1,0:T(1,128)S(1)} async-done(((f32[16,1,1024]{2,1,0:T(1,128)}), f32[16,1,1024]{2,1,0:T(1,128)S(1)}, u32[]{:S(2)}, u32[]{:S(2)}) %all-to-all-start.4) | async-done | bytes 65568 | tf_op jit(solution)/shard_map/all_to_all | solution.py:138
  500.5 3.5 all-to-all-start
  507.5 8.8 %all-to-all-done = s32[16,1,1]{2,1,0:T(1,128)S(1)} async-done(((s32[16,1,1]{2,1,0:T(1,128)}), s32[16,1,1]{2,1,0:T(1,128)S(1)}, u32[]{:S(2)}, u32[]{:S(2)}) %all-to-all-start) | async-done | bytes 96 | tf_op jit(solution)/shard_map/all_to_all | solution.py:113
  516.3 3.5 all-to-all-start.7
  519.8 0.8 reshape.323
  520.6 12.0 %all-to-all-done.7 = f32[16,1,1024]{2,1,0:T(1,128)S(1)} async-done(((f32[16,1,1024]{2,1,0:T(1,128)}), f32[16,1,1024]{2,1,0:T(1,128)S(1)}, u32[]{:S(2)}, u32[]{:S(2)}) %all-to-all-start.7) | async-done | bytes 65568 | tf_op jit(solution)/shard_map/all_to_all | solution.py:159
  532.5 3.7 all-to-all-start.5
  536.6 0.8 reduce.7
  537.5 11.3 %all-to-all-done.5 = f32[16,1,1024]{2,1,0:T(1,128)S(1)} async-done(((f32[16,1,1024]{2,1,0:T(1,128)}), f32[16,1,1024]{2,1,0:T(1,128)S(1)}, u32[]{:S(2)}, u32[]{:S(2)}) %all-to-all-start.5) | async-done | bytes 65568 | tf_op jit(solution)/shard_map/all_to_all | solution.py:158
  549.6 45.8 %while.30 = (s32[]{:T(128)}, f32[128,16,128]{0,2,1:T(8,128)}, f32[128,16,128]{0,2,1:T(8,128)}, bf16[2,8,64,2048]{3,2,1,0:T(8,128)(2,1)}, bf16[2,8,64,2048]{3,2,1...) while((s32[]{:T(128)}, f32[128,16,128]{0,2,1:T(8,128)}, ...), condition=%wide.region_13.14_spmd.clone, body=%wide.region_12.13_spmd.clone.sunk | while | flops 1353711616 | bytes 64848016 | solution.py:177
  549.7 2.7 constant_dynamic-slice_fusion.7
  554.4 4.0 fusion.93
  558.4 2.7 fusion.91
  561.1 2.4 fusion.92
  564.2 2.8 copy.158
  567.0 2.8 broadcast_in_dim.99
  569.8 1.5 constant_dynamic-update-slice_fusion.2
  571.4 2.7 constant_dynamic-slice_fusion.7
  576.2 5.1 fusion.93
  581.3 2.7 fusion.91
  584.0 3.7 fusion.92
  588.3 2.8 copy.158
  591.1 2.8 broadcast_in_dim.99
  593.9 1.4 constant_dynamic-update-slice_fusion.2
  595.4 4.5 broadcast_select_fusion
  599.9 4.5 all-to-all-start.8
  604.4 1.4 multiply_convert_fusion.1
  605.8 1.0 copy.81
  606.8 1.3 convert_element_type.38
  608.1 1.0 copy.82
  609.1 174.6 %all-to-all-done.8 = bf16[16,1,64,2048]{3,2,1,0:T(8,128)(2,1)} async-done(((bf16[16,1,64,2048]{3,2,1,0:T(8,128)(2,1)}), bf16[16,1,64,2048]{3,2,1,0:T(8,128)(2,1)}, u32[]{:S(2)}, u32[]{:S(2)}) %all-to-all-start.8) | async-done | bytes 4194336 | tf_op jit(solution)/shard_map/all_to_all | solution.py:181
  783.7 5.0 gather_fusion.7
  788.7 4.3 bitcast_reduce_fusion.1
  (79 shorter events, 18.2 us)
Async XLA Ops:
  0.6 11.9 %copy-start.2 = (s32[1,4,4]{2,1,0:T(4,128)S(1)}, s32[1,4,4]{2,1,0:T(4,128)}, u32[]{:S(2)}) copy-start(s32[1,4,4]{2,1,0:T(4,128)} %param.13) | copy-start | bytes 196
  1.6 11.5 %collective-permute-start.1 = (bf16[63,2048]{1,0:T(8,128)(2,1)S(1)}, bf16[63,2048]{1,0:T(8,128)(2,1)}, u32[]{:S(2)}, u32[]{:S(2)}) collective-permute-start(bf16[63,2048]{1,0:T(8,128)(2,1)S(1)} %slice_bitcast_fusion.2), channel_id=1, source_target_pairs={{1,0},{2,1},{3,2},{4,3},{5,4},{6,5},{7,6},{8,7},{9,8},{10,9},{11,1... | collective-permute-start | bytes 774152 | tf_op jit(solution)/shard_map/ppermute | solution.py:14
  7.2 9.8 %collective-permute-start = (bf16[63,2048]{1,0:T(8,128)(2,1)S(1)}, bf16[63,2048]{1,0:T(8,128)(2,1)S(1)}, u32[]{:S(2)}, u32[]{:S(2)}) collective-permute-start(bf16[63,2048]{1,0:T(8,128)(2,1)S(1)} %slice_bitcast_fusion.3), channel_id=1, source_target_pairs={{1,0},{2,1},{3,2},{4,3},{5,4},{6,5},{7,6},{8,7},{9,8},{10,9},{11,1... | collective-permute-start | bytes 774152 | tf_op jit(solution)/shard_map/ppermute | solution.py:14
  227.4 6.5 copy-start
  227.4 7.1 copy-start.1
  227.4 188.8 %all-to-all-start.1 = ((bf16[16,1,64,2048]{3,2,1,0:T(8,128)(2,1)}), bf16[16,1,64,2048]{3,2,1,0:T(8,128)(2,1)}, u32[]{:S(2)}, u32[]{:S(2)}) async-start(bf16[16,1,64,2048]{3,2,1,0:T(8,128)(2,1)} %get-tuple-element.255), calls=%async_computation.1 | async-start | bytes 8388608 | tf_op jit(solution)/shard_map/all_to_all | solution.py:111
  444.5 23.5 %all-to-all-start.6 = ((f32[16,1,1024]{2,1,0:T(1,128)}), f32[16,1,1024]{2,1,0:T(1,128)S(1)}, u32[]{:S(2)}, u32[]{:S(2)}) async-start(f32[16,1,1024]{2,1,0:T(1,128)} %reshape.321), calls=%async_computation.6 | async-start | bytes 131072 | tf_op jit(solution)/shard_map/all_to_all | solution.py:141
  468.0 16.3 %all-to-all-start.3 = ((f32[16,1,1024]{2,1,0:T(1,128)}), f32[16,1,1024]{2,1,0:T(1,128)S(1)}, u32[]{:S(2)}, u32[]{:S(2)}) async-start(f32[16,1,1024]{2,1,0:T(1,128)} %reshape.317), calls=%async_computation.3 | async-start | bytes 131072 | tf_op jit(solution)/shard_map/all_to_all | solution.py:135
  484.3 16.3 %all-to-all-start.4 = ((f32[16,1,1024]{2,1,0:T(1,128)}), f32[16,1,1024]{2,1,0:T(1,128)S(1)}, u32[]{:S(2)}, u32[]{:S(2)}) async-start(f32[16,1,1024]{2,1,0:T(1,128)} %reshape.319), calls=%async_computation.4 | async-start | bytes 131072 | tf_op jit(solution)/shard_map/all_to_all | solution.py:138
  500.5 15.8 %all-to-all-start = ((s32[16,1,1]{2,1,0:T(1,128)}), s32[16,1,1]{2,1,0:T(1,128)S(1)}, u32[]{:S(2)}, u32[]{:S(2)}) async-start(s32[16,1,1]{2,1,0:T(1,128)} %copy.61), calls=%async_computation | async-start | bytes 16384 | tf_op jit(solution)/shard_map/all_to_all | solution.py:113
  516.3 16.2 %all-to-all-start.7 = ((f32[16,1,1024]{2,1,0:T(1,128)}), f32[16,1,1024]{2,1,0:T(1,128)S(1)}, u32[]{:S(2)}, u32[]{:S(2)}) async-start(f32[16,1,1024]{2,1,0:T(1,128)} %reshape.325), calls=%async_computation.7 | async-start | bytes 131072 | tf_op jit(solution)/shard_map/all_to_all | solution.py:159
  532.5 16.2 %all-to-all-start.5 = ((f32[16,1,1024]{2,1,0:T(1,128)}), f32[16,1,1024]{2,1,0:T(1,128)S(1)}, u32[]{:S(2)}, u32[]{:S(2)}) async-start(f32[16,1,1024]{2,1,0:T(1,128)} %reshape.323), calls=%async_computation.5 | async-start | bytes 131072 | tf_op jit(solution)/shard_map/all_to_all | solution.py:158
  599.9 183.8 %all-to-all-start.8 = ((bf16[16,1,64,2048]{3,2,1,0:T(8,128)(2,1)}), bf16[16,1,64,2048]{3,2,1,0:T(8,128)(2,1)}, u32[]{:S(2)}, u32[]{:S(2)}) async-start(bf16[16,1,64,2048]{3,2,1,0:T(8,128)(2,1)} %broadcast_select_fusion), calls=%async_computation.8 | async-start | bytes 8388608 | tf_op jit(solution)/shard_map/all_to_all | solution.py:181
where the time goes:
time: 794 us; the launch traced here: 793 us
  waiting for transfers between devices  421 us (53%)
  blocking collectives  201 us (25%)
  local copies, waits for them, and re-layouts  52.2 us (7%)
  starting transfers between devices  46.4 us (6%)
  matrix products  37.1 us (5%)
  other arithmetic  33.9 us (4%)
    all_to_all x1, blocking collectives, shards(): lax.all_to_all(send_grad, 'grp', split_axis=0, concat_axis=0, tiled=True)  201 us
    all_to_all x1, waiting for transfers between devices, shards(): lax.all_to_all(send_query, 'grp', split_axis=0, concat_axis=0, tiled=True)  181 us
    all_to_all x1, waiting for transfers between devices, shards(): lax.all_to_all(grad_reply.reshape(groups, capacity, span_len, row_width),...  175 us
  transfers between devices with their start and end apart: 10, of which 8 were waited for; matrix products, arithmetic and copies ran while one was open for 3% of the time, Pallas kernels for 0%

commit v1 on v0

v1 whole, which is shorter than its diff:
```python
import jax
import jax.numpy as jnp
from jax import lax
from jax.sharding import PartitionSpec as P

HEAD = 128
SPAN = 64
NBRS = 4
CHUNKS = 4


def from_behind(array, axis, by):
    length = lax.axis_size(axis)
    pairs = [(i, i + by) for i in range(length) if 0 <= i + by < length]
    return lax.ppermute(array, axis, pairs)


def split_heads(block_rows):
    return block_rows.reshape(block_rows.shape[:-1] + (block_rows.shape[-1] // HEAD, HEAD))


def slot_forward(query_block, grad_block, key_heads, value_heads):
    query_heads = split_heads(query_block)
    scores = jnp.einsum(
        "nqhd,nkhd->nqhk", query_heads, key_heads, preferred_element_type=jnp.float32
    ) * HEAD ** (-0.5)
    row_max = jnp.max(scores, axis=-1)
    exp_scores = jnp.exp(scores - row_max[..., None])
    row_total = jnp.sum(exp_scores, axis=-1)
    partial_value = (
        jnp.einsum(
            "nqhk,nkhd->nqhd",
            exp_scores.astype(jnp.bfloat16),
            value_heads,
            preferred_element_type=jnp.float32,
        )
        / row_total[..., None]
    )
    dotted = jnp.sum(split_heads(grad_block).astype(jnp.float32) * partial_value, axis=-1)
    return (row_max, row_total, dotted)


def slot_backward(query_block, grad_block, log_block, delta_block, key_heads, value_heads):
    query_heads = split_heads(query_block)
    grad_heads = split_heads(grad_block)
    scores = jnp.einsum(
        "nqhd,nkhd->nqhk", query_heads, key_heads, preferred_element_type=jnp.float32
    ) * HEAD ** (-0.5)
    probabilities = jnp.exp(scores - log_block[..., None])
    grad_probs = jnp.einsum(
        "nqhd,nkhd->nqhk", grad_heads, value_heads, preferred_element_type=jnp.float32
    )
    grad_scores = (probabilities * (grad_probs - delta_block[..., None])).astype(jnp.bfloat16)
    grad_query = (
        jnp.einsum("nqhk,nkhd->nqhd", grad_scores, key_heads, preferred_element_type=jnp.float32)
        * HEAD ** (-0.5)
    ).astype(jnp.bfloat16)
    value_term = jnp.einsum(
        "nqhk,nqhd->nkhd",
        probabilities.astype(jnp.bfloat16),
        grad_heads,
        preferred_element_type=jnp.float32,
    )
    key_term = jnp.einsum(
        "nqhk,nqhd->nkhd", grad_scores, query_heads, preferred_element_type=jnp.float32
    )
    return (grad_query.reshape(query_block.shape), key_term, value_term)


def shards(queries, grad_out, neighbour_keys, neighbour_values, neighbours):
    groups = lax.axis_size("grp")
    span_len = SPAN
    tok_rows = queries.shape[1]
    row_width = queries.shape[2]
    neighbour_len = neighbour_keys.shape[2]
    span_count = tok_rows // span_len
    pair_count = span_count * NBRS
    capacity = (pair_count + groups - 1) // groups
    slot_count = groups * capacity
    score_scale = HEAD ** (-0.5)
    width = row_width // CHUNKS
    head_width = width // HEAD
    next_query, next_grad = from_behind(
        (queries[0, : span_len - 1], grad_out[0, : span_len - 1]), "seq", -1
    )
    window_query = jnp.concatenate([queries[0, span_len - 1 :], next_query], axis=0).reshape(
        span_count, span_len, row_width
    )
    window_grad = jnp.concatenate([grad_out[0, span_len - 1 :], next_grad], axis=0).reshape(
        span_count, span_len, row_width
    )
    owner_ids = neighbours[0].reshape(pair_count)
    group_ids = jnp.arange(groups, dtype=jnp.int32)
    owner_hits = (owner_ids[:, None] == group_ids[None, :]).astype(jnp.int32)
    earlier = jnp.cumsum(owner_hits, axis=0) - owner_hits
    slot_rank = jnp.sum(earlier * owner_hits, axis=1)
    slot_of = owner_ids * capacity + slot_rank
    slot_ids = jnp.arange(slot_count, dtype=jnp.int32)
    placement = (slot_of[None, :] == slot_ids[:, None]).astype(jnp.int32)
    slot_live = jnp.sum(placement, axis=1)
    slot_span = (
        jnp.sum(placement * jnp.arange(pair_count, dtype=jnp.int32)[None, :], axis=1) // NBRS
    )
    live_rows = slot_live[:, None, None] > 0
    slot_query = jnp.where(live_rows, window_query[slot_span], jnp.zeros((), queries.dtype))
    slot_grad = jnp.where(live_rows, window_grad[slot_span], jnp.zeros((), grad_out.dtype))
    key_block = neighbour_keys[0, 0]
    value_block = neighbour_values[0, 0]
    pair_shape = (span_count, NBRS, span_len, head_width)
    window_parts, key_parts, value_parts = [], [], []
    for chunk in range(CHUNKS):
        cols = slice(chunk * width, (chunk + 1) * width)
        key_all = lax.all_gather(key_block[:, cols], "grp", axis=0)
        value_all = lax.all_gather(value_block[:, cols], "grp", axis=0)
        key_heads = split_heads(jnp.repeat(key_all, capacity, axis=0))
        value_heads = split_heads(jnp.repeat(value_all, capacity, axis=0))
        query_part = slot_query[..., cols]
        grad_part = slot_grad[..., cols]
        stat_max, stat_total, stat_dot = slot_forward(query_part, grad_part, key_heads, value_heads)
        pair_max = stat_max[slot_of].reshape(pair_shape)
        pair_total = stat_total[slot_of].reshape(pair_shape)
        pair_dot = stat_dot[slot_of].reshape(pair_shape)
        top_max = jnp.max(pair_max, axis=1, keepdims=True)
        weights = pair_total * jnp.exp(pair_max - top_max)
        weight_sum = jnp.sum(weights, axis=1)
        log_total = top_max[:, 0] + jnp.log(weight_sum)
        delta_rows = jnp.sum(weights * pair_dot, axis=1) / weight_sum
        grad_query, key_term, value_term = slot_backward(
            query_part,
            grad_part,
            log_total[slot_span],
            delta_rows[slot_span],
            key_heads,
            value_heads,
        )
        pair_grad = grad_query[slot_of].reshape(span_count, NBRS, span_len, width)
        window_parts.append(jnp.sum(pair_grad.astype(jnp.float32), axis=1).astype(jnp.bfloat16))
        key_send = (
            jnp.sum(key_term.reshape(groups, capacity, neighbour_len, width), axis=1) * score_scale
        ).astype(jnp.bfloat16)
        value_send = jnp.sum(
            value_term.reshape(groups, capacity, neighbour_len, width), axis=1
        ).astype(jnp.bfloat16)
        key_parts.append(lax.psum_scatter(key_send, "grp", scatter_dimension=0, tiled=True))
        value_parts.append(lax.psum_scatter(value_send, "grp", scatter_dimension=0, tiled=True))
    grad_windows = jnp.concatenate(window_parts, axis=-1).reshape(
        1, span_count, span_len, row_width
    )
    grad_keys = jnp.concatenate(key_parts, axis=-1).reshape(1, 1, neighbour_len, row_width)
    grad_values = jnp.concatenate(value_parts, axis=-1).reshape(1, 1, neighbour_len, row_width)
    return (grad_windows, grad_keys, grad_values)


def solution(mesh):
    in_specs = (
        P("grp", "seq", None),
        P("grp", "seq", None),
        P("grp", "seq", None, None),
        P("grp", "seq", None, None),
        P("grp", "seq", None),
    )
    out_specs = (
        P("grp", "seq", None, None),
        P("grp", "seq", None, None),
        P("grp", "seq", None, None),
    )
    return jax.shard_map(shards, mesh=mesh, in_specs=in_specs, out_specs=out_specs, check_vma=False)
```

time: 794 us -> 1200 us (1.51)
  waiting for transfers between devices: 421 us -> 951 us
  blocking collectives: 201 us -> 0 us
  local copies, waits for them, and re-layouts: 52.2 us -> 111 us
  matrix products: 37.1 us -> 85.7 us
  starting transfers between devices: 46.4 us -> 8.71 us
  between operations: 1.06 us -> 14.7 us
  other arithmetic: 33.9 us -> 21.8 us
    reduce_scatter x0 -> x8, waiting for transfers between devices: none -> 504 us  [the longest x4 294 us: shards(): lax.psum_scatter(value_send, 'grp', scatter_dimension=0, tiled=True)]
    all_gather x0 -> x8, waiting for transfers between devices: none -> 444 us  [the longest x4 240 us: shards(): value_all = lax.all_gather(value_block[:, cols], 'grp', axis=0)]
    all_to_all x8 -> x0, waiting for transfers between devices: 421 us -> none  [the longest x1 181 us: shards(): lax.all_to_all(send_query, 'grp', split_axis=0, concat_axis=0, tiled=True)]
    all_to_all x1 -> x0, blocking collectives: 201 us -> none  [shards(): lax.all_to_all(send_grad, 'grp', split_axis=0, concat_axis=0, tiled=True)]
    dot_general x14 -> x24, matrix products: 37.1 us -> 85.7 us  [the longest x4 18.4 us: slot_backward(): jnp.einsum('nqhd,nkhd->nqhk', grad_heads, value_heads, preferred_element_...]
    all_to_all x8 -> x0, starting transfers between devices: 39.2 us -> none  [the longest x1 10.5 us: shards(): lax.all_to_all(stat_dot.reshape(stat_shape), 'grp', split_axis=0, concat_...]
    another operation x0 -> x8, local copies, waits for them, and re-layouts: none -> 30.4 us  [split_heads(): block_rows.reshape(block_rows.shape[:-1] + (block_rows.shape[-1] // HEAD,...]
    convert_element_type x2 -> x8, local copies, waits for them, and re-layouts: 5.59 us -> 31.4 us  [the longest x4 15.8 us: shards(): value_send = jnp.sum(value_term.reshape(groups, capacity, neighbour_len,...]
  transfers between devices with their start and end apart: 10 -> 18, of which waited for: 8 -> 15; matrix products, arithmetic and copies ran while one was open for 3% -> 17% of each run, Pallas kernels for 0% -> 0%
where the time goes in v1:
time: 1200 us; the launch traced here: 1190 us
  waiting for transfers between devices  951 us (79%)
  local copies, waits for them, and re-layouts  111 us (9%)
  matrix products  85.7 us (7%)
  other arithmetic  21.8 us (2%)
  between operations  14.7 us (1%)
    reduce_scatter x4, waiting for transfers between devices, shards(): lax.psum_scatter(value_send, 'grp', scatter_dimension=0, tiled=True)  294 us
    all_gather x4, waiting for transfers between devices, shards(): value_all = lax.all_gather(value_block[:, cols], 'grp', axis=0)  240 us
    reduce_scatter x4, waiting for transfers between devices, shards(): lax.psum_scatter(key_send, 'grp', scatter_dimension=0, tiled=True)  211 us
    all_gather x4, waiting for transfers between devices, shards(): key_all = lax.all_gather(key_block[:, cols], 'grp', axis=0)  203 us
    another operation x8, local copies, waits for them, and re-layouts, split_heads(): block_rows.reshape(block_rows.shape[:-1] + (block_rows.shape[-1] // HEAD,...  30.4 us
  transfers between devices with their start and end apart: 18, of which 15 were waited for; matrix products, arithmetic and copies ran while one was open for 17% of the time, Pallas kernels for 0%

profile of v1, /device:TPU:6, one launch (start us, length us, event | category | flops | bytes accessed | tf_op | source)
XLA Modules:
  0.0 1192.7 jit_solution(16589479043382345028)
XLA Ops:
  14.5 4.6 collective-permute-start.1
  20.1 2.6 collective-permute-start
  26.1 2.7 gather_fusion.4
  29.0 2.8 gather_fusion
  31.8 4.1 broadcast_select_fusion
  35.9 3.3 slice_bitcast_fusion.6
  39.2 49.1 %all-gather.29.cloned.1.call-done = bf16[2048,512]{1,0:T(8,128)(2,1)} async-done(((bf16[128,512]{1,0:T(8,128)(2,1)}), bf16[2048,512]{1,0:T(8,128)(2,1)}) %all-gather.29.cloned.1.call-update) | async-done | bytes 2097168 | tf_op jit(solution)/shard_map/all_gather | solution.py:113
  88.3 2.5 reshape.529
  90.9 4.1 bitcast_reduce_fusion
  95.6 2.5 fusion.35
  98.7 61.7 %all-gather.31.cloned.1.call-done = bf16[2048,512]{1,0:T(8,128)(2,1)} async-done(((bf16[128,512]{1,0:T(8,128)(2,1)}), bf16[2048,512]{1,0:T(8,128)(2,1)}) %all-gather.31.cloned.1.call-update) | async-done | bytes 2097168 | tf_op jit(solution)/shard_map/all_gather | solution.py:114
  160.4 4.0 reshape.530
  164.4 4.2 fusion.23
  170.4 4.6 fusion.2
  175.1 2.1 multiply_convert_fusion
  177.2 3.9 copy.63
  181.6 51.2 %all-gather.25.cloned.1.call-done = bf16[2048,512]{1,0:T(8,128)(2,1)} async-done(((bf16[128,512]{1,0:T(8,128)(2,1)}), bf16[2048,512]{1,0:T(8,128)(2,1)}) %all-gather.25.cloned.1.call-update) | async-done | bytes 2097168 | tf_op jit(solution)/shard_map/all_gather | solution.py:113
  232.8 4.0 reshape.527
  236.8 4.8 bitcast_reduce_fusion.1
  242.2 2.5 fusion.32
  245.3 59.3 %all-gather.27.cloned.1.call-done = bf16[2048,512]{1,0:T(8,128)(2,1)} async-done(((bf16[128,512]{1,0:T(8,128)(2,1)}), bf16[2048,512]{1,0:T(8,128)(2,1)}) %all-gather.27.cloned.1.call-update) | async-done | bytes 2097168 | tf_op jit(solution)/shard_map/all_gather | solution.py:114
  304.6 4.0 reshape.528
  308.6 4.2 fusion.22
  314.7 4.6 fusion.7
  319.3 2.1 multiply_convert_fusion.1
  321.4 3.9 copy.61
  325.4 51.2 %all-gather.21.cloned.1.call-done = bf16[2048,512]{1,0:T(8,128)(2,1)} async-done(((bf16[128,512]{1,0:T(8,128)(2,1)}), bf16[2048,512]{1,0:T(8,128)(2,1)}) %all-gather.21.cloned.1.call-update) | async-done | bytes 2097168 | tf_op jit(solution)/shard_map/all_gather | solution.py:113
  376.6 4.0 reshape.525
  380.6 4.8 bitcast_reduce_fusion.2
  386.0 2.5 fusion.29
  389.1 59.5 %all-gather.23.cloned.1.call-done = bf16[2048,512]{1,0:T(8,128)(2,1)} async-done(((bf16[128,512]{1,0:T(8,128)(2,1)}), bf16[2048,512]{1,0:T(8,128)(2,1)}) %all-gather.23.cloned.1.call-update) | async-done | bytes 2097168 | tf_op jit(solution)/shard_map/all_gather | solution.py:114
  448.7 4.0 reshape.526
  452.6 4.2 fusion.21
  458.7 4.6 fusion.12
  463.3 2.1 multiply_convert_fusion.2
  465.5 3.9 copy.59
  469.6 51.8 %all-gather.17.cloned.1.call-done = bf16[2048,512]{1,0:T(8,128)(2,1)} async-done(((bf16[128,512]{1,0:T(8,128)(2,1)}), bf16[2048,512]{1,0:T(8,128)(2,1)}) %all-gather.17.cloned.1.call-update) | async-done | bytes 2097168 | tf_op jit(solution)/shard_map/all_gather | solution.py:113
  521.4 4.0 reshape.523
  525.4 4.5 bitcast_reduce_fusion.3
  530.5 2.5 fusion.26
  533.6 60.0 %all-gather.19.cloned.1.call-done = bf16[2048,512]{1,0:T(8,128)(2,1)} async-done(((bf16[128,512]{1,0:T(8,128)(2,1)}), bf16[2048,512]{1,0:T(8,128)(2,1)}) %all-gather.19.cloned.1.call-update) | async-done | bytes 2097168 | tf_op jit(solution)/shard_map/all_gather | solution.py:114
  593.6 4.0 reshape.524
  597.6 4.2 fusion.20
  603.7 4.6 fusion.17
  608.3 2.1 multiply_convert_fusion.3
  610.4 3.9 copy.57
  615.5 4.3 convolution_convert_fusion
  619.8 3.9 copy.71
  625.0 4.4 convolution_convert_fusion.1
  629.3 3.9 copy.69
  634.5 4.4 convolution_convert_fusion.2
  638.8 3.9 copy.67
  644.0 4.4 convolution_convert_fusion.3
  648.4 3.9 copy.65
  660.4 2.8 gather_fusion.19
  666.3 2.9 gather_fusion.13
  672.2 3.0 gather_fusion.7
  677.7 62.9 %reduce-scatter.13.cloned.1.call-done = bf16[1,128,512]{2,1,0:T(8,128)(2,1)} async-done(((bf16[16,128,512]{2,1,0:T(8,128)(2,1)}), bf16[1,128,512]{2,1,0:T(8,128)(2,1)}) %reduce-scatter.13.cloned.1.call-update) | async-done | bytes 131088 | tf_op jit(solution)/shard_map/reduce_scatter | solution.py:144
  740.6 74.1 %reduce-scatter.11.cloned.1.call-done = bf16[1,128,512]{2,1,0:T(8,128)(2,1)} async-done(((bf16[16,128,512]{2,1,0:T(8,128)(2,1)}), bf16[1,128,512]{2,1,0:T(8,128)(2,1)}) %reduce-scatter.11.cloned.1.call-update) | async-done | bytes 131088 | tf_op jit(solution)/shard_map/reduce_scatter | solution.py:144
  814.7 73.7 %reduce-scatter.9.cloned.1.call-done = bf16[1,128,512]{2,1,0:T(8,128)(2,1)} async-done(((bf16[16,128,512]{2,1,0:T(8,128)(2,1)}), bf16[1,128,512]{2,1,0:T(8,128)(2,1)}) %reduce-scatter.9.cloned.1.call-update) | async-done | bytes 131088 | tf_op jit(solution)/shard_map/reduce_scatter | solution.py:144
  890.4 72.1 %reduce-scatter.23.cloned.1.call-done = bf16[1,128,512]{2,1,0:T(8,128)(2,1)} async-done(((bf16[16,128,512]{2,1,0:T(8,128)(2,1)}), bf16[1,128,512]{2,1,0:T(8,128)(2,1)}) %reduce-scatter.23.cloned.1.call-update) | async-done | bytes 131088 | tf_op jit(solution)/shard_map/reduce_scatter | solution.py:145
  962.4 73.8 %reduce-scatter.21.cloned.1.call-done = bf16[1,128,512]{2,1,0:T(8,128)(2,1)} async-done(((bf16[16,128,512]{2,1,0:T(8,128)(2,1)}), bf16[1,128,512]{2,1,0:T(8,128)(2,1)}) %reduce-scatter.21.cloned.1.call-update) | async-done | bytes 131088 | tf_op jit(solution)/shard_map/reduce_scatter | solution.py:145
  1036.2 73.9 %reduce-scatter.19.cloned.1.call-done = bf16[1,128,512]{2,1,0:T(8,128)(2,1)} async-done(((bf16[16,128,512]{2,1,0:T(8,128)(2,1)}), bf16[1,128,512]{2,1,0:T(8,128)(2,1)}) %reduce-scatter.19.cloned.1.call-update) | async-done | bytes 131088 | tf_op jit(solution)/shard_map/reduce_scatter | solution.py:145
  1110.1 73.9 %reduce-scatter.17.cloned.1.call-done = bf16[1,128,512]{2,1,0:T(8,128)(2,1)} async-done(((bf16[16,128,512]{2,1,0:T(8,128)(2,1)}), bf16[1,128,512]{2,1,0:T(8,128)(2,1)}) %reduce-scatter.17.cloned.1.call-update) | async-done | bytes 131088 | tf_op jit(solution)/shard_map/reduce_scatter | solution.py:145
  (143 shorter events, 49.8 us)
Async XLA Ops:
  7.2 7.3 copy-start.18
  7.2 81.1 %all-gather.29.cloned.1.call-start = ((), (), s32[]{:S(2)}) async-start(), calls=%async_computation.22 | async-start | bytes 2228224 | tf_op jit(solution)/shard_map/all_gather | solution.py:113
  9.2 151.2 %all-gather.31.cloned.1.call-start = ((), (), s32[]{:S(2)}) async-start(), calls=%async_computation.23 | async-start | bytes 2228224 | tf_op jit(solution)/shard_map/all_gather | solution.py:114
  11.2 221.6 %all-gather.25.cloned.1.call-start = ((), (), s32[]{:S(2)}) async-start(), calls=%async_computation.20 | async-start | bytes 2228224 | tf_op jit(solution)/shard_map/all_gather | solution.py:113
  11.9 292.7 %all-gather.27.cloned.1.call-start = ((), (), s32[]{:S(2)}) async-start(), calls=%async_computation.21 | async-start | bytes 2228224 | tf_op jit(solution)/shard_map/all_gather | solution.py:114
  12.5 364.1 %all-gather.21.cloned.1.call-start = ((), (), s32[]{:S(2)}) async-start(), calls=%async_computation.18 | async-start | bytes 2228224 | tf_op jit(solution)/shard_map/all_gather | solution.py:113
  13.1 435.6 %all-gather.23.cloned.1.call-start = ((), (), s32[]{:S(2)}) async-start(), calls=%async_computation.19 | async-start | bytes 2228224 | tf_op jit(solution)/shard_map/all_gather | solution.py:114
  13.7 507.7 %all-gather.17.cloned.1.call-start = ((), (), s32[]{:S(2)}) async-start(), calls=%async_computation.16 | async-start | bytes 2228224 | tf_op jit(solution)/shard_map/all_gather | solution.py:113
  14.4 579.2 %all-gather.19.cloned.1.call-start = ((), (), s32[]{:S(2)}) async-start(), calls=%async_computation.17 | async-start | bytes 2228224 | tf_op jit(solution)/shard_map/all_gather | solution.py:114
  14.5 9.8 copy-start.19
  14.5 10.5 collective-permute-start.1
  20.1 8.7 collective-permute-start
  22.8 654.9 %reduce-scatter.15.cloned.1.call-start = ((), (), s32[]{:S(2)}) async-start(), calls=%async_computation.11 | async-start | bytes 2228224 | tf_op jit(solution)/shard_map/reduce_scatter | solution.py:144
  170.4 4.6 copy-start.5
  175.1 2.1 copy-start.13
  181.1 559.4 %reduce-scatter.13.cloned.1.call-start = ((), (), s32[]{:S(2)}) async-start(), calls=%async_computation.10 | async-start | bytes 2228224 | tf_op jit(solution)/shard_map/reduce_scatter | solution.py:144
  314.6 4.6 copy-start.4
  319.3 2.2 copy-start.15
  325.4 489.3 %reduce-scatter.11.cloned.1.call-start = ((), (), s32[]{:S(2)}) async-start(), calls=%async_computation.9 | async-start | bytes 2228224 | tf_op jit(solution)/shard_map/reduce_scatter | solution.py:144
  458.7 4.6 copy-start.3
  463.3 2.1 copy-start.16
  469.4 419.0 %reduce-scatter.9.cloned.1.call-start = ((), (), s32[]{:S(2)}) async-start(), calls=%async_computation.8 | async-start | bytes 2228224 | tf_op jit(solution)/shard_map/reduce_scatter | solution.py:144
  608.3 2.1 copy-start.17
  614.3 1.2 copy-start.9
  614.3 348.1 %reduce-scatter.23.cloned.1.call-start = ((), (), s32[]{:S(2)}) async-start(), calls=%async_computation.15 | async-start | bytes 2228224 | tf_op jit(solution)/shard_map/reduce_scatter | solution.py:145
  623.7 1.2 copy-start.8
  623.8 412.5 %reduce-scatter.21.cloned.1.call-start = ((), (), s32[]{:S(2)}) async-start(), calls=%async_computation.14 | async-start | bytes 2228224 | tf_op jit(solution)/shard_map/reduce_scatter | solution.py:145
  633.2 1.2 copy-start.7
  633.3 476.8 %reduce-scatter.19.cloned.1.call-start = ((), (), s32[]{:S(2)}) async-start(), calls=%async_computation.13 | async-start | bytes 2228224 | tf_op jit(solution)/shard_map/reduce_scatter | solution.py:145
  642.8 1.2 copy-start.6
  642.8 541.2 %reduce-scatter.17.cloned.1.call-start = ((), (), s32[]{:S(2)}) async-start(), calls=%async_computation.12 | async-start | bytes 2228224 | tf_op jit(solution)/shard_map/reduce_scatter | solution.py:145
  652.3 1.2 copy-start.14
  654.2 3.0 copy-start
  659.2 4.0 copy-start.1
  665.1 4.0 copy-start.2
  672.2 3.1 copy-start.10
  672.2 3.3 copy-start.11
  675.2 1.2 copy-start.12
Sparse Core Ops, SparseCore 0:
  10.7 77.5 all-gather.28
  90.4 69.9 all-gather.30
  162.5 70.3 all-gather.24
  234.7 69.8 all-gather.26
  306.5 70.0 all-gather.20
  378.6 70.0 all-gather.22
  451.3 70.0 all-gather.16
  523.5 70.0 all-gather.18
  596.4 70.2 reduce-scatter.14
  669.4 71.0 reduce-scatter.12
  743.4 71.2 reduce-scatter.10
  817.4 70.9 reduce-scatter.8
  891.2 71.1 reduce-scatter.22
  965.1 71.0 reduce-scatter.20
  1038.9 71.1 reduce-scatter.18
  1112.8 71.1 reduce-scatter.16

commit v2 on v1

v2 whole, which is shorter than its diff:
```python
import jax
import jax.numpy as jnp
from jax import lax
from jax.sharding import PartitionSpec as P

HEAD = 128
SPAN = 64
NBRS = 4
CHUNKS = 4


def from_behind(array, axis, by):
    length = lax.axis_size(axis)
    pairs = [(i, i + by) for i in range(length) if 0 <= i + by < length]
    return lax.ppermute(array, axis, pairs)


def split_heads(block_rows):
    return block_rows.reshape(block_rows.shape[:-1] + (block_rows.shape[-1] // HEAD, HEAD))


def slot_forward(query_block, grad_block, key_heads, value_heads):
    query_heads = split_heads(query_block)
    scores = jnp.einsum(
        "nqhd,nkhd->nqhk", query_heads, key_heads, preferred_element_type=jnp.float32
    ) * HEAD ** (-0.5)
    row_max = jnp.max(scores, axis=-1)
    exp_scores = jnp.exp(scores - row_max[..., None])
    row_total = jnp.sum(exp_scores, axis=-1)
    partial_value = (
        jnp.einsum(
            "nqhk,nkhd->nqhd",
            exp_scores.astype(jnp.bfloat16),
            value_heads,
            preferred_element_type=jnp.float32,
        )
        / row_total[..., None]
    )
    dotted = jnp.sum(split_heads(grad_block).astype(jnp.float32) * partial_value, axis=-1)
    return (row_max, row_total, dotted)


def slot_backward(query_block, grad_block, log_block, delta_block, key_heads, value_heads):
    query_heads = split_heads(query_block)
    grad_heads = split_heads(grad_block)
    scores = jnp.einsum(
        "nqhd,nkhd->nqhk", query_heads, key_heads, preferred_element_type=jnp.float32
    ) * HEAD ** (-0.5)
    probabilities = jnp.exp(scores - log_block[..., None])
    grad_probs = jnp.einsum(
        "nqhd,nkhd->nqhk", grad_heads, value_heads, preferred_element_type=jnp.float32
    )
    grad_scores = (probabilities * (grad_probs - delta_block[..., None])).astype(jnp.bfloat16)
    grad_query = (
        jnp.einsum("nqhk,nkhd->nqhd", grad_scores, key_heads, preferred_element_type=jnp.float32)
        * HEAD ** (-0.5)
    ).astype(jnp.bfloat16)
    value_term = jnp.einsum(
        "nqhk,nqhd->nkhd",
        probabilities.astype(jnp.bfloat16),
        grad_heads,
        preferred_element_type=jnp.float32,
    )
    key_term = jnp.einsum(
        "nqhk,nqhd->nkhd", grad_scores, query_heads, preferred_element_type=jnp.float32
    )
    return (grad_query.reshape(query_block.shape), key_term, value_term)


def ring_step(array, axis, by):
    length = lax.axis_size(axis)
    pairs = [(i, (i + by) % length) for i in range(length)]
    return lax.ppermute(array, axis, pairs)


def shards(queries, grad_out, neighbour_keys, neighbour_values, neighbours):
    groups = lax.axis_size("grp")
    me = lax.axis_index("grp")
    span_len = SPAN
    tok_rows = queries.shape[1]
    row_width = queries.shape[2]
    head_count = row_width // HEAD
    neighbour_len = neighbour_keys.shape[2]
    span_count = tok_rows // span_len
    pair_count = span_count * NBRS
    assert pair_count == groups
    score_scale = HEAD ** (-0.5)
    ahead = groups // 2
    behind = groups - 1 - ahead
    next_query, next_grad = from_behind(
        (queries[0, : span_len - 1], grad_out[0, : span_len - 1]), "seq", -1
    )
    window_query = jnp.concatenate([queries[0, span_len - 1 :], next_query], axis=0).reshape(
        span_count, span_len, row_width
    )
    window_grad = jnp.concatenate([grad_out[0, span_len - 1 :], next_grad], axis=0).reshape(
        span_count, span_len, row_width
    )
    owner_ids = neighbours[0].reshape(pair_count)
    group_ids = jnp.arange(groups, dtype=jnp.int32)
    placement = (owner_ids[None, :] == group_ids[:, None]).astype(jnp.int32)
    owner_span = jnp.sum(placement * jnp.arange(pair_count, dtype=jnp.int32)[None, :], axis=1) // NBRS
    rel_groups = (me + group_ids) % groups
    slot_span = owner_span[rel_groups]
    pair_slot = (owner_ids - me) % groups
    slot_query = window_query[slot_span]
    slot_grad = window_grad[slot_span]
    held = jnp.stack([neighbour_keys[0, 0], neighbour_values[0, 0]])
    ahead_blocks, behind_blocks = [], []
    going_up, going_down = held, held
    for step in range(1, ahead + 1):
        going_up = ring_step(going_up, "grp", 1)
        ahead_blocks.append(going_up)
        if step <= behind:
            going_down = ring_step(going_down, "grp", -1)
            behind_blocks.append(going_down)
    all_blocks = jnp.stack([held] + behind_blocks + ahead_blocks[::-1], axis=0)
    key_heads = split_heads(all_blocks[:, 0])
    value_heads = split_heads(all_blocks[:, 1])
    stat_max, stat_total, stat_dot = slot_forward(slot_query, slot_grad, key_heads, value_heads)
    pair_shape = (span_count, NBRS, span_len, head_count)
    pair_max = stat_max[pair_slot].reshape(pair_shape)
    pair_total = stat_total[pair_slot].reshape(pair_shape)
    pair_dot = stat_dot[pair_slot].reshape(pair_shape)
    top_max = jnp.max(pair_max, axis=1, keepdims=True)
    weights = pair_total * jnp.exp(pair_max - top_max)
    weight_sum = jnp.sum(weights, axis=1)
    log_total = top_max[:, 0] + jnp.log(weight_sum)
    delta_rows = jnp.sum(weights * pair_dot, axis=1) / weight_sum
    grad_query, key_term, value_term = slot_backward(
        slot_query,
        slot_grad,
        log_total[slot_span],
        delta_rows[slot_span],
        key_heads,
        value_heads,
    )
    pair_grad = grad_query[pair_slot].reshape(span_count, NBRS, span_len, row_width)
    grad_windows = (
        jnp.sum(pair_grad.astype(jnp.float32), axis=1)
        .astype(jnp.bfloat16)
        .reshape(1, span_count, span_len, row_width)
    )
    terms = jnp.stack(
        [key_term.reshape(groups, neighbour_len, row_width) * score_scale,
         value_term.reshape(groups, neighbour_len, row_width)],
        axis=1,
    ).astype(jnp.bfloat16)
    up_sum = terms[ahead]
    for step in range(1, ahead + 1):
        up_arrived = ring_step(up_sum, "grp", 1).astype(jnp.float32)
        if step < ahead:
            up_sum = (up_arrived + terms[ahead - step]).astype(jnp.bfloat16)
    down_sum = terms[groups - behind]
    for step in range(1, behind + 1):
        down_arrived = ring_step(down_sum, "grp", -1).astype(jnp.float32)
        if step < behind:
            down_sum = (down_arrived + terms[groups - behind + step]).astype(jnp.bfloat16)
    total = up_arrived + down_arrived + terms[0].astype(jnp.float32)
    grad_keys = total[0].astype(jnp.bfloat16).reshape(1, 1, neighbour_len, row_width)
    grad_values = total[1].astype(jnp.bfloat16).reshape(1, 1, neighbour_len, row_width)
    return (grad_windows, grad_keys, grad_values)


def solution(mesh):
    in_specs = (
        P("grp", "seq", None),
        P("grp", "seq", None),
        P("grp", "seq", None, None),
        P("grp", "seq", None, None),
        P("grp", "seq", None),
    )
    out_specs = (
        P("grp", "seq", None, None),
        P("grp", "seq", None, None),
        P("grp", "seq", None, None),
    )
    return jax.shard_map(shards, mesh=mesh, in_specs=in_specs, out_specs=out_specs, check_vma=False)
```

time: 1200 us -> 656 us (0.55)
  waiting for transfers between devices: 951 us -> 370 us
  starting transfers between devices: 8.71 us -> 108 us
  matrix products: 85.7 us -> 57.1 us
  local copies, waits for them, and re-layouts: 111 us -> 91.5 us
  between operations: 14.7 us -> 1.27 us
    reduce_scatter x8 -> x0, waiting for transfers between devices: 504 us -> none  [the longest x4 294 us: shards(): lax.psum_scatter(value_send, 'grp', scatter_dimension=0, tiled=True)]
    all_gather x8 -> x0, waiting for transfers between devices: 444 us -> none  [the longest x4 240 us: shards(): value_all = lax.all_gather(value_block[:, cols], 'grp', axis=0)]
    ppermute x0 -> x30, waiting for transfers between devices: none -> 370 us  [ring_step(): return lax.ppermute(array, axis, pairs)]
    ppermute x0 -> x30, starting transfers between devices: none -> 101 us  [ring_step(): return lax.ppermute(array, axis, pairs)]
    convert_element_type x8 -> x1, local copies, waits for them, and re-layouts: 31.4 us -> 1.04 us  [shards(): total[1].astype(jnp.bfloat16).reshape(1, 1, neighbour_len, row_width)]
    unnamed x41 -> x42, local copies, waits for them, and re-layouts: 9.7 us -> 29.8 us
    another operation x10 -> x2, local copies, waits for them, and re-layouts: 30.6 us -> 13.4 us  [the longest x1 12.3 us: shards(): jnp.stack([key_term.reshape(groups, neighbour_len, row_width) * score_sca...]
    dot_general x4 -> x1, matrix products: 18.3 us -> 4.93 us  [slot_backward(): jnp.einsum('nqhd,nkhd->nqhk', query_heads, key_heads, preferred_element_t...]
  transfers between devices with their start and end apart: 18 -> 32, of which waited for: 15 -> 24; matrix products, arithmetic and copies ran while one was open for 17% -> 9% of each run, Pallas kernels for 0% -> 0%
where the time goes in v2:
time: 656 us; the launch traced here: 653 us
  waiting for transfers between devices  370 us (56%)
  starting transfers between devices  108 us (16%)
  local copies, waits for them, and re-layouts  91.5 us (14%)
  matrix products  57.1 us (9%)
  other arithmetic  26 us (4%)
    ppermute x30, waiting for transfers between devices, ring_step(): return lax.ppermute(array, axis, pairs)  370 us
    ppermute x30, starting transfers between devices, ring_step(): return lax.ppermute(array, axis, pairs)  101 us
    unnamed x42, local copies, waits for them, and re-layouts  29.8 us
  transfers between devices with their start and end apart: 32, of which 24 were waited for; matrix products, arithmetic and copies ran while one was open for 9% of the time, Pallas kernels for 0%

profile of v2, /device:TPU:6, one launch (start us, length us, event | category | flops | bytes accessed | tf_op | source)
XLA Modules:
  0.0 653.3 jit_solution(5265534847997921243)
XLA Ops:
  3.4 3.8 collective-permute-start.7
  7.2 9.5 %collective-permute-start = (bf16[2,128,2048]{1,2,0:T(8,128)(2,1)S(1)}, bf16[2,128,2048]{1,2,0:T(8,128)(2,1)S(1)}, u32[]{:S(2)}, u32[]{:S(2)}) collective-permute-start(bf16[2,128,2048]{1,2,0:T(8,128)(2,1)S(1)} %pad_maximum_fusion.1), channel_id=1, source_target_pairs={{0,480},{32,0},{64,32},{96,64},{128,96},{160,128},{192,160},{224,1... | collective-permute-start | bytes 3145736 | tf_op jit(solution)/shard_map/ppermute | solution.py:73
  16.7 21.2 %collective-permute-done.7 = bf16[2,128,2048]{1,2,0:T(8,128)(2,1)S(1)} collective-permute-done((bf16[2,128,2048]{1,2,0:T(8,128)(2,1)S(1)}, bf16[2,128,2048]{1,2,0:T(8,128)(2,1)S(1)}, u32[]{:S(2)}, u32[]{:S(2)}) %collective-permute-start.7) | collective-permute-done | bytes 1048608 | tf_op jit(solution)/shard_map/ppermute | solution.py:73
  40.9 5.1 collective-permute-start.1
  46.0 20.4 %collective-permute-done.8 = bf16[2,128,2048]{1,2,0:T(8,128)(2,1)S(1)} collective-permute-done((bf16[2,128,2048]{1,2,0:T(8,128)(2,1)S(1)}, bf16[2,128,2048]{1,2,0:T(8,128)(2,1)S(1)}, u32[]{:S(2)}, u32[]{:S(2)}) %collective-permute-start.8) | collective-permute-done | bytes 1048608 | tf_op jit(solution)/shard_map/ppermute | solution.py:73
  69.3 3.2 collective-permute-start.15
  72.5 4.9 collective-permute-start.2
  79.0 4.0 collective-permute-start.16
  84.7 8.2 %collective-permute-done.9 = bf16[2,128,2048]{1,2,0:T(8,128)(2,1)S(1)} collective-permute-done((bf16[2,128,2048]{1,2,0:T(8,128)(2,1)S(1)}, bf16[2,128,2048]{1,2,0:T(8,128)(2,1)S(1)}, u32[]{:S(2)}, u32[]{:S(2)}) %collective-permute-start.9) | collective-permute-done | bytes 1048608 | tf_op jit(solution)/shard_map/ppermute | solution.py:73
  94.9 4.9 collective-permute-done.2
  99.7 5.6 collective-permute-start.3
  106.7 11.9 %collective-permute-done.10 = bf16[2,128,2048]{1,2,0:T(8,128)(2,1)} collective-permute-done((bf16[2,128,2048]{1,2,0:T(8,128)(2,1)S(1)}, bf16[2,128,2048]{1,2,0:T(8,128)(2,1)}, u32[]{:S(2)}, u32[]{:S(2)}) %collective-permute-start.10) | collective-permute-done | bytes 1048608 | tf_op jit(solution)/shard_map/ppermute | solution.py:73
  122.6 4.3 collective-permute-done.3
  126.8 5.6 collective-permute-start.4
  133.5 10.1 %collective-permute-done.11 = bf16[2,128,2048]{1,2,0:T(8,128)(2,1)} collective-permute-done((bf16[2,128,2048]{1,2,0:T(8,128)(2,1)}, bf16[2,128,2048]{1,2,0:T(8,128)(2,1)}, u32[]{:S(2)}, u32[]{:S(2)}) %collective-permute-start.11) | collective-permute-done | bytes 1048608 | tf_op jit(solution)/shard_map/ppermute | solution.py:73
  146.6 2.9 gather_fusion.1
  150.6 2.8 gather_fusion.5
  153.4 5.2 collective-permute-start.5
  158.6 2.4 bitcast_dynamic-update-slice_fusion.13
  161.0 6.7 %collective-permute-done.12 = bf16[2,128,2048]{1,2,0:T(8,128)(2,1)} collective-permute-done((bf16[2,128,2048]{1,2,0:T(8,128)(2,1)}, bf16[2,128,2048]{1,2,0:T(8,128)(2,1)}, u32[]{:S(2)}, u32[]{:S(2)}) %collective-permute-start.12) | collective-permute-done | bytes 1048608 | tf_op jit(solution)/shard_map/ppermute | solution.py:73
  169.6 2.4 bitcast_dynamic-update-slice_fusion.12
  172.0 2.4 bitcast_dynamic-update-slice_fusion.11
  174.4 3.9 collective-permute-done.5
  178.3 5.5 collective-permute-start.6
  183.8 2.4 bitcast_dynamic-update-slice_fusion.10
  186.2 5.0 collective-permute-done.13
  193.1 2.4 bitcast_dynamic-update-slice_fusion.9
  196.5 5.7 collective-permute-done.6
  203.3 9.9 %collective-permute-done.14 = bf16[2,128,2048]{1,2,0:T(8,128)(2,1)S(1)} collective-permute-done((bf16[2,128,2048]{1,2,0:T(8,128)(2,1)S(1)}, bf16[2,128,2048]{1,2,0:T(8,128)(2,1)S(1)}, u32[]{:S(2)}, u32[]{:S(2)}) %collective-permute-start.14) | collective-permute-done | bytes 1048608 | tf_op jit(solution)/shard_map/ppermute | solution.py:73
  215.3 2.4 bitcast_dynamic-update-slice_fusion.4
  217.7 2.4 bitcast_dynamic-update-slice_fusion.3
  220.1 2.4 bitcast_dynamic-update-slice_fusion.2
  225.5 9.2 %fusion.73 = (bf16[16,1,128,2048]{2,3,0,1:T(8,128)(2,1)}, bf16[16,1,128,2048]{2,3,0,1:T(8,128)(2,1)S(1)}) fusion(bf16[16,2,128,2048]{2,3,0,1:T(8,128)(2,1)} %bitcast_dynamic-update-slice_fusion.15), kind=kLoop, calls=%fused_computation.179 | loop fusion | bytes 33554432 | tf_op jit(solution)/shard_map/slice | solution.py:119
  235.6 4.9 bitcast_reduce_fusion
  241.2 6.8 %fusion.8 = f32[16,64,16]{1,2,0:T(8,128)S(1)} fusion(f32[16,16,128,64]{2,3,1,0:T(8,128)} %get-tuple-element.16, f32[16,64,16]{1,2,0:T(8,128)S(1)} %get-tuple-element.15), kind=kLoop, calls=%fused_computation.54 | loop fusion | flops 6275072 | bytes 8519680 | tf_op jit(solution)/shard_map/reduce_sum | solution.py:29
  248.5 10.4 %fusion.5 = f32[16,64,16]{1,2,0:T(8,128)S(1)} fusion(f32[16,64,16]{1,2,0:T(8,128)S(1)} %fusion.8, bf16[16,128,16,128]{1,3,2,0:T(8,128)(2,1)} %bitcast.240, f32[16,16,128,64]{2,3,1,0:T(8,128)} %get-tuple-element.16, f32[16,64,16]{1,2,0:T(8,128)S(1)} %get-tuple-element.15, bf16[16,64,2048]{2,1,0:T(8,128)(2,1)} %gather_fusion.5), kind=kOutput, calls=%fused_computation.51 | convolution fusion | flops 551534592 | bytes 21168128 | tf_op jit(solution)/shard_map/nqhk,nkhd->nqhd/dot_general | solution.py:31
  260.7 9.9 %convolution_convert_fusion = bf16[16,16,128,128]{3,2,1,0:T(8,128)(2,1)} fusion(f32[16,16,128,64]{2,3,1,0:T(8,128)} %get-tuple-element.16, f32[16,64,16]{1,2,0:T(8,128)S(1)} %gather_fusion.4, bf16[16,64,2048]{2,1,0:T(8,128)(2,1)} %gather_fusion.5), kind=kOutput, calls=%fused_computation.55 | convolution fusion | flops 547356672 | bytes 21037056 | tf_op jit(solution)/shard_map/nqhk,nqhd->nkhd/dot_general | solution.py:58
  270.7 10.1 %fusion.2 = bf16[16,64,16,128]{3,1,2,0:T(8,128)(2,1)} fusion(f32[16,16,128,64]{2,3,1,0:T(8,128)} %get-tuple-element.16, f32[16,64,16]{1,2,0:T(8,128)S(1)} %gather_fusion.7, f32[16,64,16]{1,2,0:T(8,128)S(1)} %gather_fusion.4, bf16[16,128,16,128]{1,3,2,0:T(8,128)(2,1)} %bitcast.241, bf16[16,64,2048]{2,1,0:T(8,128)(2,1)S(1)} %copy-done.2), kind=kOutput, calls=%fused_computation.44 | convolution fusion | flops 547356672 | bytes 25296896 | tf_op jit(solution)/shard_map/nqhd,nkhd->nqhk/dot_general | solution.py:50
  280.7 12.3 %copy.67 = bf16[16,1,128,2048]{3,2,1,0:T(8,128)(2,1)} copy(bf16[16,1,128,2048]{2,3,0,1:T(8,128)(2,1)} %bitcast.242) | data formatting | bytes 16777216 | tf_op jit(solution)/shard_map/stack;reshape | solution.py:144
  293.0 9.4 %multiply_convert_fusion = bf16[16,16,128,128]{3,2,1,0:T(8,128)(2,1)} fusion(bf16[16,64,16,128]{3,1,2,0:T(8,128)(2,1)} %fusion.2, bf16[16,64,2048]{2,1,0:T(8,128)(2,1)} %gather_fusion.1), kind=kOutput, calls=%fused_computation.39 | convolution fusion | flops 545259520 | bytes 16777216 | tf_op jit(solution)/shard_map/nqhk,nqhd->nkhd/dot_general | solution.py:64
  302.4 12.3 %copy.66 = bf16[16,1,128,2048]{3,2,1,0:T(8,128)(2,1)} copy(bf16[16,1,128,2048]{2,3,0,1:T(8,128)(2,1)} %bitcast.243) | data formatting | bytes 16777216 | tf_op jit(solution)/shard_map/mul | solution.py:145
  316.7 2.3 collective-permute-start.17
  319.0 19.8 %collective-permute-done.17 = bf16[2,128,2048]{2,1,0:T(8,128)(2,1)S(1)} collective-permute-done((bf16[2,128,2048]{2,1,0:T(8,128)(2,1)S(1)}, bf16[2,128,2048]{2,1,0:T(8,128)(2,1)S(1)}, u32[]{:S(2)}, u32[]{:S(2)}) %collective-permute-start.17) | collective-permute-done | bytes 1048608 | tf_op jit(solution)/shard_map/ppermute | solution.py:73
  342.2 21.0 %collective-permute-done.18 = bf16[2,128,2048]{2,1,0:T(8,128)(2,1)S(1)} collective-permute-done((bf16[2,128,2048]{2,1,0:T(8,128)(2,1)S(1)}, bf16[2,128,2048]{2,1,0:T(8,128)(2,1)S(1)}, u32[]{:S(2)}, u32[]{:S(2)}) %collective-permute-start.18) | collective-permute-done | bytes 1048608 | tf_op jit(solution)/shard_map/ppermute | solution.py:73
  363.6 1.9 collective-permute-start.19
  365.5 21.0 %collective-permute-done.19 = bf16[2,128,2048]{2,1,0:T(8,128)(2,1)S(1)} collective-permute-done((bf16[2,128,2048]{2,1,0:T(8,128)(2,1)S(1)}, bf16[2,128,2048]{2,1,0:T(8,128)(2,1)S(1)}, u32[]{:S(2)}, u32[]{:S(2)}) %collective-permute-start.19) | collective-permute-done | bytes 1048608 | tf_op jit(solution)/shard_map/ppermute | solution.py:73
  386.9 1.9 collective-permute-start.20
  388.8 21.0 %collective-permute-done.20 = bf16[2,128,2048]{2,1,0:T(8,128)(2,1)S(1)} collective-permute-done((bf16[2,128,2048]{2,1,0:T(8,128)(2,1)S(1)}, bf16[2,128,2048]{2,1,0:T(8,128)(2,1)S(1)}, u32[]{:S(2)}, u32[]{:S(2)}) %collective-permute-start.20) | collective-permute-done | bytes 1048608 | tf_op jit(solution)/shard_map/ppermute | solution.py:73
  412.2 21.5 %collective-permute-done.21 = bf16[2,128,2048]{2,1,0:T(8,128)(2,1)S(1)} collective-permute-done((bf16[2,128,2048]{2,1,0:T(8,128)(2,1)S(1)}, bf16[2,128,2048]{2,1,0:T(8,128)(2,1)S(1)}, u32[]{:S(2)}, u32[]{:S(2)}) %collective-permute-start.21) | collective-permute-done | bytes 1048608 | tf_op jit(solution)/shard_map/ppermute | solution.py:73
  436.0 5.1 collective-permute-start.25
  441.1 17.4 %collective-permute-done.22 = bf16[2,128,2048]{2,1,0:T(8,128)(2,1)S(1)} collective-permute-done((bf16[2,128,2048]{2,1,0:T(8,128)(2,1)S(1)}, bf16[2,128,2048]{2,1,0:T(8,128)(2,1)S(1)}, u32[]{:S(2)}, u32[]{:S(2)}) %collective-permute-start.22) | collective-permute-done | bytes 1048608 | tf_op jit(solution)/shard_map/ppermute | solution.py:73
  460.9 16.0 %collective-permute-done.23 = bf16[2,128,2048]{2,1,0:T(8,128)(2,1)S(1)} collective-permute-done((bf16[2,128,2048]{2,1,0:T(8,128)(2,1)S(1)}, bf16[2,128,2048]{2,1,0:T(8,128)(2,1)S(1)}, u32[]{:S(2)}, u32[]{:S(2)}) %collective-permute-start.23) | collective-permute-done | bytes 1048608 | tf_op jit(solution)/shard_map/ppermute | solution.py:73
  479.6 24.8 %collective-permute-done.26 = bf16[2,128,2048]{2,1,0:T(8,128)(2,1)S(1)} collective-permute-done((bf16[2,128,2048]{2,1,0:T(8,128)(2,1)S(1)}, bf16[2,128,2048]{2,1,0:T(8,128)(2,1)S(1)}, u32[]{:S(2)}, u32[]{:S(2)}) %collective-permute-start.26) | collective-permute-done | bytes 1048608 | tf_op jit(solution)/shard_map/ppermute | solution.py:73
  506.8 26.0 %collective-permute-done.27 = bf16[2,128,2048]{2,1,0:T(8,128)(2,1)S(1)} collective-permute-done((bf16[2,128,2048]{2,1,0:T(8,128)(2,1)S(1)}, bf16[2,128,2048]{2,1,0:T(8,128)(2,1)S(1)}, u32[]{:S(2)}, u32[]{:S(2)}) %collective-permute-start.27) | collective-permute-done | bytes 1048608 | tf_op jit(solution)/shard_map/ppermute | solution.py:73
  535.1 25.1 %collective-permute-done.28 = bf16[2,128,2048]{2,1,0:T(8,128)(2,1)S(1)} collective-permute-done((bf16[2,128,2048]{2,1,0:T(8,128)(2,1)S(1)}, bf16[2,128,2048]{2,1,0:T(8,128)(2,1)S(1)}, u32[]{:S(2)}, u32[]{:S(2)}) %collective-permute-start.28) | collective-permute-done | bytes 1048608 | tf_op jit(solution)/shard_map/ppermute | solution.py:73
  560.6 3.9 collective-permute-start.29
  564.5 22.7 %collective-permute-done.29 = bf16[2,128,2048]{2,1,0:T(8,128)(2,1)S(1)} collective-permute-done((bf16[2,128,2048]{2,1,0:T(8,128)(2,1)S(1)}, bf16[2,128,2048]{2,1,0:T(8,128)(2,1)S(1)}, u32[]{:S(2)}, u32[]{:S(2)}) %collective-permute-start.29) | collective-permute-done | bytes 1048608 | tf_op jit(solution)/shard_map/ppermute | solution.py:73
  587.6 5.6 collective-permute-start.30
  595.1 21.1 %collective-permute-done.30 = bf16[2,128,2048]{2,1,0:T(8,128)(2,1)S(1)} collective-permute-done((bf16[2,128,2048]{2,1,0:T(8,128)(2,1)S(1)}, bf16[2,128,2048]{2,1,0:T(8,128)(2,1)S(1)}, u32[]{:S(2)}, u32[]{:S(2)}) %collective-permute-start.30) | collective-permute-done | bytes 1048608 | tf_op jit(solution)/shard_map/ppermute | solution.py:73
  617.6 5.8 collective-permute-start.31
  623.5 12.4 %fusion.12 = bf16[16,16,8,8,128]{4,3,2,1,0:T(8,128)(2,1)} fusion(bf16[16,128,16,128]{1,3,2,0:T(8,128)(2,1)} %bitcast.239, bf16[16,64,16,128]{3,1,2,0:T(8,128)(2,1)} %fusion.2), kind=kOutput, calls=%fused_computation.57 | convolution fusion | flops 541065216 | bytes 16777216 | tf_op jit(solution)/shard_map/nqhk,nkhd->nqhd/dot_general | solution.py:55
  635.9 5.4 copy.95
  641.3 4.9 gather_fusion.8
  646.2 4.3 bitcast_reduce_fusion.1
  (101 shorter events, 66.1 us)
Async XLA Ops:
  3.4 34.6 %collective-permute-start.7 = (bf16[2,128,2048]{1,2,0:T(8,128)(2,1)S(1)}, bf16[2,128,2048]{1,2,0:T(8,128)(2,1)S(1)}, u32[]{:S(2)}, u32[]{:S(2)}) collective-permute-start(bf16[2,128,2048]{1,2,0:T(8,128)(2,1)S(1)} %pad_maximum_fusion.1), channel_id=1, source_target_pairs={{0,32},{32,64},{64,96},{96,128},{128,160},{160,192},{192,224},{224... | collective-permute-start | bytes 3145736 | tf_op jit(solution)/shard_map/ppermute | solution.py:73
  7.2 33.6 %collective-permute-start = (bf16[2,128,2048]{1,2,0:T(8,128)(2,1)S(1)}, bf16[2,128,2048]{1,2,0:T(8,128)(2,1)S(1)}, u32[]{:S(2)}, u32[]{:S(2)}) collective-permute-start(bf16[2,128,2048]{1,2,0:T(8,128)(2,1)S(1)} %pad_maximum_fusion.1), channel_id=1, source_target_pairs={{0,480},{32,0},{64,32},{96,64},{128,96},{160,128},{192,160},{224,1... | collective-permute-start | bytes 3145736 | tf_op jit(solution)/shard_map/ppermute | solution.py:73
  38.0 1.0 copy-start.4
  38.9 27.4 %collective-permute-start.8 = (bf16[2,128,2048]{1,2,0:T(8,128)(2,1)S(1)}, bf16[2,128,2048]{1,2,0:T(8,128)(2,1)S(1)}, u32[]{:S(2)}, u32[]{:S(2)}) collective-permute-start(bf16[2,128,2048]{1,2,0:T(8,128)(2,1)S(1)} %collective-permute-done.7), channel_id=1, source_target_pairs={{0,32},{32,64},{64,96},{96,128},{128,160},{160,192},{192,224},{224... | collective-permute-start | bytes 3145736 | tf_op jit(solution)/shard_map/ppermute | solution.py:73
  40.9 25.5 %copy-start.10 = (bf16[2,128,2048]{1,2,0:T(8,128)(2,1)}, bf16[2,128,2048]{1,2,0:T(8,128)(2,1)S(1)}, u32[]{:S(2)}) copy-start(bf16[2,128,2048]{1,2,0:T(8,128)(2,1)S(1)} %collective-permute-done) | copy-start | bytes 3145732
  40.9 31.6 %collective-permute-start.1 = (bf16[2,128,2048]{1,2,0:T(8,128)(2,1)S(1)}, bf16[2,128,2048]{1,2,0:T(8,128)(2,1)}, u32[]{:S(2)}, u32[]{:S(2)}) collective-permute-start(bf16[2,128,2048]{1,2,0:T(8,128)(2,1)S(1)} %collective-permute-done), channel_id=1, source_target_pairs={{0,480},{32,0},{64,32},{96,64},{128,96},{160,128},{192,160},{224,1... | collective-permute-start | bytes 3145736 | tf_op jit(solution)/shard_map/ppermute | solution.py:73
  66.4 33.4 %copy-start.6 = (bf16[2,128,2048]{1,2,0:T(8,128)(2,1)}, bf16[2,128,2048]{1,2,0:T(8,128)(2,1)S(1)}, u32[]{:S(2)}) copy-start(bf16[2,128,2048]{1,2,0:T(8,128)(2,1)S(1)} %collective-permute-done.8) | copy-start | bytes 3145732
  66.4 26.5 %collective-permute-start.9 = (bf16[2,128,2048]{1,2,0:T(8,128)(2,1)S(1)}, bf16[2,128,2048]{1,2,0:T(8,128)(2,1)S(1)}, u32[]{:S(2)}, u32[]{:S(2)}) collective-permute-start(bf16[2,128,2048]{1,2,0:T(8,128)(2,1)S(1)} %collective-permute-done.8), channel_id=1, source_target_pairs={{0,32},{32,64},{64,96},{96,128},{128,160},{160,192},{192,224},{224... | collective-permute-start | bytes 3145736 | tf_op jit(solution)/shard_map/ppermute | solution.py:73
  69.3 76.3 %collective-permute-start.15 = (bf16[63,2048]{1,0:T(8,128)(2,1)S(1)}, bf16[63,2048]{1,0:T(8,128)(2,1)}, u32[]{:S(2)}, u32[]{:S(2)}) collective-permute-start(bf16[63,2048]{1,0:T(8,128)(2,1)S(1)} %slice_bitcast_fusion.5), channel_id=1, source_target_pairs={{1,0},{2,1},{3,2},{4,3},{5,4},{6,5},{7,6},{8,7},{9,8},{10,9},{11,1... | collective-permute-start | bytes 774152 | tf_op jit(solution)/shard_map/ppermute | solution.py:15
  72.5 27.3 %collective-permute-start.2 = (bf16[2,128,2048]{1,2,0:T(8,128)(2,1)}, bf16[2,128,2048]{1,2,0:T(8,128)(2,1)}, u32[]{:S(2)}, u32[]{:S(2)}) collective-permute-start(bf16[2,128,2048]{1,2,0:T(8,128)(2,1)} %collective-permute-done.1), channel_id=1, source_target_pairs={{0,480},{32,0},{64,32},{96,64},{128,96},{160,128},{192,160},{224,1... | collective-permute-start | bytes 3145736 | tf_op jit(solution)/shard_map/ppermute | solution.py:73
  79.0 70.5 %collective-permute-start.16 = (bf16[63,2048]{1,0:T(8,128)(2,1)}, bf16[63,2048]{1,0:T(8,128)(2,1)}, u32[]{:S(2)}, u32[]{:S(2)}) collective-permute-start(bf16[63,2048]{1,0:T(8,128)(2,1)} %slice_bitcast_fusion.4), channel_id=1, source_target_pairs={{1,0},{2,1},{3,2},{4,3},{5,4},{6,5},{7,6},{8,7},{9,8},{10,9},{11,1... | collective-permute-start | bytes 774152 | tf_op jit(solution)/shard_map/ppermute | solution.py:15
  92.9 27.6 %copy-start.8 = (bf16[2,128,2048]{1,2,0:T(8,128)(2,1)}, bf16[2,128,2048]{1,2,0:T(8,128)(2,1)S(1)}, u32[]{:S(2)}) copy-start(bf16[2,128,2048]{1,2,0:T(8,128)(2,1)S(1)} %collective-permute-done.9) | copy-start | bytes 3145732
  92.9 25.7 %collective-permute-start.10 = (bf16[2,128,2048]{1,2,0:T(8,128)(2,1)S(1)}, bf16[2,128,2048]{1,2,0:T(8,128)(2,1)}, u32[]{:S(2)}, u32[]{:S(2)}) collective-permute-start(bf16[2,128,2048]{1,2,0:T(8,128)(2,1)S(1)} %collective-permute-done.9), channel_id=1, source_target_pairs={{0,32},{32,64},{64,96},{96,128},{128,160},{160,192},{192,224},{224... | collective-permute-start | bytes 3145736 | tf_op jit(solution)/shard_map/ppermute | solution.py:73
  99.7 27.1 %collective-permute-start.3 = (bf16[2,128,2048]{1,2,0:T(8,128)(2,1)}, bf16[2,128,2048]{1,2,0:T(8,128)(2,1)}, u32[]{:S(2)}, u32[]{:S(2)}) collective-permute-start(bf16[2,128,2048]{1,2,0:T(8,128)(2,1)} %collective-permute-done.2), channel_id=1, source_target_pairs={{0,480},{32,0},{64,32},{96,64},{128,96},{160,128},{192,160},{224,1... | collective-permute-start | bytes 3145736 | tf_op jit(solution)/shard_map/ppermute | solution.py:73
  118.6 25.0 %collective-permute-start.11 = (bf16[2,128,2048]{1,2,0:T(8,128)(2,1)}, bf16[2,128,2048]{1,2,0:T(8,128)(2,1)}, u32[]{:S(2)}, u32[]{:S(2)}) collective-permute-start(bf16[2,128,2048]{1,2,0:T(8,128)(2,1)} %collective-permute-done.10), channel_id=1, source_target_pairs={{0,32},{32,64},{64,96},{96,128},{128,160},{160,192},{192,224},{224... | collective-permute-start | bytes 3145736 | tf_op jit(solution)/shard_map/ppermute | solution.py:73
  126.8 26.5 %collective-permute-start.4 = (bf16[2,128,2048]{1,2,0:T(8,128)(2,1)}, bf16[2,128,2048]{1,2,0:T(8,128)(2,1)}, u32[]{:S(2)}, u32[]{:S(2)}) collective-permute-start(bf16[2,128,2048]{1,2,0:T(8,128)(2,1)} %collective-permute-done.3), channel_id=1, source_target_pairs={{0,480},{32,0},{64,32},{96,64},{128,96},{160,128},{192,160},{224,1... | collective-permute-start | bytes 3145736 | tf_op jit(solution)/shard_map/ppermute | solution.py:73
  143.6 24.1 %collective-permute-start.12 = (bf16[2,128,2048]{1,2,0:T(8,128)(2,1)}, bf16[2,128,2048]{1,2,0:T(8,128)(2,1)}, u32[]{:S(2)}, u32[]{:S(2)}) collective-permute-start(bf16[2,128,2048]{1,2,0:T(8,128)(2,1)} %collective-permute-done.11), channel_id=1, source_target_pairs={{0,32},{32,64},{64,96},{96,128},{128,160},{160,192},{192,224},{224... | collective-permute-start | bytes 3145736 | tf_op jit(solution)/shard_map/ppermute | solution.py:73
  153.4 24.9 %collective-permute-start.5 = (bf16[2,128,2048]{1,2,0:T(8,128)(2,1)}, bf16[2,128,2048]{1,2,0:T(8,128)(2,1)S(1)}, u32[]{:S(2)}, u32[]{:S(2)}) collective-permute-start(bf16[2,128,2048]{1,2,0:T(8,128)(2,1)} %collective-permute-done.4), channel_id=1, source_target_pairs={{0,480},{32,0},{64,32},{96,64},{128,96},{160,128},{192,160},{224,1... | collective-permute-start | bytes 3145736 | tf_op jit(solution)/shard_map/ppermute | solution.py:73
  167.7 23.5 %collective-permute-start.13 = (bf16[2,128,2048]{1,2,0:T(8,128)(2,1)}, bf16[2,128,2048]{1,2,0:T(8,128)(2,1)S(1)}, u32[]{:S(2)}, u32[]{:S(2)}) collective-permute-start(bf16[2,128,2048]{1,2,0:T(8,128)(2,1)} %collective-permute-done.12), channel_id=1, source_target_pairs={{0,32},{32,64},{64,96},{96,128},{128,160},{160,192},{192,224},{224... | collective-permute-start | bytes 3145736 | tf_op jit(solution)/shard_map/ppermute | solution.py:73
  178.3 23.9 %collective-permute-start.6 = (bf16[2,128,2048]{1,2,0:T(8,128)(2,1)S(1)}, bf16[2,128,2048]{1,2,0:T(8,128)(2,1)S(1)}, u32[]{:S(2)}, u32[]{:S(2)}) collective-permute-start(bf16[2,128,2048]{1,2,0:T(8,128)(2,1)S(1)} %collective-permute-done.5), channel_id=1, source_target_pairs={{0,480},{32,0},{64,32},{96,64},{128,96},{160,128},{192,160},{224,1... | collective-permute-start | bytes 3145736 | tf_op jit(solution)/shard_map/ppermute | solution.py:73
  186.2 36.3 %copy-start.9 = (bf16[2,128,2048]{1,2,0:T(8,128)(2,1)S(1)}, bf16[2,128,2048]{1,2,0:T(8,128)(2,1)}, u32[]{:S(2)}) copy-start(bf16[2,128,2048]{1,2,0:T(8,128)(2,1)} %copy-done.8) | copy-start | bytes 3145732
  191.2 22.0 %collective-permute-start.14 = (bf16[2,128,2048]{1,2,0:T(8,128)(2,1)S(1)}, bf16[2,128,2048]{1,2,0:T(8,128)(2,1)S(1)}, u32[]{:S(2)}, u32[]{:S(2)}) collective-permute-start(bf16[2,128,2048]{1,2,0:T(8,128)(2,1)S(1)} %collective-permute-done.13), channel_id=1, source_target_pairs={{0,32},{32,64},{64,96},{96,128},{128,160},{160,192},{192,224},{224... | collective-permute-start | bytes 3145736 | tf_op jit(solution)/shard_map/ppermute | solution.py:73
  195.5 28.0 %copy-start.7 = (bf16[2,128,2048]{1,2,0:T(8,128)(2,1)S(1)}, bf16[2,128,2048]{1,2,0:T(8,128)(2,1)}, u32[]{:S(2)}) copy-start(bf16[2,128,2048]{1,2,0:T(8,128)(2,1)} %copy-done.6) | copy-start | bytes 3145732
  196.5 28.0 %copy-start.5 = (bf16[2,128,2048]{1,2,0:T(8,128)(2,1)S(1)}, bf16[2,128,2048]{1,2,0:T(8,128)(2,1)}, u32[]{:S(2)}) copy-start(bf16[2,128,2048]{1,2,0:T(8,128)(2,1)} %copy-done.4) | copy-start | bytes 3145732
  225.5 10.1 %copy-start.3 = (bf16[16,64,2048]{2,1,0:T(8,128)(2,1)S(1)}, bf16[16,64,2048]{2,1,0:T(8,128)(2,1)}, u32[]{:S(2)}) copy-start(bf16[16,64,2048]{2,1,0:T(8,128)(2,1)} %gather_fusion.1) | copy-start | bytes 12582916
  234.8 5.8 copy-start.1
  260.7 9.9 %copy-start.2 = (bf16[16,64,2048]{2,1,0:T(8,128)(2,1)S(1)}, bf16[16,64,2048]{2,1,0:T(8,128)(2,1)}, u32[]{:S(2)}) copy-start(bf16[16,64,2048]{2,1,0:T(8,128)(2,1)} %gather_fusion.5) | copy-start | bytes 12582916
  314.8 24.0 %copy-start = (bf16[16,1,128,2048]{3,2,1,0:T(8,128)(2,1)S(1)}, bf16[16,1,128,2048]{3,2,1,0:T(8,128)(2,1)}, u32[]{:S(2)}) copy-start(bf16[16,1,128,2048]{3,2,1,0:T(8,128)(2,1)} %copy.66) | copy-start | bytes 25165828
  316.7 46.5 %slice-start = ((s8[8388608]{0:T(1024)(128)(4,1)}), s8[4194304]{0:T(1024)(128)(4,1)S(1)}, s32[]{:S(2)}) async-start(s8[8388608]{0:T(1024)(128)(4,1)} %bitcast.236), calls=%async_computation | async-start | bytes 8388608
  316.7 46.5 %slice-start.1 = ((s8[8388608]{0:T(1024)(128)(4,1)}), s8[4194304]{0:T(1024)(128)(4,1)S(1)}, s32[]{:S(2)}) async-start(s8[8388608]{0:T(1024)(128)(4,1)} %bitcast.236), calls=%async_computation.1 | async-start | bytes 8388608
  316.7 22.2 %collective-permute-start.17 = (bf16[2,128,2048]{2,1,0:T(8,128)(2,1)S(1)}, bf16[2,128,2048]{2,1,0:T(8,128)(2,1)S(1)}, u32[]{:S(2)}, u32[]{:S(2)}) collective-permute-start(bf16[2,128,2048]{2,1,0:T(8,128)(2,1)S(1)} %get-tuple-element.7), channel_id=1, source_target_pairs={{0,32},{32,64},{64,96},{96,128},{128,160},{160,192},{192,224},{224... | collective-permute-start | bytes 3145736 | tf_op jit(solution)/shard_map/ppermute | solution.py:73
  340.3 22.9 %collective-permute-start.18 = (bf16[2,128,2048]{2,1,0:T(8,128)(2,1)S(1)}, bf16[2,128,2048]{2,1,0:T(8,128)(2,1)S(1)}, u32[]{:S(2)}, u32[]{:S(2)}) collective-permute-start(bf16[2,128,2048]{2,1,0:T(8,128)(2,1)S(1)} %fusion.42), channel_id=1, source_target_pairs={{0,32},{32,64},{64,96},{96,128},{128,160},{160,192},{192,224},{224... | collective-permute-start | bytes 3145736 | tf_op jit(solution)/shard_map/ppermute | solution.py:73
  363.6 22.9 %collective-permute-start.19 = (bf16[2,128,2048]{2,1,0:T(8,128)(2,1)S(1)}, bf16[2,128,2048]{2,1,0:T(8,128)(2,1)S(1)}, u32[]{:S(2)}, u32[]{:S(2)}) collective-permute-start(bf16[2,128,2048]{2,1,0:T(8,128)(2,1)S(1)} %fusion.41), channel_id=1, source_target_pairs={{0,32},{32,64},{64,96},{96,128},{128,160},{160,192},{192,224},{224... | collective-permute-start | bytes 3145736 | tf_op jit(solution)/shard_map/ppermute | solution.py:73
  386.9 22.9 %collective-permute-start.20 = (bf16[2,128,2048]{2,1,0:T(8,128)(2,1)S(1)}, bf16[2,128,2048]{2,1,0:T(8,128)(2,1)S(1)}, u32[]{:S(2)}, u32[]{:S(2)}) collective-permute-start(bf16[2,128,2048]{2,1,0:T(8,128)(2,1)S(1)} %fusion.40), channel_id=1, source_target_pairs={{0,32},{32,64},{64,96},{96,128},{128,160},{160,192},{192,224},{224... | collective-permute-start | bytes 3145736 | tf_op jit(solution)/shard_map/ppermute | solution.py:73
  410.2 23.4 %collective-permute-start.21 = (bf16[2,128,2048]{2,1,0:T(8,128)(2,1)S(1)}, bf16[2,128,2048]{2,1,0:T(8,128)(2,1)S(1)}, u32[]{:S(2)}, u32[]{:S(2)}) collective-permute-start(bf16[2,128,2048]{2,1,0:T(8,128)(2,1)S(1)} %fusion.39), channel_id=1, source_target_pairs={{0,32},{32,64},{64,96},{96,128},{128,160},{160,192},{192,224},{224... | collective-permute-start | bytes 3145736 | tf_op jit(solution)/shard_map/ppermute | solution.py:73
  434.1 24.5 %collective-permute-start.22 = (bf16[2,128,2048]{2,1,0:T(8,128)(2,1)S(1)}, bf16[2,128,2048]{2,1,0:T(8,128)(2,1)S(1)}, u32[]{:S(2)}, u32[]{:S(2)}) collective-permute-start(bf16[2,128,2048]{2,1,0:T(8,128)(2,1)S(1)} %fusion.38), channel_id=1, source_target_pairs={{0,32},{32,64},{64,96},{96,128},{128,160},{160,192},{192,224},{224... | collective-permute-start | bytes 3145736 | tf_op jit(solution)/shard_map/ppermute | solution.py:73
  436.0 24.9 %collective-permute-start.25 = (bf16[2,128,2048]{2,1,0:T(8,128)(2,1)S(1)}, bf16[2,128,2048]{2,1,0:T(8,128)(2,1)S(1)}, u32[]{:S(2)}, u32[]{:S(2)}) collective-permute-start(bf16[2,128,2048]{2,1,0:T(8,128)(2,1)S(1)} %get-tuple-element.8), channel_id=1, source_target_pairs={{0,480},{32,0},{64,32},{96,64},{128,96},{160,128},{192,160},{224,1... | collective-permute-start | bytes 3145736 | tf_op jit(solution)/shard_map/ppermute | solution.py:73
  458.9 17.9 %collective-permute-start.23 = (bf16[2,128,2048]{2,1,0:T(8,128)(2,1)S(1)}, bf16[2,128,2048]{2,1,0:T(8,128)(2,1)S(1)}, u32[]{:S(2)}, u32[]{:S(2)}) collective-permute-start(bf16[2,128,2048]{2,1,0:T(8,128)(2,1)S(1)} %fusion.37), channel_id=1, source_target_pairs={{0,32},{32,64},{64,96},{96,128},{128,160},{160,192},{192,224},{224... | collective-permute-start | bytes 3145736 | tf_op jit(solution)/shard_map/ppermute | solution.py:73
  477.7 26.8 %collective-permute-start.26 = (bf16[2,128,2048]{2,1,0:T(8,128)(2,1)S(1)}, bf16[2,128,2048]{2,1,0:T(8,128)(2,1)S(1)}, u32[]{:S(2)}, u32[]{:S(2)}) collective-permute-start(bf16[2,128,2048]{2,1,0:T(8,128)(2,1)S(1)} %get-tuple-element.6), channel_id=1, source_target_pairs={{0,480},{32,0},{64,32},{96,64},{128,96},{160,128},{192,160},{224,1... | collective-permute-start | bytes 3145736 | tf_op jit(solution)/shard_map/ppermute | solution.py:73
  504.8 27.9 %collective-permute-start.27 = (bf16[2,128,2048]{2,1,0:T(8,128)(2,1)S(1)}, bf16[2,128,2048]{2,1,0:T(8,128)(2,1)S(1)}, u32[]{:S(2)}, u32[]{:S(2)}) collective-permute-start(bf16[2,128,2048]{2,1,0:T(8,128)(2,1)S(1)} %fusion.34), channel_id=1, source_target_pairs={{0,480},{32,0},{64,32},{96,64},{128,96},{160,128},{192,160},{224,1... | collective-permute-start | bytes 3145736 | tf_op jit(solution)/shard_map/ppermute | solution.py:73
  533.1 27.1 %collective-permute-start.28 = (bf16[2,128,2048]{2,1,0:T(8,128)(2,1)S(1)}, bf16[2,128,2048]{2,1,0:T(8,128)(2,1)S(1)}, u32[]{:S(2)}, u32[]{:S(2)}) collective-permute-start(bf16[2,128,2048]{2,1,0:T(8,128)(2,1)S(1)} %fusion.33), channel_id=1, source_target_pairs={{0,480},{32,0},{64,32},{96,64},{128,96},{160,128},{192,160},{224,1... | collective-permute-start | bytes 3145736 | tf_op jit(solution)/shard_map/ppermute | solution.py:73
  560.6 26.6 %collective-permute-start.29 = (bf16[2,128,2048]{2,1,0:T(8,128)(2,1)S(1)}, bf16[2,128,2048]{2,1,0:T(8,128)(2,1)S(1)}, u32[]{:S(2)}, u32[]{:S(2)}) collective-permute-start(bf16[2,128,2048]{2,1,0:T(8,128)(2,1)S(1)} %fusion.32), channel_id=1, source_target_pairs={{0,480},{32,0},{64,32},{96,64},{128,96},{160,128},{192,160},{224,1... | collective-permute-start | bytes 3145736 | tf_op jit(solution)/shard_map/ppermute | solution.py:73
  587.6 28.6 %collective-permute-start.30 = (bf16[2,128,2048]{2,1,0:T(8,128)(2,1)S(1)}, bf16[2,128,2048]{2,1,0:T(8,128)(2,1)S(1)}, u32[]{:S(2)}, u32[]{:S(2)}) collective-permute-start(bf16[2,128,2048]{2,1,0:T(8,128)(2,1)S(1)} %fusion.31), channel_id=1, source_target_pairs={{0,480},{32,0},{64,32},{96,64},{128,96},{160,128},{192,160},{224,1... | collective-permute-start | bytes 3145736 | tf_op jit(solution)/shard_map/ppermute | solution.py:73
  593.2 57.3 %collective-permute-start.24 = (bf16[2,128,2048]{2,1,0:T(8,128)(2,1)S(1)}, bf16[2,128,2048]{2,1,0:T(8,128)(2,1)S(1)}, u32[]{:S(2)}, u32[]{:S(2)}) collective-permute-start(bf16[2,128,2048]{2,1,0:T(8,128)(2,1)S(1)} %get-tuple-element.5), channel_id=1, source_target_pairs={{0,32},{32,64},{64,96},{96,128},{128,160},{160,192},{192,224},{224... | collective-permute-start | bytes 3145736 | tf_op jit(solution)/shard_map/ppermute | solution.py:73
  617.6 32.9 %collective-permute-start.31 = (bf16[2,128,2048]{2,1,0:T(8,128)(2,1)}, bf16[2,128,2048]{2,1,0:T(8,128)(2,1)S(1)}, u32[]{:S(2)}, u32[]{:S(2)}) collective-permute-start(bf16[2,128,2048]{2,1,0:T(8,128)(2,1)} %fusion.30), channel_id=1, source_target_pairs={{0,480},{32,0},{64,32},{96,64},{128,96},{160,128},{192,160},{224,1... | collective-permute-start | bytes 3145736 | tf_op jit(solution)/shard_map/ppermute | solution.py:73

commit v3 on v2

--- a/solution.py
+++ b/solution.py
@@ -110,10 +110,11 @@
     going_up, going_down = held, held
     for step in range(1, ahead + 1):
         going_up = ring_step(going_up, "grp", 1)
-        ahead_blocks.append(going_up)
         if step <= behind:
             going_down = ring_step(going_down, "grp", -1)
+            going_up, going_down = lax.optimization_barrier((going_up, going_down))
             behind_blocks.append(going_down)
+        ahead_blocks.append(going_up)
     all_blocks = jnp.stack([held] + behind_blocks + ahead_blocks[::-1], axis=0)
     key_heads = split_heads(all_blocks[:, 0])
     value_heads = split_heads(all_blocks[:, 1])
@@ -147,13 +148,14 @@
         axis=1,
     ).astype(jnp.bfloat16)
     up_sum = terms[ahead]
+    down_sum = terms[groups - behind]
     for step in range(1, ahead + 1):
         up_arrived = ring_step(up_sum, "grp", 1).astype(jnp.float32)
+        if step <= behind:
+            down_arrived = ring_step(down_sum, "grp", -1).astype(jnp.float32)
+            up_arrived, down_arrived = lax.optimization_barrier((up_arrived, down_arrived))
         if step < ahead:
             up_sum = (up_arrived + terms[ahead - step]).astype(jnp.bfloat16)
-    down_sum = terms[groups - behind]
-    for step in range(1, behind + 1):
-        down_arrived = ring_step(down_sum, "grp", -1).astype(jnp.float32)
         if step < behind:
             down_sum = (down_arrived + terms[groups - behind + step]).astype(jnp.bfloat16)
     total = up_arrived + down_arrived + terms[0].astype(jnp.float32)

time: 656 us -> 533 us (0.81)
  waiting for transfers between devices: 370 us -> 227 us
  starting transfers between devices: 108 us -> 123 us
    ppermute x30, waiting for transfers between devices: 370 us -> 227 us  [ring_step(): return lax.ppermute(array, axis, pairs)]
    ppermute x30, starting transfers between devices: 101 us -> 116 us  [ring_step(): return lax.ppermute(array, axis, pairs)]
  transfers between devices with their start and end apart: 32 -> 32, of which waited for: 24 -> 28; matrix products, arithmetic and copies ran while one was open for 9% -> 11% of each run, Pallas kernels for 0% -> 0%
where the time goes in v3:
time: 533 us; the launch traced here: 530 us
  waiting for transfers between devices  227 us (43%)
  starting transfers between devices  123 us (23%)
  local copies, waits for them, and re-layouts  91.9 us (17%)
  matrix products  57.1 us (11%)
  other arithmetic  29 us (5%)
    ppermute x30, waiting for transfers between devices, ring_step(): return lax.ppermute(array, axis, pairs)  227 us
    ppermute x30, starting transfers between devices, ring_step(): return lax.ppermute(array, axis, pairs)  116 us
    unnamed x42, local copies, waits for them, and re-layouts  30.2 us
    dot_general x1, matrix products, slot_backward(): jnp.einsum('nqhk,nkhd->nqhd', grad_scores, key_heads, preferred_element_t...  12.4 us
    another operation x1, local copies, waits for them, and re-layouts, shards(): jnp.stack([key_term.reshape(groups, neighbour_len, row_width) * score_sca...  12.3 us
    mul x1, local copies, waits for them, and re-layouts, shards(): key_term.reshape(groups, neighbour_len, row_width) * score_scale  12.3 us
  transfers between devices with their start and end apart: 32, of which 28 were waited for; matrix products, arithmetic and copies ran while one was open for 11% of the time, Pallas kernels for 0%

profile of v3, /device:TPU:6, one launch (start us, length us, event | category | flops | bytes accessed | tf_op | source)
XLA Modules:
  0.0 530.1 jit_solution(852285077219935046)
XLA Ops:
  3.4 3.8 collective-permute-start
  7.2 9.5 %collective-permute-start.1 = (bf16[2,128,2048]{1,2,0:T(8,128)(2,1)S(1)}, bf16[2,128,2048]{1,2,0:T(8,128)(2,1)S(1)}, u32[]{:S(2)}, u32[]{:S(2)}) collective-permute-start(bf16[2,128,2048]{1,2,0:T(8,128)(2,1)S(1)} %pad_maximum_fusion.1), channel_id=1, source_target_pairs={{0,480},{32,0},{64,32},{96,64},{128,96},{160,128},{192,160},{224,1... | collective-permute-start | bytes 3145736 | tf_op jit(solution)/shard_map/ppermute | solution.py:73
  16.7 21.2 %collective-permute-done = bf16[2,128,2048]{1,2,0:T(8,128)(2,1)S(1)} collective-permute-done((bf16[2,128,2048]{1,2,0:T(8,128)(2,1)S(1)}, bf16[2,128,2048]{1,2,0:T(8,128)(2,1)S(1)}, u32[]{:S(2)}, u32[]{:S(2)}) %collective-permute-start) | collective-permute-done | bytes 1048608 | tf_op jit(solution)/shard_map/ppermute | solution.py:73
  41.1 5.6 %collective-permute-start.3 = (bf16[2,128,2048]{1,2,0:T(8,128)(2,1)S(1)}, bf16[2,128,2048]{1,2,0:T(8,128)(2,1)}, u32[]{:S(2)}, u32[]{:S(2)}) collective-permute-start(bf16[2,128,2048]{1,2,0:T(8,128)(2,1)S(1)} %collective-permute-done.1), channel_id=1, source_target_pairs={{0,480},{32,0},{64,32},{96,64},{128,96},{160,128},{192,160},{224,1... | collective-permute-start | bytes 3145736 | tf_op jit(solution)/shard_map/ppermute | solution.py:73
  46.7 20.3 %collective-permute-done.2 = bf16[2,128,2048]{1,2,0:T(8,128)(2,1)S(1)} collective-permute-done((bf16[2,128,2048]{1,2,0:T(8,128)(2,1)S(1)}, bf16[2,128,2048]{1,2,0:T(8,128)(2,1)S(1)}, u32[]{:S(2)}, u32[]{:S(2)}) %collective-permute-start.2) | collective-permute-done | bytes 1048608 | tf_op jit(solution)/shard_map/ppermute | solution.py:73
  70.1 5.7 %collective-permute-start.5 = (bf16[2,128,2048]{1,2,0:T(8,128)(2,1)}, bf16[2,128,2048]{1,2,0:T(8,128)(2,1)}, u32[]{:S(2)}, u32[]{:S(2)}) collective-permute-start(bf16[2,128,2048]{1,2,0:T(8,128)(2,1)} %collective-permute-done.3), channel_id=1, source_target_pairs={{0,480},{32,0},{64,32},{96,64},{128,96},{160,128},{192,160},{224,1... | collective-permute-start | bytes 3145736 | tf_op jit(solution)/shard_map/ppermute | solution.py:73
  77.5 2.5 collective-permute-start.15
  81.0 4.7 collective-permute-start.16
  87.3 7.9 %collective-permute-done.4 = bf16[2,128,2048]{1,2,0:T(8,128)(2,1)S(1)} collective-permute-done((bf16[2,128,2048]{1,2,0:T(8,128)(2,1)S(1)}, bf16[2,128,2048]{1,2,0:T(8,128)(2,1)S(1)}, u32[]{:S(2)}, u32[]{:S(2)}) %collective-permute-start.4) | collective-permute-done | bytes 1048608 | tf_op jit(solution)/shard_map/ppermute | solution.py:73
  98.7 5.6 %collective-permute-start.7 = (bf16[2,128,2048]{1,2,0:T(8,128)(2,1)}, bf16[2,128,2048]{1,2,0:T(8,128)(2,1)}, u32[]{:S(2)}, u32[]{:S(2)}) collective-permute-start(bf16[2,128,2048]{1,2,0:T(8,128)(2,1)} %collective-permute-done.5), channel_id=1, source_target_pairs={{0,480},{32,0},{64,32},{96,64},{128,96},{160,128},{192,160},{224,1... | collective-permute-start | bytes 3145736 | tf_op jit(solution)/shard_map/ppermute | solution.py:73
  105.7 17.2 %collective-permute-done.6 = bf16[2,128,2048]{1,2,0:T(8,128)(2,1)} collective-permute-done((bf16[2,128,2048]{1,2,0:T(8,128)(2,1)S(1)}, bf16[2,128,2048]{1,2,0:T(8,128)(2,1)}, u32[]{:S(2)}, u32[]{:S(2)}) %collective-permute-start.6) | collective-permute-done | bytes 1048608 | tf_op jit(solution)/shard_map/ppermute | solution.py:73
  124.3 3.6 collective-permute-start.8
  127.9 3.9 collective-permute-start.9
  134.9 14.8 %collective-permute-done.8 = bf16[2,128,2048]{1,2,0:T(8,128)(2,1)} collective-permute-done((bf16[2,128,2048]{1,2,0:T(8,128)(2,1)}, bf16[2,128,2048]{1,2,0:T(8,128)(2,1)}, u32[]{:S(2)}, u32[]{:S(2)}) %collective-permute-start.8) | collective-permute-done | bytes 1048608 | tf_op jit(solution)/shard_map/ppermute | solution.py:73
  150.9 3.2 collective-permute-start.10
  154.1 4.3 collective-permute-start.11
  159.5 2.9 gather_fusion.1
  163.4 2.8 gather_fusion.5
  166.3 2.4 bitcast_dynamic-update-slice_fusion.13
  168.6 6.8 %collective-permute-done.10 = bf16[2,128,2048]{1,2,0:T(8,128)(2,1)} collective-permute-done((bf16[2,128,2048]{1,2,0:T(8,128)(2,1)}, bf16[2,128,2048]{1,2,0:T(8,128)(2,1)}, u32[]{:S(2)}, u32[]{:S(2)}) %collective-permute-start.10) | collective-permute-done | bytes 1048608 | tf_op jit(solution)/shard_map/ppermute | solution.py:73
  176.6 2.3 collective-permute-start.12
  178.8 5.3 collective-permute-start.13
  184.1 2.4 bitcast_dynamic-update-slice_fusion.12
  186.4 2.4 bitcast_dynamic-update-slice_fusion.11
  188.8 2.4 bitcast_dynamic-update-slice_fusion.10
  191.2 8.8 %collective-permute-done.12 = bf16[2,128,2048]{1,2,0:T(8,128)(2,1)S(1)} collective-permute-done((bf16[2,128,2048]{1,2,0:T(8,128)(2,1)}, bf16[2,128,2048]{1,2,0:T(8,128)(2,1)S(1)}, u32[]{:S(2)}, u32[]{:S(2)}) %collective-permute-start.12) | collective-permute-done | bytes 1048608 | tf_op jit(solution)/shard_map/ppermute | solution.py:73
  203.2 2.4 bitcast_dynamic-update-slice_fusion.9
  205.6 2.4 bitcast_dynamic-update-slice_fusion.8
  209.1 14.5 %collective-permute-done.14 = bf16[2,128,2048]{1,2,0:T(8,128)(2,1)S(1)} collective-permute-done((bf16[2,128,2048]{1,2,0:T(8,128)(2,1)S(1)}, bf16[2,128,2048]{1,2,0:T(8,128)(2,1)S(1)}, u32[]{:S(2)}, u32[]{:S(2)}) %collective-permute-start.14) | collective-permute-done | bytes 1048608 | tf_op jit(solution)/shard_map/ppermute | solution.py:73
  225.7 2.4 bitcast_dynamic-update-slice_fusion.4
  228.0 2.4 bitcast_dynamic-update-slice_fusion.3
  230.4 2.4 bitcast_dynamic-update-slice_fusion.2
  236.0 9.3 %fusion.73 = (bf16[16,1,128,2048]{2,3,0,1:T(8,128)(2,1)}, bf16[16,1,128,2048]{2,3,0,1:T(8,128)(2,1)S(1)}) fusion(bf16[16,2,128,2048]{2,3,0,1:T(8,128)(2,1)} %bitcast_dynamic-update-slice_fusion.15), kind=kLoop, calls=%fused_computation.179 | loop fusion | bytes 33554432 | tf_op jit(solution)/shard_map/slice | solution.py:120
  246.0 5.0 bitcast_reduce_fusion
  251.6 6.8 %fusion.8 = f32[16,64,16]{1,2,0:T(8,128)S(1)} fusion(f32[16,16,128,64]{2,3,1,0:T(8,128)} %get-tuple-element.82, f32[16,64,16]{1,2,0:T(8,128)S(1)} %get-tuple-element.81), kind=kLoop, calls=%fused_computation.54 | loop fusion | flops 6275072 | bytes 8519680 | tf_op jit(solution)/shard_map/reduce_sum | solution.py:29
  259.0 10.4 %fusion.5 = f32[16,64,16]{1,2,0:T(8,128)S(1)} fusion(f32[16,64,16]{1,2,0:T(8,128)S(1)} %fusion.8, bf16[16,128,16,128]{1,3,2,0:T(8,128)(2,1)} %bitcast.240, f32[16,16,128,64]{2,3,1,0:T(8,128)} %get-tuple-element.82, f32[16,64,16]{1,2,0:T(8,128)S(1)} %get-tuple-element.81, bf16[16,64,2048]{2,1,0:T(8,128)(2,1)} %gather_fusion.5), kind=kOutput, calls=%fused_computation.51 | convolution fusion | flops 551534592 | bytes 21168128 | tf_op jit(solution)/shard_map/nqhk,nkhd->nqhd/dot_general | solution.py:31
  271.2 9.9 %convolution_convert_fusion = bf16[16,16,128,128]{3,2,1,0:T(8,128)(2,1)} fusion(f32[16,16,128,64]{2,3,1,0:T(8,128)} %get-tuple-element.82, f32[16,64,16]{1,2,0:T(8,128)S(1)} %gather_fusion.4, bf16[16,64,2048]{2,1,0:T(8,128)(2,1)} %gather_fusion.5), kind=kOutput, calls=%fused_computation.55 | convolution fusion | flops 547356672 | bytes 21037056 | tf_op jit(solution)/shard_map/nqhk,nqhd->nkhd/dot_general | solution.py:58
  281.1 10.0 %fusion.2 = bf16[16,64,16,128]{3,1,2,0:T(8,128)(2,1)} fusion(f32[16,16,128,64]{2,3,1,0:T(8,128)} %get-tuple-element.82, f32[16,64,16]{1,2,0:T(8,128)S(1)} %gather_fusion.7, f32[16,64,16]{1,2,0:T(8,128)S(1)} %gather_fusion.4, bf16[16,128,16,128]{1,3,2,0:T(8,128)(2,1)} %bitcast.241, bf16[16,64,2048]{2,1,0:T(8,128)(2,1)S(1)} %copy-done.2), kind=kOutput, calls=%fused_computation.44 | convolution fusion | flops 547356672 | bytes 25296896 | tf_op jit(solution)/shard_map/nqhd,nkhd->nqhk/dot_general | solution.py:50
  291.1 12.3 %copy.67 = bf16[16,1,128,2048]{3,2,1,0:T(8,128)(2,1)} copy(bf16[16,1,128,2048]{2,3,0,1:T(8,128)(2,1)} %bitcast.242) | data formatting | bytes 16777216 | tf_op jit(solution)/shard_map/stack;reshape | solution.py:145
  303.5 9.4 %multiply_convert_fusion = bf16[16,16,128,128]{3,2,1,0:T(8,128)(2,1)} fusion(bf16[16,64,16,128]{3,1,2,0:T(8,128)(2,1)} %fusion.2, bf16[16,64,2048]{2,1,0:T(8,128)(2,1)} %gather_fusion.1), kind=kOutput, calls=%fused_computation.39 | convolution fusion | flops 545259520 | bytes 16777216 | tf_op jit(solution)/shard_map/nqhk,nqhd->nkhd/dot_general | solution.py:64
  312.9 12.3 %copy.66 = bf16[16,1,128,2048]{3,2,1,0:T(8,128)(2,1)} copy(bf16[16,1,128,2048]{2,3,0,1:T(8,128)(2,1)} %bitcast.243) | data formatting | bytes 16777216 | tf_op jit(solution)/shard_map/mul | solution.py:146
  327.0 2.2 collective-permute-start.17
  329.2 5.1 collective-permute-start.18
  334.4 13.9 %collective-permute-done.17 = bf16[2,128,2048]{2,1,0:T(8,128)(2,1)S(1)} collective-permute-done((bf16[2,128,2048]{2,1,0:T(8,128)(2,1)S(1)}, bf16[2,128,2048]{2,1,0:T(8,128)(2,1)S(1)}, u32[]{:S(2)}, u32[]{:S(2)}) %collective-permute-start.17) | collective-permute-done | bytes 1048608 | tf_op jit(solution)/shard_map/ppermute | solution.py:73
  353.8 5.6 %collective-permute-start.20 = (bf16[2,128,2048]{2,1,0:T(8,128)(2,1)S(1)}, bf16[2,128,2048]{2,1,0:T(8,128)(2,1)S(1)}, u32[]{:S(2)}, u32[]{:S(2)}) collective-permute-start(bf16[2,128,2048]{2,1,0:T(8,128)(2,1)S(1)} %get-tuple-element.71), channel_id=1, source_target_pairs={{0,480},{32,0},{64,32},{96,64},{128,96},{160,128},{192,160},{224,1... | collective-permute-start | bytes 3145736 | tf_op jit(solution)/shard_map/ppermute | solution.py:73
  359.4 13.6 %collective-permute-done.19 = bf16[2,128,2048]{2,1,0:T(8,128)(2,1)S(1)} collective-permute-done((bf16[2,128,2048]{2,1,0:T(8,128)(2,1)S(1)}, bf16[2,128,2048]{2,1,0:T(8,128)(2,1)S(1)}, u32[]{:S(2)}, u32[]{:S(2)}) %collective-permute-start.19) | collective-permute-done | bytes 1048608 | tf_op jit(solution)/shard_map/ppermute | solution.py:73
  377.2 5.6 %collective-permute-start.22 = (bf16[2,128,2048]{2,1,0:T(8,128)(2,1)S(1)}, bf16[2,128,2048]{2,1,0:T(8,128)(2,1)S(1)}, u32[]{:S(2)}, u32[]{:S(2)}) collective-permute-start(bf16[2,128,2048]{2,1,0:T(8,128)(2,1)S(1)} %get-tuple-element.69), channel_id=1, source_target_pairs={{0,480},{32,0},{64,32},{96,64},{128,96},{160,128},{192,160},{224,1... | collective-permute-start | bytes 3145736 | tf_op jit(solution)/shard_map/ppermute | solution.py:73
  382.8 13.7 %collective-permute-done.21 = bf16[2,128,2048]{2,1,0:T(8,128)(2,1)S(1)} collective-permute-done((bf16[2,128,2048]{2,1,0:T(8,128)(2,1)S(1)}, bf16[2,128,2048]{2,1,0:T(8,128)(2,1)S(1)}, u32[]{:S(2)}, u32[]{:S(2)}) %collective-permute-start.21) | collective-permute-done | bytes 1048608 | tf_op jit(solution)/shard_map/ppermute | solution.py:73
  400.5 5.6 %collective-permute-start.24 = (bf16[2,128,2048]{2,1,0:T(8,128)(2,1)S(1)}, bf16[2,128,2048]{2,1,0:T(8,128)(2,1)S(1)}, u32[]{:S(2)}, u32[]{:S(2)}) collective-permute-start(bf16[2,128,2048]{2,1,0:T(8,128)(2,1)S(1)} %get-tuple-element.67), channel_id=1, source_target_pairs={{0,480},{32,0},{64,32},{96,64},{128,96},{160,128},{192,160},{224,1... | collective-permute-start | bytes 3145736 | tf_op jit(solution)/shard_map/ppermute | solution.py:73
  406.1 13.7 %collective-permute-done.23 = bf16[2,128,2048]{2,1,0:T(8,128)(2,1)S(1)} collective-permute-done((bf16[2,128,2048]{2,1,0:T(8,128)(2,1)S(1)}, bf16[2,128,2048]{2,1,0:T(8,128)(2,1)S(1)}, u32[]{:S(2)}, u32[]{:S(2)}) %collective-permute-start.23) | collective-permute-done | bytes 1048608 | tf_op jit(solution)/shard_map/ppermute | solution.py:73
  421.9 2.3 collective-permute-start.25
  424.2 5.2 collective-permute-start.26
  429.4 14.0 %collective-permute-done.25 = bf16[2,128,2048]{2,1,0:T(8,128)(2,1)S(1)} collective-permute-done((bf16[2,128,2048]{2,1,0:T(8,128)(2,1)S(1)}, bf16[2,128,2048]{2,1,0:T(8,128)(2,1)S(1)}, u32[]{:S(2)}, u32[]{:S(2)}) %collective-permute-start.25) | collective-permute-done | bytes 1048608 | tf_op jit(solution)/shard_map/ppermute | solution.py:73
  446.2 3.1 collective-permute-start.27
  449.3 4.4 collective-permute-start.28
  453.7 15.1 %collective-permute-done.27 = bf16[2,128,2048]{2,1,0:T(8,128)(2,1)S(1)} collective-permute-done((bf16[2,128,2048]{2,1,0:T(8,128)(2,1)S(1)}, bf16[2,128,2048]{2,1,0:T(8,128)(2,1)S(1)}, u32[]{:S(2)}, u32[]{:S(2)}) %collective-permute-start.27) | collective-permute-done | bytes 1048608 | tf_op jit(solution)/shard_map/ppermute | solution.py:73
  472.2 4.1 collective-permute-start.29
  476.2 3.0 collective-permute-start.30
  479.2 15.6 %collective-permute-done.29 = bf16[2,128,2048]{2,1,0:T(8,128)(2,1)S(1)} collective-permute-done((bf16[2,128,2048]{2,1,0:T(8,128)(2,1)S(1)}, bf16[2,128,2048]{2,1,0:T(8,128)(2,1)S(1)}, u32[]{:S(2)}, u32[]{:S(2)}) %collective-permute-start.29) | collective-permute-done | bytes 1048608 | tf_op jit(solution)/shard_map/ppermute | solution.py:73
  496.6 3.8 collective-permute-start.31
  500.4 12.4 %fusion.12 = bf16[16,16,8,8,128]{4,3,2,1,0:T(8,128)(2,1)} fusion(bf16[16,128,16,128]{1,3,2,0:T(8,128)(2,1)} %bitcast.239, bf16[16,64,16,128]{3,1,2,0:T(8,128)(2,1)} %fusion.2), kind=kOutput, calls=%fused_computation.57 | convolution fusion | flops 541065216 | bytes 16777216 | tf_op jit(solution)/shard_map/nqhk,nkhd->nqhd/dot_general | solution.py:55
  512.8 5.4 %copy.95 = bf16[16,16,8,8,128]{4,3,1,2,0:T(8,128)(2,1)} copy(bf16[16,16,8,8,128]{4,3,2,1,0:T(8,128)(2,1)} %fusion.12) | data formatting | bytes 8388608 | tf_op jit(solution)/shard_map/reshape | solution.py:67
  518.2 4.9 gather_fusion.8
  523.1 4.3 bitcast_reduce_fusion.1
  (110 shorter events, 68.2 us)
Async XLA Ops:
  3.4 34.6 %collective-permute-start = (bf16[2,128,2048]{1,2,0:T(8,128)(2,1)S(1)}, bf16[2,128,2048]{1,2,0:T(8,128)(2,1)S(1)}, u32[]{:S(2)}, u32[]{:S(2)}) collective-permute-start(bf16[2,128,2048]{1,2,0:T(8,128)(2,1)S(1)} %pad_maximum_fusion.1), channel_id=1, source_target_pairs={{0,32},{32,64},{64,96},{96,128},{128,160},{160,192},{192,224},{224... | collective-permute-start | bytes 3145736 | tf_op jit(solution)/shard_map/ppermute | solution.py:73
  7.2 31.9 %collective-permute-start.1 = (bf16[2,128,2048]{1,2,0:T(8,128)(2,1)S(1)}, bf16[2,128,2048]{1,2,0:T(8,128)(2,1)S(1)}, u32[]{:S(2)}, u32[]{:S(2)}) collective-permute-start(bf16[2,128,2048]{1,2,0:T(8,128)(2,1)S(1)} %pad_maximum_fusion.1), channel_id=1, source_target_pairs={{0,480},{32,0},{64,32},{96,64},{128,96},{160,128},{192,160},{224,1... | collective-permute-start | bytes 3145736 | tf_op jit(solution)/shard_map/ppermute | solution.py:73
  38.0 1.2 copy-start.4
  39.1 27.9 %copy-start.10 = (bf16[2,128,2048]{1,2,0:T(8,128)(2,1)}, bf16[2,128,2048]{1,2,0:T(8,128)(2,1)S(1)}, u32[]{:S(2)}) copy-start(bf16[2,128,2048]{1,2,0:T(8,128)(2,1)S(1)} %collective-permute-done.1) | copy-start | bytes 3145732
  39.1 27.9 %collective-permute-start.2 = (bf16[2,128,2048]{1,2,0:T(8,128)(2,1)S(1)}, bf16[2,128,2048]{1,2,0:T(8,128)(2,1)S(1)}, u32[]{:S(2)}, u32[]{:S(2)}) collective-permute-start(bf16[2,128,2048]{1,2,0:T(8,128)(2,1)S(1)} %collective-permute-done), channel_id=1, source_target_pairs={{0,32},{32,64},{64,96},{96,128},{128,160},{160,192},{192,224},{224... | collective-permute-start | bytes 3145736 | tf_op jit(solution)/shard_map/ppermute | solution.py:73
  41.1 27.1 %collective-permute-start.3 = (bf16[2,128,2048]{1,2,0:T(8,128)(2,1)S(1)}, bf16[2,128,2048]{1,2,0:T(8,128)(2,1)}, u32[]{:S(2)}, u32[]{:S(2)}) collective-permute-start(bf16[2,128,2048]{1,2,0:T(8,128)(2,1)S(1)} %collective-permute-done.1), channel_id=1, source_target_pairs={{0,480},{32,0},{64,32},{96,64},{128,96},{160,128},{192,160},{224,1... | collective-permute-start | bytes 3145736 | tf_op jit(solution)/shard_map/ppermute | solution.py:73
  67.0 37.3 %copy-start.6 = (bf16[2,128,2048]{1,2,0:T(8,128)(2,1)}, bf16[2,128,2048]{1,2,0:T(8,128)(2,1)S(1)}, u32[]{:S(2)}) copy-start(bf16[2,128,2048]{1,2,0:T(8,128)(2,1)S(1)} %collective-permute-done.2) | copy-start | bytes 3145732
  68.2 27.1 %collective-permute-start.4 = (bf16[2,128,2048]{1,2,0:T(8,128)(2,1)S(1)}, bf16[2,128,2048]{1,2,0:T(8,128)(2,1)S(1)}, u32[]{:S(2)}, u32[]{:S(2)}) collective-permute-start(bf16[2,128,2048]{1,2,0:T(8,128)(2,1)S(1)} %collective-permute-done.2), channel_id=1, source_target_pairs={{0,32},{32,64},{64,96},{96,128},{128,160},{160,192},{192,224},{224... | collective-permute-start | bytes 3145736 | tf_op jit(solution)/shard_map/ppermute | solution.py:73
  70.1 26.6 %collective-permute-start.5 = (bf16[2,128,2048]{1,2,0:T(8,128)(2,1)}, bf16[2,128,2048]{1,2,0:T(8,128)(2,1)}, u32[]{:S(2)}, u32[]{:S(2)}) collective-permute-start(bf16[2,128,2048]{1,2,0:T(8,128)(2,1)} %collective-permute-done.3), channel_id=1, source_target_pairs={{0,480},{32,0},{64,32},{96,64},{128,96},{160,128},{192,160},{224,1... | collective-permute-start | bytes 3145736 | tf_op jit(solution)/shard_map/ppermute | solution.py:73
  77.5 80.9 %collective-permute-start.15 = (bf16[63,2048]{1,0:T(8,128)(2,1)}, bf16[63,2048]{1,0:T(8,128)(2,1)}, u32[]{:S(2)}, u32[]{:S(2)}) collective-permute-start(bf16[63,2048]{1,0:T(8,128)(2,1)} %slice_bitcast_fusion.5), channel_id=1, source_target_pairs={{1,0},{2,1},{3,2},{4,3},{5,4},{6,5},{7,6},{8,7},{9,8},{10,9},{11,1... | collective-permute-start | bytes 774152 | tf_op jit(solution)/shard_map/ppermute | solution.py:15
  81.0 81.3 %collective-permute-start.16 = (bf16[63,2048]{1,0:T(8,128)(2,1)S(1)}, bf16[63,2048]{1,0:T(8,128)(2,1)}, u32[]{:S(2)}, u32[]{:S(2)}) collective-permute-start(bf16[63,2048]{1,0:T(8,128)(2,1)S(1)} %slice_bitcast_fusion.4), channel_id=1, source_target_pairs={{1,0},{2,1},{3,2},{4,3},{5,4},{6,5},{7,6},{8,7},{9,8},{10,9},{11,1... | collective-permute-start | bytes 774152 | tf_op jit(solution)/shard_map/ppermute | solution.py:15
  95.3 37.2 %copy-start.8 = (bf16[2,128,2048]{1,2,0:T(8,128)(2,1)}, bf16[2,128,2048]{1,2,0:T(8,128)(2,1)S(1)}, u32[]{:S(2)}) copy-start(bf16[2,128,2048]{1,2,0:T(8,128)(2,1)S(1)} %collective-permute-done.4) | copy-start | bytes 3145732
  96.7 26.1 %collective-permute-start.6 = (bf16[2,128,2048]{1,2,0:T(8,128)(2,1)S(1)}, bf16[2,128,2048]{1,2,0:T(8,128)(2,1)}, u32[]{:S(2)}, u32[]{:S(2)}) collective-permute-start(bf16[2,128,2048]{1,2,0:T(8,128)(2,1)S(1)} %collective-permute-done.4), channel_id=1, source_target_pairs={{0,32},{32,64},{64,96},{96,128},{128,160},{160,192},{192,224},{224... | collective-permute-start | bytes 3145736 | tf_op jit(solution)/shard_map/ppermute | solution.py:73
  98.7 25.6 %collective-permute-start.7 = (bf16[2,128,2048]{1,2,0:T(8,128)(2,1)}, bf16[2,128,2048]{1,2,0:T(8,128)(2,1)}, u32[]{:S(2)}, u32[]{:S(2)}) collective-permute-start(bf16[2,128,2048]{1,2,0:T(8,128)(2,1)} %collective-permute-done.5), channel_id=1, source_target_pairs={{0,480},{32,0},{64,32},{96,64},{128,96},{160,128},{192,160},{224,1... | collective-permute-start | bytes 3145736 | tf_op jit(solution)/shard_map/ppermute | solution.py:73
  124.3 25.4 %collective-permute-start.8 = (bf16[2,128,2048]{1,2,0:T(8,128)(2,1)}, bf16[2,128,2048]{1,2,0:T(8,128)(2,1)}, u32[]{:S(2)}, u32[]{:S(2)}) collective-permute-start(bf16[2,128,2048]{1,2,0:T(8,128)(2,1)} %collective-permute-done.6), channel_id=1, source_target_pairs={{0,32},{32,64},{64,96},{96,128},{128,160},{160,192},{192,224},{224... | collective-permute-start | bytes 3145736 | tf_op jit(solution)/shard_map/ppermute | solution.py:73
  127.9 23.0 %collective-permute-start.9 = (bf16[2,128,2048]{1,2,0:T(8,128)(2,1)}, bf16[2,128,2048]{1,2,0:T(8,128)(2,1)}, u32[]{:S(2)}, u32[]{:S(2)}) collective-permute-start(bf16[2,128,2048]{1,2,0:T(8,128)(2,1)} %collective-permute-done.7), channel_id=1, source_target_pairs={{0,480},{32,0},{64,32},{96,64},{128,96},{160,128},{192,160},{224,1... | collective-permute-start | bytes 3145736 | tf_op jit(solution)/shard_map/ppermute | solution.py:73
  150.9 24.5 %collective-permute-start.10 = (bf16[2,128,2048]{1,2,0:T(8,128)(2,1)}, bf16[2,128,2048]{1,2,0:T(8,128)(2,1)}, u32[]{:S(2)}, u32[]{:S(2)}) collective-permute-start(bf16[2,128,2048]{1,2,0:T(8,128)(2,1)} %collective-permute-done.8), channel_id=1, source_target_pairs={{0,32},{32,64},{64,96},{96,128},{128,160},{160,192},{192,224},{224... | collective-permute-start | bytes 3145736 | tf_op jit(solution)/shard_map/ppermute | solution.py:73
  154.1 22.4 %collective-permute-start.11 = (bf16[2,128,2048]{1,2,0:T(8,128)(2,1)}, bf16[2,128,2048]{1,2,0:T(8,128)(2,1)}, u32[]{:S(2)}, u32[]{:S(2)}) collective-permute-start(bf16[2,128,2048]{1,2,0:T(8,128)(2,1)} %collective-permute-done.9), channel_id=1, source_target_pairs={{0,480},{32,0},{64,32},{96,64},{128,96},{160,128},{192,160},{224,1... | collective-permute-start | bytes 3145736 | tf_op jit(solution)/shard_map/ppermute | solution.py:73
  176.6 23.5 %collective-permute-start.12 = (bf16[2,128,2048]{1,2,0:T(8,128)(2,1)}, bf16[2,128,2048]{1,2,0:T(8,128)(2,1)S(1)}, u32[]{:S(2)}, u32[]{:S(2)}) collective-permute-start(bf16[2,128,2048]{1,2,0:T(8,128)(2,1)} %collective-permute-done.10), channel_id=1, source_target_pairs={{0,32},{32,64},{64,96},{96,128},{128,160},{160,192},{192,224},{224... | collective-permute-start | bytes 3145736 | tf_op jit(solution)/shard_map/ppermute | solution.py:73
  178.8 22.5 %collective-permute-start.13 = (bf16[2,128,2048]{1,2,0:T(8,128)(2,1)}, bf16[2,128,2048]{1,2,0:T(8,128)(2,1)S(1)}, u32[]{:S(2)}, u32[]{:S(2)}) collective-permute-start(bf16[2,128,2048]{1,2,0:T(8,128)(2,1)} %collective-permute-done.11), channel_id=1, source_target_pairs={{0,480},{32,0},{64,32},{96,64},{128,96},{160,128},{192,160},{224,1... | collective-permute-start | bytes 3145736 | tf_op jit(solution)/shard_map/ppermute | solution.py:73
  191.2 41.6 %copy-start.9 = (bf16[2,128,2048]{1,2,0:T(8,128)(2,1)S(1)}, bf16[2,128,2048]{1,2,0:T(8,128)(2,1)}, u32[]{:S(2)}) copy-start(bf16[2,128,2048]{1,2,0:T(8,128)(2,1)} %copy-done.8) | copy-start | bytes 3145732
  201.3 22.2 %collective-permute-start.14 = (bf16[2,128,2048]{1,2,0:T(8,128)(2,1)S(1)}, bf16[2,128,2048]{1,2,0:T(8,128)(2,1)S(1)}, u32[]{:S(2)}, u32[]{:S(2)}) collective-permute-start(bf16[2,128,2048]{1,2,0:T(8,128)(2,1)S(1)} %collective-permute-done.12), channel_id=1, source_target_pairs={{0,32},{32,64},{64,96},{96,128},{128,160},{160,192},{192,224},{224... | collective-permute-start | bytes 3145736 | tf_op jit(solution)/shard_map/ppermute | solution.py:73
  205.6 28.3 %copy-start.7 = (bf16[2,128,2048]{1,2,0:T(8,128)(2,1)S(1)}, bf16[2,128,2048]{1,2,0:T(8,128)(2,1)}, u32[]{:S(2)}) copy-start(bf16[2,128,2048]{1,2,0:T(8,128)(2,1)} %copy-done.6) | copy-start | bytes 3145732
  208.0 26.8 %copy-start.5 = (bf16[2,128,2048]{1,2,0:T(8,128)(2,1)S(1)}, bf16[2,128,2048]{1,2,0:T(8,128)(2,1)}, u32[]{:S(2)}) copy-start(bf16[2,128,2048]{1,2,0:T(8,128)(2,1)} %copy-done.4) | copy-start | bytes 3145732
  236.0 10.1 %copy-start.3 = (bf16[16,64,2048]{2,1,0:T(8,128)(2,1)S(1)}, bf16[16,64,2048]{2,1,0:T(8,128)(2,1)}, u32[]{:S(2)}) copy-start(bf16[16,64,2048]{2,1,0:T(8,128)(2,1)} %gather_fusion.1) | copy-start | bytes 12582916
  245.2 5.8 %copy-start.1 = (bf16[16,1,128,2048]{2,3,0,1:T(8,128)(2,1)}, bf16[16,1,128,2048]{2,3,0,1:T(8,128)(2,1)S(1)}, u32[]{:S(2)}) copy-start(bf16[16,1,128,2048]{2,3,0,1:T(8,128)(2,1)S(1)} %get-tuple-element.76) | copy-start | bytes 25165828
  271.2 9.9 %copy-start.2 = (bf16[16,64,2048]{2,1,0:T(8,128)(2,1)S(1)}, bf16[16,64,2048]{2,1,0:T(8,128)(2,1)}, u32[]{:S(2)}) copy-start(bf16[16,64,2048]{2,1,0:T(8,128)(2,1)} %gather_fusion.5) | copy-start | bytes 12582916
  325.2 24.5 %copy-start = (bf16[16,1,128,2048]{3,2,1,0:T(8,128)(2,1)S(1)}, bf16[16,1,128,2048]{3,2,1,0:T(8,128)(2,1)}, u32[]{:S(2)}) copy-start(bf16[16,1,128,2048]{3,2,1,0:T(8,128)(2,1)} %copy.66) | copy-start | bytes 25165828
  327.0 21.2 %collective-permute-start.17 = (bf16[2,128,2048]{2,1,0:T(8,128)(2,1)S(1)}, bf16[2,128,2048]{2,1,0:T(8,128)(2,1)S(1)}, u32[]{:S(2)}, u32[]{:S(2)}) collective-permute-start(bf16[2,128,2048]{2,1,0:T(8,128)(2,1)S(1)} %get-tuple-element.74), channel_id=1, source_target_pairs={{0,32},{32,64},{64,96},{96,128},{128,160},{160,192},{192,224},{224... | collective-permute-start | bytes 3145736 | tf_op jit(solution)/shard_map/ppermute | solution.py:73
  329.2 20.2 %collective-permute-start.18 = (bf16[2,128,2048]{2,1,0:T(8,128)(2,1)S(1)}, bf16[2,128,2048]{2,1,0:T(8,128)(2,1)S(1)}, u32[]{:S(2)}, u32[]{:S(2)}) collective-permute-start(bf16[2,128,2048]{2,1,0:T(8,128)(2,1)S(1)} %get-tuple-element.73), channel_id=1, source_target_pairs={{0,480},{32,0},{64,32},{96,64},{128,96},{160,128},{192,160},{224,1... | collective-permute-start | bytes 3145736 | tf_op jit(solution)/shard_map/ppermute | solution.py:73
  349.4 25.1 %slice-start = ((s8[8388608]{0:T(1024)(128)(4,1)}), s8[4194304]{0:T(1024)(128)(4,1)S(1)}, s32[]{:S(2)}) async-start(s8[8388608]{0:T(1024)(128)(4,1)} %bitcast.236), calls=%async_computation | async-start | bytes 8388608
  349.7 24.8 %slice-start.1 = ((s8[8388608]{0:T(1024)(128)(4,1)}), s8[4194304]{0:T(1024)(128)(4,1)S(1)}, s32[]{:S(2)}) async-start(s8[8388608]{0:T(1024)(128)(4,1)} %bitcast.236), calls=%async_computation.1 | async-start | bytes 8388608
  351.8 21.3 %collective-permute-start.19 = (bf16[2,128,2048]{2,1,0:T(8,128)(2,1)S(1)}, bf16[2,128,2048]{2,1,0:T(8,128)(2,1)S(1)}, u32[]{:S(2)}, u32[]{:S(2)}) collective-permute-start(bf16[2,128,2048]{2,1,0:T(8,128)(2,1)S(1)} %get-tuple-element.72), channel_id=1, source_target_pairs={{0,32},{32,64},{64,96},{96,128},{128,160},{160,192},{192,224},{224... | collective-permute-start | bytes 3145736 | tf_op jit(solution)/shard_map/ppermute | solution.py:73
  353.8 20.4 %collective-permute-start.20 = (bf16[2,128,2048]{2,1,0:T(8,128)(2,1)S(1)}, bf16[2,128,2048]{2,1,0:T(8,128)(2,1)S(1)}, u32[]{:S(2)}, u32[]{:S(2)}) collective-permute-start(bf16[2,128,2048]{2,1,0:T(8,128)(2,1)S(1)} %get-tuple-element.71), channel_id=1, source_target_pairs={{0,480},{32,0},{64,32},{96,64},{128,96},{160,128},{192,160},{224,1... | collective-permute-start | bytes 3145736 | tf_op jit(solution)/shard_map/ppermute | solution.py:73
  375.2 21.2 %collective-permute-start.21 = (bf16[2,128,2048]{2,1,0:T(8,128)(2,1)S(1)}, bf16[2,128,2048]{2,1,0:T(8,128)(2,1)S(1)}, u32[]{:S(2)}, u32[]{:S(2)}) collective-permute-start(bf16[2,128,2048]{2,1,0:T(8,128)(2,1)S(1)} %get-tuple-element.70), channel_id=1, source_target_pairs={{0,32},{32,64},{64,96},{96,128},{128,160},{160,192},{192,224},{224... | collective-permute-start | bytes 3145736 | tf_op jit(solution)/shard_map/ppermute | solution.py:73
  377.2 20.5 %collective-permute-start.22 = (bf16[2,128,2048]{2,1,0:T(8,128)(2,1)S(1)}, bf16[2,128,2048]{2,1,0:T(8,128)(2,1)S(1)}, u32[]{:S(2)}, u32[]{:S(2)}) collective-permute-start(bf16[2,128,2048]{2,1,0:T(8,128)(2,1)S(1)} %get-tuple-element.69), channel_id=1, source_target_pairs={{0,480},{32,0},{64,32},{96,64},{128,96},{160,128},{192,160},{224,1... | collective-permute-start | bytes 3145736 | tf_op jit(solution)/shard_map/ppermute | solution.py:73
  398.6 21.2 %collective-permute-start.23 = (bf16[2,128,2048]{2,1,0:T(8,128)(2,1)S(1)}, bf16[2,128,2048]{2,1,0:T(8,128)(2,1)S(1)}, u32[]{:S(2)}, u32[]{:S(2)}) collective-permute-start(bf16[2,128,2048]{2,1,0:T(8,128)(2,1)S(1)} %get-tuple-element.68), channel_id=1, source_target_pairs={{0,32},{32,64},{64,96},{96,128},{128,160},{160,192},{192,224},{224... | collective-permute-start | bytes 3145736 | tf_op jit(solution)/shard_map/ppermute | solution.py:73
  400.5 20.5 %collective-permute-start.24 = (bf16[2,128,2048]{2,1,0:T(8,128)(2,1)S(1)}, bf16[2,128,2048]{2,1,0:T(8,128)(2,1)S(1)}, u32[]{:S(2)}, u32[]{:S(2)}) collective-permute-start(bf16[2,128,2048]{2,1,0:T(8,128)(2,1)S(1)} %get-tuple-element.67), channel_id=1, source_target_pairs={{0,480},{32,0},{64,32},{96,64},{128,96},{160,128},{192,160},{224,1... | collective-permute-start | bytes 3145736 | tf_op jit(solution)/shard_map/ppermute | solution.py:73
  421.9 21.6 %collective-permute-start.25 = (bf16[2,128,2048]{2,1,0:T(8,128)(2,1)S(1)}, bf16[2,128,2048]{2,1,0:T(8,128)(2,1)S(1)}, u32[]{:S(2)}, u32[]{:S(2)}) collective-permute-start(bf16[2,128,2048]{2,1,0:T(8,128)(2,1)S(1)} %get-tuple-element.66), channel_id=1, source_target_pairs={{0,32},{32,64},{64,96},{96,128},{128,160},{160,192},{192,224},{224... | collective-permute-start | bytes 3145736 | tf_op jit(solution)/shard_map/ppermute | solution.py:73
  424.2 21.0 %collective-permute-start.26 = (bf16[2,128,2048]{2,1,0:T(8,128)(2,1)S(1)}, bf16[2,128,2048]{2,1,0:T(8,128)(2,1)S(1)}, u32[]{:S(2)}, u32[]{:S(2)}) collective-permute-start(bf16[2,128,2048]{2,1,0:T(8,128)(2,1)S(1)} %get-tuple-element.65), channel_id=1, source_target_pairs={{0,480},{32,0},{64,32},{96,64},{128,96},{160,128},{192,160},{224,1... | collective-permute-start | bytes 3145736 | tf_op jit(solution)/shard_map/ppermute | solution.py:73
  446.2 22.7 %collective-permute-start.27 = (bf16[2,128,2048]{2,1,0:T(8,128)(2,1)S(1)}, bf16[2,128,2048]{2,1,0:T(8,128)(2,1)S(1)}, u32[]{:S(2)}, u32[]{:S(2)}) collective-permute-start(bf16[2,128,2048]{2,1,0:T(8,128)(2,1)S(1)} %get-tuple-element.64), channel_id=1, source_target_pairs={{0,32},{32,64},{64,96},{96,128},{128,160},{160,192},{192,224},{224... | collective-permute-start | bytes 3145736 | tf_op jit(solution)/shard_map/ppermute | solution.py:73
  449.3 21.9 %collective-permute-start.28 = (bf16[2,128,2048]{2,1,0:T(8,128)(2,1)S(1)}, bf16[2,128,2048]{2,1,0:T(8,128)(2,1)S(1)}, u32[]{:S(2)}, u32[]{:S(2)}) collective-permute-start(bf16[2,128,2048]{2,1,0:T(8,128)(2,1)S(1)} %get-tuple-element.63), channel_id=1, source_target_pairs={{0,480},{32,0},{64,32},{96,64},{128,96},{160,128},{192,160},{224,1... | collective-permute-start | bytes 3145736 | tf_op jit(solution)/shard_map/ppermute | solution.py:73
  472.2 22.6 %collective-permute-start.29 = (bf16[2,128,2048]{2,1,0:T(8,128)(2,1)S(1)}, bf16[2,128,2048]{2,1,0:T(8,128)(2,1)S(1)}, u32[]{:S(2)}, u32[]{:S(2)}) collective-permute-start(bf16[2,128,2048]{2,1,0:T(8,128)(2,1)S(1)} %get-tuple-element.62), channel_id=1, source_target_pairs={{0,32},{32,64},{64,96},{96,128},{128,160},{160,192},{192,224},{224... | collective-permute-start | bytes 3145736 | tf_op jit(solution)/shard_map/ppermute | solution.py:73
  476.2 18.8 %collective-permute-start.30 = (bf16[2,128,2048]{2,1,0:T(8,128)(2,1)S(1)}, bf16[2,128,2048]{2,1,0:T(8,128)(2,1)S(1)}, u32[]{:S(2)}, u32[]{:S(2)}) collective-permute-start(bf16[2,128,2048]{2,1,0:T(8,128)(2,1)S(1)} %get-tuple-element.61), channel_id=1, source_target_pairs={{0,480},{32,0},{64,32},{96,64},{128,96},{160,128},{192,160},{224,1... | collective-permute-start | bytes 3145736 | tf_op jit(solution)/shard_map/ppermute | solution.py:73
  496.6 30.8 %collective-permute-start.31 = (bf16[2,128,2048]{2,1,0:T(8,128)(2,1)}, bf16[2,128,2048]{2,1,0:T(8,128)(2,1)S(1)}, u32[]{:S(2)}, u32[]{:S(2)}) collective-permute-start(bf16[2,128,2048]{2,1,0:T(8,128)(2,1)} %fusion.30), channel_id=1, source_target_pairs={{0,32},{32,64},{64,96},{96,128},{128,160},{160,192},{192,224},{224... | collective-permute-start | bytes 3145736 | tf_op jit(solution)/shard_map/ppermute | solution.py:73

commit v4 on v3

v4 whole, which is shorter than its diff:
```python
import jax
import jax.numpy as jnp
from jax import lax
from jax.experimental import pallas as pl
from jax.experimental.pallas import tpu as pltpu
from jax.sharding import PartitionSpec as P

HEAD = 128
SPAN = 64
NBRS = 4


def from_behind(array, axis, by):
    length = lax.axis_size(axis)
    pairs = [(i, i + by) for i in range(length) if 0 <= i + by < length]
    return lax.ppermute(array, axis, pairs)


def span_kernel(slot_ref, query_ref, grad_ref, *refs):
    key_refs = refs[:NBRS]
    value_refs = refs[NBRS : 2 * NBRS]
    window_ref, term_ref = refs[2 * NBRS :]
    scale = HEAD ** (-0.5)
    query = query_ref[0]
    grad = grad_ref[0]
    keys = jnp.concatenate([ref[0, 0] for ref in key_refs], axis=0)
    values = jnp.concatenate([ref[0, 0] for ref in value_refs], axis=0)
    contract_last = (((1,), (1,)), ((), ()))
    scores = lax.dot_general(query, keys, contract_last, preferred_element_type=jnp.float32) * scale
    grad_probs = lax.dot_general(grad, values, contract_last, preferred_element_type=jnp.float32)
    maxes, totals, dots = [], [], []
    for j in range(NBRS):
        part = scores[:, j * HEAD : (j + 1) * HEAD]
        row_max = jnp.max(part, axis=-1, keepdims=True)
        exp_part = jnp.exp(part - row_max)
        row_total = jnp.sum(exp_part, axis=-1, keepdims=True)
        rounded = exp_part.astype(jnp.bfloat16).astype(jnp.float32)
        dotted = jnp.sum(rounded * grad_probs[:, j * HEAD : (j + 1) * HEAD], axis=-1, keepdims=True)
        maxes.append(row_max)
        totals.append(row_total)
        dots.append(dotted / row_total)
    top = maxes[0]
    for j in range(1, NBRS):
        top = jnp.maximum(top, maxes[j])
    weights = [totals[j] * jnp.exp(maxes[j] - top) for j in range(NBRS)]
    weight_sum = weights[0] + weights[1] + weights[2] + weights[3]
    weighted = weights[0] * dots[0] + weights[1] * dots[1] + weights[2] * dots[2] + weights[3] * dots[3]
    log_total = top + jnp.log(weight_sum)
    delta = weighted / weight_sum
    probs = jnp.exp(scores - log_total)
    grad_scores = (probs * (grad_probs - delta)).astype(jnp.bfloat16)
    window = jnp.zeros(query.shape, jnp.float32)
    for j in range(NBRS):
        part = lax.dot_general(
            grad_scores[:, j * HEAD : (j + 1) * HEAD],
            keys[j * HEAD : (j + 1) * HEAD],
            (((1,), (0,)), ((), ())),
            preferred_element_type=jnp.float32,
        )
        window = window + (part * scale).astype(jnp.bfloat16).astype(jnp.float32)
    window_ref[0] = window.astype(window_ref.dtype)
    probs_t = probs.astype(jnp.bfloat16).astype(jnp.float32).T.astype(jnp.bfloat16)
    scores_t = grad_scores.astype(jnp.float32).T.astype(jnp.bfloat16)
    plain = (((1,), (0,)), ((), ()))
    value_term = lax.dot_general(probs_t, grad, plain, preferred_element_type=jnp.float32)
    key_term = lax.dot_general(scores_t, query, plain, preferred_element_type=jnp.float32) * scale
    for j in range(NBRS):
        term_ref[j, 0] = key_term[j * HEAD : (j + 1) * HEAD].astype(term_ref.dtype)
        term_ref[j, 1] = value_term[j * HEAD : (j + 1) * HEAD].astype(term_ref.dtype)


def span_attention(pair_slot, window_query, window_grad, blocks):
    span_count, span_len, row_width = window_query.shape
    slot_count, _, block_len, _ = blocks.shape
    head_count = row_width // HEAD
    pair_count = span_count * NBRS

    def window_map(h, i, slots):
        return (i, 0, h)

    def block_map(j, kind):
        return lambda h, i, slots: (slots[i * NBRS + j], kind, 0, h)

    in_specs = [
        pl.BlockSpec((1, span_len, HEAD), window_map),
        pl.BlockSpec((1, span_len, HEAD), window_map),
    ]
    in_specs += [pl.BlockSpec((1, 1, block_len, HEAD), block_map(j, 0)) for j in range(NBRS)]
    in_specs += [pl.BlockSpec((1, 1, block_len, HEAD), block_map(j, 1)) for j in range(NBRS)]
    out_specs = [
        pl.BlockSpec((1, span_len, HEAD), window_map),
        pl.BlockSpec((NBRS, 2, block_len, HEAD), lambda h, i, slots: (i, 0, 0, h)),
    ]
    flops = 2 * span_len * block_len * HEAD * 9 * pair_count * head_count
    return pl.pallas_call(
        span_kernel,
        grid_spec=pltpu.PrefetchScalarGridSpec(
            num_scalar_prefetch=1,
            grid=(head_count, span_count),
            in_specs=in_specs,
            out_specs=out_specs,
        ),
        out_shape=[
            jax.ShapeDtypeStruct((span_count, span_len, row_width), jnp.bfloat16),
            jax.ShapeDtypeStruct((pair_count, 2, block_len, row_width), jnp.bfloat16),
        ],
        cost_estimate=pl.CostEstimate(
            flops=flops,
            transcendentals=2 * pair_count * span_len * block_len * head_count,
            bytes_accessed=2 * (3 * blocks.size + 4 * window_query.size),
        ),
    )(pair_slot, window_query, window_grad, *([blocks] * (2 * NBRS)))


def ring_step(array, axis, by):
    length = lax.axis_size(axis)
    pairs = [(i, (i + by) % length) for i in range(length)]
    return lax.ppermute(array, axis, pairs)


def shards(queries, grad_out, neighbour_keys, neighbour_values, neighbours):
    groups = lax.axis_size("grp")
    me = lax.axis_index("grp")
    span_len = SPAN
    tok_rows = queries.shape[1]
    row_width = queries.shape[2]
    head_count = row_width // HEAD
    neighbour_len = neighbour_keys.shape[2]
    span_count = tok_rows // span_len
    pair_count = span_count * NBRS
    assert pair_count == groups
    score_scale = HEAD ** (-0.5)
    ahead = groups // 2
    behind = groups - 1 - ahead
    next_query, next_grad = from_behind(
        (queries[0, : span_len - 1], grad_out[0, : span_len - 1]), "seq", -1
    )
    window_query = jnp.concatenate([queries[0, span_len - 1 :], next_query], axis=0).reshape(
        span_count, span_len, row_width
    )
    window_grad = jnp.concatenate([grad_out[0, span_len - 1 :], next_grad], axis=0).reshape(
        span_count, span_len, row_width
    )
    owner_ids = neighbours[0].reshape(pair_count)
    group_ids = jnp.arange(groups, dtype=jnp.int32)
    placement = (owner_ids[None, :] == group_ids[:, None]).astype(jnp.int32)
    rel_groups = (me + group_ids) % groups
    pair_slot = (owner_ids - me) % groups
    held = jnp.stack([neighbour_keys[0, 0], neighbour_values[0, 0]])
    ahead_blocks, behind_blocks = [], []
    going_up, going_down = held, held
    for step in range(1, ahead + 1):
        going_up = ring_step(going_up, "grp", 1)
        if step <= behind:
            going_down = ring_step(going_down, "grp", -1)
            going_up, going_down = lax.optimization_barrier((going_up, going_down))
            behind_blocks.append(going_down)
        ahead_blocks.append(going_up)
    all_blocks = jnp.stack([held] + behind_blocks + ahead_blocks[::-1], axis=0)
    grad_windows, pair_terms = span_attention(pair_slot, window_query, window_grad, all_blocks)
    grad_windows = grad_windows.reshape(1, span_count, span_len, row_width)
    slot_pair = jnp.sum(placement * jnp.arange(pair_count, dtype=jnp.int32)[None, :], axis=1)
    slot_pair = slot_pair[rel_groups]

    def terms(slot):
        return lax.dynamic_index_in_dim(pair_terms, slot_pair[slot], axis=0, keepdims=False)

    up_sum = terms(ahead)
    down_sum = terms(groups - behind)
    for step in range(1, ahead + 1):
        up_arrived = ring_step(up_sum, "grp", 1).astype(jnp.float32)
        if step <= behind:
            down_arrived = ring_step(down_sum, "grp", -1).astype(jnp.float32)
            up_arrived, down_arrived = lax.optimization_barrier((up_arrived, down_arrived))
        if step < ahead:
            up_sum = (up_arrived + terms(ahead - step)).astype(jnp.bfloat16)
        if step < behind:
            down_sum = (down_arrived + terms(groups - behind + step)).astype(jnp.bfloat16)
    total = up_arrived + down_arrived + terms(0).astype(jnp.float32)
    grad_keys = total[0].astype(jnp.bfloat16).reshape(1, 1, neighbour_len, row_width)
    grad_values = total[1].astype(jnp.bfloat16).reshape(1, 1, neighbour_len, row_width)
    return (grad_windows, grad_keys, grad_values)


def solution(mesh):
    in_specs = (
        P("grp", "seq", None),
        P("grp", "seq", None),
        P("grp", "seq", None, None),
        P("grp", "seq", None, None),
        P("grp", "seq", None),
    )
    out_specs = (
        P("grp", "seq", None, None),
        P("grp", "seq", None, None),
        P("grp", "seq", None, None),
    )
    return jax.shard_map(shards, mesh=mesh, in_specs=in_specs, out_specs=out_specs, check_vma=False)
```

time: 533 us -> 496 us (0.931)
  local copies, waits for them, and re-layouts: 91.9 us -> 30.4 us
  Pallas kernels: 0 us -> 57.7 us
  matrix products: 57.1 us -> 0 us
  between operations: 1.35 us -> 30.3 us
  waiting for transfers between devices: 227 us -> 216 us
  other arithmetic: 29 us -> 36.1 us
    pallas_call x0 -> x1, Pallas kernels: none -> 57.7 us  [span_attention(): pl.pallas_call(span_kernel, grid_spec=pltpu.PrefetchScalarGridSpec(num_sc...]
    dot_general x6 -> x0, matrix products: 57.1 us -> none  [the longest x1 12.4 us: slot_backward(): jnp.einsum('nqhk,nkhd->nqhd', grad_scores, key_heads, preferred_element_t...]
    gather x9 -> x1, local copies, waits for them, and re-layouts: 14.1 us -> 0.66 us  [shards(): slot_pair = slot_pair[rel_groups]]
    mul x1 -> x0, local copies, waits for them, and re-layouts: 12.3 us -> none  [shards(): key_term.reshape(groups, neighbour_len, row_width) * score_scale]
    another operation x1, local copies, waits for them, and re-layouts: 12.3 us -> 0.08 us  [shards(): owner_ids = neighbours[0].reshape(pair_count)]
    ppermute x30, waiting for transfers between devices: 227 us -> 216 us  [ring_step(): return lax.ppermute(array, axis, pairs)]
    reduce_sum x3 -> x0, other arithmetic: 11.2 us -> none  [the longest x1 6.81 us: slot_forward(): row_total = jnp.sum(exp_scores, axis=-1)]
    convert_element_type x7, other arithmetic: 1.64 us -> 10.2 us  [shards(): up_arrived = ring_step(up_sum, 'grp', 1).astype(jnp.float32)]
  transfers between devices with their start and end apart: 32 -> 32, of which waited for: 28 -> 25; matrix products, arithmetic and copies ran while one was open for 11% -> 6% of each run, Pallas kernels for 0% -> 0%
where the time goes in v4:
time: 496 us; the launch traced here: 489 us
  waiting for transfers between devices  216 us (44%)
  starting transfers between devices  119 us (24%)
  Pallas kernels  57.7 us (12%)
  other arithmetic  36.1 us (7%)
  local copies, waits for them, and re-layouts  30.4 us (6%)
  between operations  30.3 us (6%)
    ppermute x30, waiting for transfers between devices, ring_step(): return lax.ppermute(array, axis, pairs)  216 us
    ppermute x30, starting transfers between devices, ring_step(): return lax.ppermute(array, axis, pairs)  114 us
    pallas_call x1, Pallas kernels, span_attention(): pl.pallas_call(span_kernel, grid_spec=pltpu.PrefetchScalarGridSpec(num_sc...  57.7 us
    unnamed x40, local copies, waits for them, and re-layouts  23.8 us
    convert_element_type x6, other arithmetic, shards(): (down_arrived + terms(groups - behind + step)).astype(jnp.bfloat16)  13.3 us
    convert_element_type x7, other arithmetic, shards(): up_arrived = ring_step(up_sum, 'grp', 1).astype(jnp.float32)  10.2 us
  transfers between devices with their start and end apart: 32, of which 25 were waited for; matrix products, arithmetic and copies ran while one was open for 6% of the time, Pallas kernels for 0%

profile of v4, /device:TPU:6, one launch (start us, length us, event | category | flops | bytes accessed | tf_op | source)
XLA Modules:
  0.0 488.9 jit_solution(13314709621715620714)
XLA Ops:
  2.1 4.0 collective-permute-start.2
  6.0 9.5 %collective-permute-start.3 = (bf16[2,128,2048]{2,1,0:T(8,128)(2,1)S(1)}, bf16[2,128,2048]{2,1,0:T(8,128)(2,1)S(1)}, u32[]{:S(2)}, u32[]{:S(2)}) collective-permute-start(bf16[2,128,2048]{2,1,0:T(8,128)(2,1)S(1)} %pad_maximum_fusion.2), channel_id=1, source_target_pairs={{0,480},{32,0},{64,32},{96,64},{128,96},{160,128},{192,160},{224,1... | collective-permute-start | bytes 3145736 | tf_op jit(solution)/shard_map/ppermute | solution.py:118
  15.5 21.2 %collective-permute-done.2 = bf16[2,128,2048]{2,1,0:T(8,128)(2,1)S(1)} collective-permute-done((bf16[2,128,2048]{2,1,0:T(8,128)(2,1)S(1)}, bf16[2,128,2048]{2,1,0:T(8,128)(2,1)S(1)}, u32[]{:S(2)}, u32[]{:S(2)}) %collective-permute-start.2) | collective-permute-done | bytes 1048608 | tf_op jit(solution)/shard_map/ppermute | solution.py:118
  39.8 5.6 %collective-permute-start.5 = (bf16[2,128,2048]{2,1,0:T(8,128)(2,1)S(1)}, bf16[2,128,2048]{2,1,0:T(8,128)(2,1)S(1)}, u32[]{:S(2)}, u32[]{:S(2)}) collective-permute-start(bf16[2,128,2048]{2,1,0:T(8,128)(2,1)S(1)} %collective-permute-done.3), channel_id=1, source_target_pairs={{0,480},{32,0},{64,32},{96,64},{128,96},{160,128},{192,160},{224,1... | collective-permute-start | bytes 3145736 | tf_op jit(solution)/shard_map/ppermute | solution.py:118
  45.5 20.3 %collective-permute-done.4 = bf16[2,128,2048]{2,1,0:T(8,128)(2,1)S(1)} collective-permute-done((bf16[2,128,2048]{2,1,0:T(8,128)(2,1)S(1)}, bf16[2,128,2048]{2,1,0:T(8,128)(2,1)S(1)}, u32[]{:S(2)}, u32[]{:S(2)}) %collective-permute-start.4) | collective-permute-done | bytes 1048608 | tf_op jit(solution)/shard_map/ppermute | solution.py:118
  67.0 1.9 collective-permute-start.6
  68.9 5.6 %collective-permute-start.7 = (bf16[2,128,2048]{2,1,0:T(8,128)(2,1)S(1)}, bf16[2,128,2048]{2,1,0:T(8,128)(2,1)}, u32[]{:S(2)}, u32[]{:S(2)}) collective-permute-start(bf16[2,128,2048]{2,1,0:T(8,128)(2,1)S(1)} %collective-permute-done.5), channel_id=1, source_target_pairs={{0,480},{32,0},{64,32},{96,64},{128,96},{160,128},{192,160},{224,1... | collective-permute-start | bytes 3145736 | tf_op jit(solution)/shard_map/ppermute | solution.py:118
  74.6 2.6 collective-permute-start
  77.1 16.9 %collective-permute-done.6 = bf16[2,128,2048]{2,1,0:T(8,128)(2,1)} collective-permute-done((bf16[2,128,2048]{2,1,0:T(8,128)(2,1)S(1)}, bf16[2,128,2048]{2,1,0:T(8,128)(2,1)}, u32[]{:S(2)}, u32[]{:S(2)}) %collective-permute-start.6) | collective-permute-done | bytes 1048608 | tf_op jit(solution)/shard_map/ppermute | solution.py:118
  95.1 1.9 collective-permute-start.8
  97.0 5.7 %collective-permute-start.9 = (bf16[2,128,2048]{2,1,0:T(8,128)(2,1)}, bf16[2,128,2048]{2,1,0:T(8,128)(2,1)}, u32[]{:S(2)}, u32[]{:S(2)}) collective-permute-start(bf16[2,128,2048]{2,1,0:T(8,128)(2,1)} %collective-permute-done.7), channel_id=1, source_target_pairs={{0,480},{32,0},{64,32},{96,64},{128,96},{160,128},{192,160},{224,1... | collective-permute-start | bytes 3145736 | tf_op jit(solution)/shard_map/ppermute | solution.py:118
  103.7 1.9 collective-permute-start.1
  106.1 15.5 %collective-permute-done.8 = bf16[2,128,2048]{2,1,0:T(8,128)(2,1)} collective-permute-done((bf16[2,128,2048]{2,1,0:T(8,128)(2,1)}, bf16[2,128,2048]{2,1,0:T(8,128)(2,1)}, u32[]{:S(2)}, u32[]{:S(2)}) %collective-permute-start.8) | collective-permute-done | bytes 1048608 | tf_op jit(solution)/shard_map/ppermute | solution.py:118
  122.8 3.6 collective-permute-start.10
  126.3 3.9 collective-permute-start.11
  132.8 15.4 %collective-permute-done.10 = bf16[2,128,2048]{2,1,0:T(8,128)(2,1)} collective-permute-done((bf16[2,128,2048]{2,1,0:T(8,128)(2,1)}, bf16[2,128,2048]{2,1,0:T(8,128)(2,1)}, u32[]{:S(2)}, u32[]{:S(2)}) %collective-permute-start.10) | collective-permute-done | bytes 1048608 | tf_op jit(solution)/shard_map/ppermute | solution.py:118
  149.4 3.2 collective-permute-start.12
  152.6 4.3 collective-permute-start.13
  161.2 2.1 pad_maximum_fusion
  163.3 2.1 pad_maximum_fusion.1
  166.5 7.3 %collective-permute-done.12 = bf16[2,128,2048]{2,1,0:T(8,128)(2,1)S(1)} collective-permute-done((bf16[2,128,2048]{2,1,0:T(8,128)(2,1)}, bf16[2,128,2048]{2,1,0:T(8,128)(2,1)S(1)}, u32[]{:S(2)}, u32[]{:S(2)}) %collective-permute-start.12) | collective-permute-done | bytes 1048608 | tf_op jit(solution)/shard_map/ppermute | solution.py:118
  175.0 2.3 collective-permute-start.14
  177.3 5.3 %collective-permute-start.15 = (bf16[2,128,2048]{2,1,0:T(8,128)(2,1)}, bf16[2,128,2048]{2,1,0:T(8,128)(2,1)S(1)}, u32[]{:S(2)}, u32[]{:S(2)}) collective-permute-start(bf16[2,128,2048]{2,1,0:T(8,128)(2,1)} %collective-permute-done.13), channel_id=1, source_target_pairs={{0,480},{32,0},{64,32},{96,64},{128,96},{160,128},{192,160},{224,1... | collective-permute-start | bytes 3145736 | tf_op jit(solution)/shard_map/ppermute | solution.py:118
  183.6 2.3 bitcast_dynamic-update-slice_fusion.12
  185.9 2.3 bitcast_dynamic-update-slice_fusion.11
  188.2 10.1 %collective-permute-done.14 = bf16[2,128,2048]{2,1,0:T(8,128)(2,1)S(1)} collective-permute-done((bf16[2,128,2048]{2,1,0:T(8,128)(2,1)S(1)}, bf16[2,128,2048]{2,1,0:T(8,128)(2,1)S(1)}, u32[]{:S(2)}, u32[]{:S(2)}) %collective-permute-start.14) | collective-permute-done | bytes 1048608 | tf_op jit(solution)/shard_map/ppermute | solution.py:118
  201.7 2.3 bitcast_dynamic-update-slice_fusion.10
  204.0 2.3 bitcast_dynamic-update-slice_fusion.9
  207.4 14.6 %collective-permute-done.16 = bf16[2,128,2048]{2,1,0:T(8,128)(2,1)S(1)} collective-permute-done((bf16[2,128,2048]{2,1,0:T(8,128)(2,1)S(1)}, bf16[2,128,2048]{2,1,0:T(8,128)(2,1)S(1)}, u32[]{:S(2)}, u32[]{:S(2)}) %collective-permute-start.16) | collective-permute-done | bytes 1048608 | tf_op jit(solution)/shard_map/ppermute | solution.py:118
  225.1 2.4 bitcast_dynamic-update-slice_fusion.4
  227.5 2.4 bitcast_dynamic-update-slice_fusion.3
  229.9 2.4 bitcast_dynamic-update-slice_fusion.2
  234.4 57.7 %shard_map.76 = (bf16[4,64,2048]{2,1,0:T(8,128)(2,1)}, bf16[16,2,128,2048]{3,2,1,0:T(8,128)(2,1)}) custom-call(s32[16]{0:T(128)} %and_select_fusion.1.slot_ref, bf16[4,64,2048]{2,1,0:T(8,128)(2,1)} %bitcast.113, bf16[4,64,2048]{2,1,0:T(8,128)(2,1)} %bitcast.114, ...), custom_call_target="tpu_custom_call" | custom-call | flops 4831838208 | bytes 54525952 | tf_op jit(solution)/shard_map/pallas_call | solution.py:95
  293.8 1.9 collective-permute-start.17
  295.7 5.1 %collective-permute-start.18 = (bf16[2,128,2048]{2,1,0:T(8,128)(2,1)S(1)}, bf16[2,128,2048]{2,1,0:T(8,128)(2,1)S(1)}, u32[]{:S(2)}, u32[]{:S(2)}) collective-permute-start(bf16[2,128,2048]{2,1,0:T(8,128)(2,1)S(1)} %get-tuple-element.75), channel_id=1, source_target_pairs={{0,480},{32,0},{64,32},{96,64},{128,96},{160,128},{192,160},{224,1... | collective-permute-start | bytes 3145736 | tf_op jit(solution)/shard_map/ppermute | solution.py:118
  304.5 10.4 %collective-permute-done.17 = bf16[2,128,2048]{2,1,0:T(8,128)(2,1)} collective-permute-done((bf16[2,128,2048]{2,1,0:T(8,128)(2,1)S(1)}, bf16[2,128,2048]{2,1,0:T(8,128)(2,1)}, u32[]{:S(2)}, u32[]{:S(2)}) %collective-permute-start.17) | collective-permute-done | bytes 1048608 | tf_op jit(solution)/shard_map/ppermute | solution.py:118
  316.6 2.2 fusion.12
  318.8 1.9 collective-permute-start.19
  320.7 5.2 %collective-permute-start.20 = (bf16[2,128,2048]{2,1,0:T(8,128)(2,1)S(1)}, bf16[2,128,2048]{2,1,0:T(8,128)(2,1)S(1)}, u32[]{:S(2)}, u32[]{:S(2)}) collective-permute-start(bf16[2,128,2048]{2,1,0:T(8,128)(2,1)S(1)} %get-tuple-element.73), channel_id=1, source_target_pairs={{0,480},{32,0},{64,32},{96,64},{128,96},{160,128},{192,160},{224,1... | collective-permute-start | bytes 3145736 | tf_op jit(solution)/shard_map/ppermute | solution.py:118
  329.6 9.4 %collective-permute-done.19 = bf16[2,128,2048]{2,1,0:T(8,128)(2,1)} collective-permute-done((bf16[2,128,2048]{2,1,0:T(8,128)(2,1)S(1)}, bf16[2,128,2048]{2,1,0:T(8,128)(2,1)}, u32[]{:S(2)}, u32[]{:S(2)}) %collective-permute-start.19) | collective-permute-done | bytes 1048608 | tf_op jit(solution)/shard_map/ppermute | solution.py:118
  340.7 2.2 fusion.10
  343.0 1.9 collective-permute-start.21
  344.9 5.2 %collective-permute-start.22 = (bf16[2,128,2048]{2,1,0:T(8,128)(2,1)S(1)}, bf16[2,128,2048]{2,1,0:T(8,128)(2,1)S(1)}, u32[]{:S(2)}, u32[]{:S(2)}) collective-permute-start(bf16[2,128,2048]{2,1,0:T(8,128)(2,1)S(1)} %get-tuple-element.71), channel_id=1, source_target_pairs={{0,480},{32,0},{64,32},{96,64},{128,96},{160,128},{192,160},{224,1... | collective-permute-start | bytes 3145736 | tf_op jit(solution)/shard_map/ppermute | solution.py:118
  353.8 8.5 %collective-permute-done.21 = bf16[2,128,2048]{2,1,0:T(8,128)(2,1)} collective-permute-done((bf16[2,128,2048]{2,1,0:T(8,128)(2,1)S(1)}, bf16[2,128,2048]{2,1,0:T(8,128)(2,1)}, u32[]{:S(2)}, u32[]{:S(2)}) %collective-permute-start.21) | collective-permute-done | bytes 1048608 | tf_op jit(solution)/shard_map/ppermute | solution.py:118
  364.1 2.2 fusion.8
  366.3 1.9 collective-permute-start.23
  368.2 5.2 %collective-permute-start.24 = (bf16[2,128,2048]{2,1,0:T(8,128)(2,1)S(1)}, bf16[2,128,2048]{2,1,0:T(8,128)(2,1)S(1)}, u32[]{:S(2)}, u32[]{:S(2)}) collective-permute-start(bf16[2,128,2048]{2,1,0:T(8,128)(2,1)S(1)} %get-tuple-element.69), channel_id=1, source_target_pairs={{0,480},{32,0},{64,32},{96,64},{128,96},{160,128},{192,160},{224,1... | collective-permute-start | bytes 3145736 | tf_op jit(solution)/shard_map/ppermute | solution.py:118
  377.0 8.7 %collective-permute-done.23 = bf16[2,128,2048]{2,1,0:T(8,128)(2,1)} collective-permute-done((bf16[2,128,2048]{2,1,0:T(8,128)(2,1)S(1)}, bf16[2,128,2048]{2,1,0:T(8,128)(2,1)}, u32[]{:S(2)}, u32[]{:S(2)}) %collective-permute-start.23) | collective-permute-done | bytes 1048608 | tf_op jit(solution)/shard_map/ppermute | solution.py:118
  387.4 2.2 fusion.6
  389.6 1.9 collective-permute-start.25
  391.5 5.4 %collective-permute-start.26 = (bf16[2,128,2048]{2,1,0:T(8,128)(2,1)S(1)}, bf16[2,128,2048]{2,1,0:T(8,128)(2,1)S(1)}, u32[]{:S(2)}, u32[]{:S(2)}) collective-permute-start(bf16[2,128,2048]{2,1,0:T(8,128)(2,1)S(1)} %get-tuple-element.67), channel_id=1, source_target_pairs={{0,480},{32,0},{64,32},{96,64},{128,96},{160,128},{192,160},{224,1... | collective-permute-start | bytes 3145736 | tf_op jit(solution)/shard_map/ppermute | solution.py:118
  400.4 9.0 %collective-permute-done.25 = bf16[2,128,2048]{2,1,0:T(8,128)(2,1)} collective-permute-done((bf16[2,128,2048]{2,1,0:T(8,128)(2,1)S(1)}, bf16[2,128,2048]{2,1,0:T(8,128)(2,1)}, u32[]{:S(2)}, u32[]{:S(2)}) %collective-permute-start.25) | collective-permute-done | bytes 1048608 | tf_op jit(solution)/shard_map/ppermute | solution.py:118
  411.3 2.2 fusion.4
  413.5 4.4 collective-permute-start.27
  418.0 3.1 collective-permute-start.28
  424.8 10.1 %collective-permute-done.27 = bf16[2,128,2048]{2,1,0:T(8,128)(2,1)} collective-permute-done((bf16[2,128,2048]{2,1,0:T(8,128)(2,1)S(1)}, bf16[2,128,2048]{2,1,0:T(8,128)(2,1)}, u32[]{:S(2)}, u32[]{:S(2)}) %collective-permute-start.27) | collective-permute-done | bytes 1048608 | tf_op jit(solution)/shard_map/ppermute | solution.py:118
  436.3 2.3 collective-permute-done.28
  438.9 2.2 fusion.2
  441.1 4.2 collective-permute-start.29
  445.3 2.9 collective-permute-start.30
  449.9 14.7 %collective-permute-done.29 = bf16[2,128,2048]{2,1,0:T(8,128)(2,1)} collective-permute-done((bf16[2,128,2048]{2,1,0:T(8,128)(2,1)S(1)}, bf16[2,128,2048]{2,1,0:T(8,128)(2,1)}, u32[]{:S(2)}, u32[]{:S(2)}) %collective-permute-start.29) | collective-permute-done | bytes 1048608 | tf_op jit(solution)/shard_map/ppermute | solution.py:118
  467.8 3.3 collective-permute-start.31
  473.0 12.8 %collective-permute-done.31 = bf16[2,128,2048]{2,1,0:T(8,128)(2,1)} collective-permute-done((bf16[2,128,2048]{2,1,0:T(8,128)(2,1)S(1)}, bf16[2,128,2048]{2,1,0:T(8,128)(2,1)}, u32[]{:S(2)}, u32[]{:S(2)}) %collective-permute-start.31) | collective-permute-done | bytes 1048608 | tf_op jit(solution)/shard_map/ppermute | solution.py:118
  485.8 2.0 fusion
  (81 shorter events, 43.1 us)
Async XLA Ops:
  0.6 73.9 %copy-start.2 = (bf16[1,256,2048]{2,1,0:T(8,128)(2,1)S(1)}, bf16[1,256,2048]{2,1,0:T(8,128)(2,1)}, u32[]{:S(2)}) copy-start(bf16[1,256,2048]{2,1,0:T(8,128)(2,1)} %param.5) | copy-start | bytes 3145732
  0.6 105.0 %copy-start.12 = (s32[1,4,4]{2,1,0:T(4,128)S(1)}, s32[1,4,4]{2,1,0:T(4,128)}, u32[]{:S(2)}) copy-start(s32[1,4,4]{2,1,0:T(4,128)} %param.9) | copy-start | bytes 196
  2.0 128.9 %copy-start = (bf16[1,1,128,2048]{3,2,1,0:T(8,128)(2,1)S(1)}, bf16[1,1,128,2048]{3,2,1,0:T(8,128)(2,1)}, u32[]{:S(2)}) copy-start(bf16[1,1,128,2048]{3,2,1,0:T(8,128)(2,1)} %param.8) | copy-start | bytes 1572868
  2.0 128.9 %copy-start.1 = (bf16[1,1,128,2048]{3,2,1,0:T(8,128)(2,1)S(1)}, bf16[1,1,128,2048]{3,2,1,0:T(8,128)(2,1)}, u32[]{:S(2)}) copy-start(bf16[1,1,128,2048]{3,2,1,0:T(8,128)(2,1)} %param.7) | copy-start | bytes 1572868
  2.1 34.7 %collective-permute-start.2 = (bf16[2,128,2048]{2,1,0:T(8,128)(2,1)S(1)}, bf16[2,128,2048]{2,1,0:T(8,128)(2,1)S(1)}, u32[]{:S(2)}, u32[]{:S(2)}) collective-permute-start(bf16[2,128,2048]{2,1,0:T(8,128)(2,1)S(1)} %pad_maximum_fusion.2), channel_id=1, source_target_pairs={{0,32},{32,64},{64,96},{96,128},{128,160},{160,192},{192,224},{224... | collective-permute-start | bytes 3145736 | tf_op jit(solution)/shard_map/ppermute | solution.py:118
  6.0 31.9 %collective-permute-start.3 = (bf16[2,128,2048]{2,1,0:T(8,128)(2,1)S(1)}, bf16[2,128,2048]{2,1,0:T(8,128)(2,1)S(1)}, u32[]{:S(2)}, u32[]{:S(2)}) collective-permute-start(bf16[2,128,2048]{2,1,0:T(8,128)(2,1)S(1)} %pad_maximum_fusion.2), channel_id=1, source_target_pairs={{0,480},{32,0},{64,32},{96,64},{128,96},{160,128},{192,160},{224,1... | collective-permute-start | bytes 3145736 | tf_op jit(solution)/shard_map/ppermute | solution.py:118
  36.7 1.2 copy-start.4
  37.9 31.0 %copy-start.10 = (bf16[2,128,2048]{2,1,0:T(8,128)(2,1)}, bf16[2,128,2048]{2,1,0:T(8,128)(2,1)S(1)}, u32[]{:S(2)}) copy-start(bf16[2,128,2048]{2,1,0:T(8,128)(2,1)S(1)} %collective-permute-done.3) | copy-start | bytes 3145732
  37.9 27.9 %collective-permute-start.4 = (bf16[2,128,2048]{2,1,0:T(8,128)(2,1)S(1)}, bf16[2,128,2048]{2,1,0:T(8,128)(2,1)S(1)}, u32[]{:S(2)}, u32[]{:S(2)}) collective-permute-start(bf16[2,128,2048]{2,1,0:T(8,128)(2,1)S(1)} %collective-permute-done.2), channel_id=1, source_target_pairs={{0,32},{32,64},{64,96},{96,128},{128,160},{160,192},{192,224},{224... | collective-permute-start | bytes 3145736 | tf_op jit(solution)/shard_map/ppermute | solution.py:118
  39.8 27.1 %collective-permute-start.5 = (bf16[2,128,2048]{2,1,0:T(8,128)(2,1)S(1)}, bf16[2,128,2048]{2,1,0:T(8,128)(2,1)S(1)}, u32[]{:S(2)}, u32[]{:S(2)}) collective-permute-start(bf16[2,128,2048]{2,1,0:T(8,128)(2,1)S(1)} %collective-permute-done.3), channel_id=1, source_target_pairs={{0,480},{32,0},{64,32},{96,64},{128,96},{160,128},{192,160},{224,1... | collective-permute-start | bytes 3145736 | tf_op jit(solution)/shard_map/ppermute | solution.py:118
  65.8 1.2 copy-start.6
  67.0 27.1 %copy-start.8 = (bf16[2,128,2048]{2,1,0:T(8,128)(2,1)}, bf16[2,128,2048]{2,1,0:T(8,128)(2,1)S(1)}, u32[]{:S(2)}) copy-start(bf16[2,128,2048]{2,1,0:T(8,128)(2,1)S(1)} %collective-permute-done.5) | copy-start | bytes 3145732
  67.0 27.1 %collective-permute-start.6 = (bf16[2,128,2048]{2,1,0:T(8,128)(2,1)S(1)}, bf16[2,128,2048]{2,1,0:T(8,128)(2,1)}, u32[]{:S(2)}, u32[]{:S(2)}) collective-permute-start(bf16[2,128,2048]{2,1,0:T(8,128)(2,1)S(1)} %collective-permute-done.4), channel_id=1, source_target_pairs={{0,32},{32,64},{64,96},{96,128},{128,160},{160,192},{192,224},{224... | collective-permute-start | bytes 3145736 | tf_op jit(solution)/shard_map/ppermute | solution.py:118
  68.9 26.2 %collective-permute-start.7 = (bf16[2,128,2048]{2,1,0:T(8,128)(2,1)S(1)}, bf16[2,128,2048]{2,1,0:T(8,128)(2,1)}, u32[]{:S(2)}, u32[]{:S(2)}) collective-permute-start(bf16[2,128,2048]{2,1,0:T(8,128)(2,1)S(1)} %collective-permute-done.5), channel_id=1, source_target_pairs={{0,480},{32,0},{64,32},{96,64},{128,96},{160,128},{192,160},{224,1... | collective-permute-start | bytes 3145736 | tf_op jit(solution)/shard_map/ppermute | solution.py:118
  74.6 86.6 %collective-permute-start = (bf16[63,2048]{1,0:T(8,128)(2,1)S(1)}, bf16[63,2048]{1,0:T(8,128)(2,1)}, u32[]{:S(2)}, u32[]{:S(2)}) collective-permute-start(bf16[63,2048]{1,0:T(8,128)(2,1)S(1)} %slice_bitcast_fusion.5), channel_id=1, source_target_pairs={{1,0},{2,1},{3,2},{4,3},{5,4},{6,5},{7,6},{8,7},{9,8},{10,9},{11,1... | collective-permute-start | bytes 774152 | tf_op jit(solution)/shard_map/ppermute | solution.py:16
  95.1 26.4 %collective-permute-start.8 = (bf16[2,128,2048]{2,1,0:T(8,128)(2,1)}, bf16[2,128,2048]{2,1,0:T(8,128)(2,1)}, u32[]{:S(2)}, u32[]{:S(2)}) collective-permute-start(bf16[2,128,2048]{2,1,0:T(8,128)(2,1)} %collective-permute-done.6), channel_id=1, source_target_pairs={{0,32},{32,64},{64,96},{96,128},{128,160},{160,192},{192,224},{224... | collective-permute-start | bytes 3145736 | tf_op jit(solution)/shard_map/ppermute | solution.py:118
  97.0 25.7 %collective-permute-start.9 = (bf16[2,128,2048]{2,1,0:T(8,128)(2,1)}, bf16[2,128,2048]{2,1,0:T(8,128)(2,1)}, u32[]{:S(2)}, u32[]{:S(2)}) collective-permute-start(bf16[2,128,2048]{2,1,0:T(8,128)(2,1)} %collective-permute-done.7), channel_id=1, source_target_pairs={{0,480},{32,0},{64,32},{96,64},{128,96},{160,128},{192,160},{224,1... | collective-permute-start | bytes 3145736 | tf_op jit(solution)/shard_map/ppermute | solution.py:118
  103.7 59.6 %collective-permute-start.1 = (bf16[63,2048]{1,0:T(8,128)(2,1)S(1)}, bf16[63,2048]{1,0:T(8,128)(2,1)}, u32[]{:S(2)}, u32[]{:S(2)}) collective-permute-start(bf16[63,2048]{1,0:T(8,128)(2,1)S(1)} %slice_bitcast_fusion.4), channel_id=1, source_target_pairs={{1,0},{2,1},{3,2},{4,3},{5,4},{6,5},{7,6},{8,7},{9,8},{10,9},{11,1... | collective-permute-start | bytes 774152 | tf_op jit(solution)/shard_map/ppermute | solution.py:16
  106.1 26.0 %copy-start.3 = (bf16[1,256,2048]{2,1,0:T(8,128)(2,1)S(1)}, bf16[1,256,2048]{2,1,0:T(8,128)(2,1)}, u32[]{:S(2)}) copy-start(bf16[1,256,2048]{2,1,0:T(8,128)(2,1)} %param.6) | copy-start | bytes 3145732
  122.8 25.4 %collective-permute-start.10 = (bf16[2,128,2048]{2,1,0:T(8,128)(2,1)}, bf16[2,128,2048]{2,1,0:T(8,128)(2,1)}, u32[]{:S(2)}, u32[]{:S(2)}) collective-permute-start(bf16[2,128,2048]{2,1,0:T(8,128)(2,1)} %collective-permute-done.8), channel_id=1, source_target_pairs={{0,32},{32,64},{64,96},{96,128},{128,160},{160,192},{192,224},{224... | collective-permute-start | bytes 3145736 | tf_op jit(solution)/shard_map/ppermute | solution.py:118
  126.3 23.0 %collective-permute-start.11 = (bf16[2,128,2048]{2,1,0:T(8,128)(2,1)}, bf16[2,128,2048]{2,1,0:T(8,128)(2,1)}, u32[]{:S(2)}, u32[]{:S(2)}) collective-permute-start(bf16[2,128,2048]{2,1,0:T(8,128)(2,1)} %collective-permute-done.9), channel_id=1, source_target_pairs={{0,480},{32,0},{64,32},{96,64},{128,96},{160,128},{192,160},{224,1... | collective-permute-start | bytes 3145736 | tf_op jit(solution)/shard_map/ppermute | solution.py:118
  149.4 24.4 %collective-permute-start.12 = (bf16[2,128,2048]{2,1,0:T(8,128)(2,1)}, bf16[2,128,2048]{2,1,0:T(8,128)(2,1)S(1)}, u32[]{:S(2)}, u32[]{:S(2)}) collective-permute-start(bf16[2,128,2048]{2,1,0:T(8,128)(2,1)} %collective-permute-done.10), channel_id=1, source_target_pairs={{0,32},{32,64},{64,96},{96,128},{128,160},{160,192},{192,224},{224... | collective-permute-start | bytes 3145736 | tf_op jit(solution)/shard_map/ppermute | solution.py:118
  152.6 22.4 %collective-permute-start.13 = (bf16[2,128,2048]{2,1,0:T(8,128)(2,1)}, bf16[2,128,2048]{2,1,0:T(8,128)(2,1)}, u32[]{:S(2)}, u32[]{:S(2)}) collective-permute-start(bf16[2,128,2048]{2,1,0:T(8,128)(2,1)} %collective-permute-done.11), channel_id=1, source_target_pairs={{0,480},{32,0},{64,32},{96,64},{128,96},{160,128},{192,160},{224,1... | collective-permute-start | bytes 3145736 | tf_op jit(solution)/shard_map/ppermute | solution.py:118
  161.1 4.3 copy-start.11
  163.3 19.3 %copy-start.9 = (bf16[2,128,2048]{2,1,0:T(8,128)(2,1)S(1)}, bf16[2,128,2048]{2,1,0:T(8,128)(2,1)}, u32[]{:S(2)}) copy-start(bf16[2,128,2048]{2,1,0:T(8,128)(2,1)} %copy-done.8) | copy-start | bytes 3145732
  175.0 23.3 %collective-permute-start.14 = (bf16[2,128,2048]{2,1,0:T(8,128)(2,1)S(1)}, bf16[2,128,2048]{2,1,0:T(8,128)(2,1)S(1)}, u32[]{:S(2)}, u32[]{:S(2)}) collective-permute-start(bf16[2,128,2048]{2,1,0:T(8,128)(2,1)S(1)} %collective-permute-done.12), channel_id=1, source_target_pairs={{0,32},{32,64},{64,96},{96,128},{128,160},{160,192},{192,224},{224... | collective-permute-start | bytes 3145736 | tf_op jit(solution)/shard_map/ppermute | solution.py:118
  177.3 22.5 %collective-permute-start.15 = (bf16[2,128,2048]{2,1,0:T(8,128)(2,1)}, bf16[2,128,2048]{2,1,0:T(8,128)(2,1)S(1)}, u32[]{:S(2)}, u32[]{:S(2)}) collective-permute-start(bf16[2,128,2048]{2,1,0:T(8,128)(2,1)} %collective-permute-done.13), channel_id=1, source_target_pairs={{0,480},{32,0},{64,32},{96,64},{128,96},{160,128},{192,160},{224,1... | collective-permute-start | bytes 3145736 | tf_op jit(solution)/shard_map/ppermute | solution.py:118
  199.8 22.2 %collective-permute-start.16 = (bf16[2,128,2048]{2,1,0:T(8,128)(2,1)S(1)}, bf16[2,128,2048]{2,1,0:T(8,128)(2,1)S(1)}, u32[]{:S(2)}, u32[]{:S(2)}) collective-permute-start(bf16[2,128,2048]{2,1,0:T(8,128)(2,1)S(1)} %collective-permute-done.14), channel_id=1, source_target_pairs={{0,32},{32,64},{64,96},{96,128},{128,160},{160,192},{192,224},{224... | collective-permute-start | bytes 3145736 | tf_op jit(solution)/shard_map/ppermute | solution.py:118
  227.5 4.8 copy-start.7
  229.9 3.5 copy-start.5
  293.8 21.1 %collective-permute-start.17 = (bf16[2,128,2048]{2,1,0:T(8,128)(2,1)S(1)}, bf16[2,128,2048]{2,1,0:T(8,128)(2,1)}, u32[]{:S(2)}, u32[]{:S(2)}) collective-permute-start(bf16[2,128,2048]{2,1,0:T(8,128)(2,1)S(1)} %get-tuple-element.76), channel_id=1, source_target_pairs={{0,32},{32,64},{64,96},{96,128},{128,160},{160,192},{192,224},{224... | collective-permute-start | bytes 3145736 | tf_op jit(solution)/shard_map/ppermute | solution.py:118
  295.7 20.6 %collective-permute-start.18 = (bf16[2,128,2048]{2,1,0:T(8,128)(2,1)S(1)}, bf16[2,128,2048]{2,1,0:T(8,128)(2,1)S(1)}, u32[]{:S(2)}, u32[]{:S(2)}) collective-permute-start(bf16[2,128,2048]{2,1,0:T(8,128)(2,1)S(1)} %get-tuple-element.75), channel_id=1, source_target_pairs={{0,480},{32,0},{64,32},{96,64},{128,96},{160,128},{192,160},{224,1... | collective-permute-start | bytes 3145736 | tf_op jit(solution)/shard_map/ppermute | solution.py:118
  318.8 20.2 %collective-permute-start.19 = (bf16[2,128,2048]{2,1,0:T(8,128)(2,1)S(1)}, bf16[2,128,2048]{2,1,0:T(8,128)(2,1)}, u32[]{:S(2)}, u32[]{:S(2)}) collective-permute-start(bf16[2,128,2048]{2,1,0:T(8,128)(2,1)S(1)} %get-tuple-element.74), channel_id=1, source_target_pairs={{0,32},{32,64},{64,96},{96,128},{128,160},{160,192},{192,224},{224... | collective-permute-start | bytes 3145736 | tf_op jit(solution)/shard_map/ppermute | solution.py:118
  320.7 19.7 %collective-permute-start.20 = (bf16[2,128,2048]{2,1,0:T(8,128)(2,1)S(1)}, bf16[2,128,2048]{2,1,0:T(8,128)(2,1)S(1)}, u32[]{:S(2)}, u32[]{:S(2)}) collective-permute-start(bf16[2,128,2048]{2,1,0:T(8,128)(2,1)S(1)} %get-tuple-element.73), channel_id=1, source_target_pairs={{0,480},{32,0},{64,32},{96,64},{128,96},{160,128},{192,160},{224,1... | collective-permute-start | bytes 3145736 | tf_op jit(solution)/shard_map/ppermute | solution.py:118
  343.0 19.4 %collective-permute-start.21 = (bf16[2,128,2048]{2,1,0:T(8,128)(2,1)S(1)}, bf16[2,128,2048]{2,1,0:T(8,128)(2,1)}, u32[]{:S(2)}, u32[]{:S(2)}) collective-permute-start(bf16[2,128,2048]{2,1,0:T(8,128)(2,1)S(1)} %get-tuple-element.72), channel_id=1, source_target_pairs={{0,32},{32,64},{64,96},{96,128},{128,160},{160,192},{192,224},{224... | collective-permute-start | bytes 3145736 | tf_op jit(solution)/shard_map/ppermute | solution.py:118
  344.9 18.9 %collective-permute-start.22 = (bf16[2,128,2048]{2,1,0:T(8,128)(2,1)S(1)}, bf16[2,128,2048]{2,1,0:T(8,128)(2,1)S(1)}, u32[]{:S(2)}, u32[]{:S(2)}) collective-permute-start(bf16[2,128,2048]{2,1,0:T(8,128)(2,1)S(1)} %get-tuple-element.71), channel_id=1, source_target_pairs={{0,480},{32,0},{64,32},{96,64},{128,96},{160,128},{192,160},{224,1... | collective-permute-start | bytes 3145736 | tf_op jit(solution)/shard_map/ppermute | solution.py:118
  366.3 19.4 %collective-permute-start.23 = (bf16[2,128,2048]{2,1,0:T(8,128)(2,1)S(1)}, bf16[2,128,2048]{2,1,0:T(8,128)(2,1)}, u32[]{:S(2)}, u32[]{:S(2)}) collective-permute-start(bf16[2,128,2048]{2,1,0:T(8,128)(2,1)S(1)} %get-tuple-element.70), channel_id=1, source_target_pairs={{0,32},{32,64},{64,96},{96,128},{128,160},{160,192},{192,224},{224... | collective-permute-start | bytes 3145736 | tf_op jit(solution)/shard_map/ppermute | solution.py:118
  368.2 18.9 %collective-permute-start.24 = (bf16[2,128,2048]{2,1,0:T(8,128)(2,1)S(1)}, bf16[2,128,2048]{2,1,0:T(8,128)(2,1)S(1)}, u32[]{:S(2)}, u32[]{:S(2)}) collective-permute-start(bf16[2,128,2048]{2,1,0:T(8,128)(2,1)S(1)} %get-tuple-element.69), channel_id=1, source_target_pairs={{0,480},{32,0},{64,32},{96,64},{128,96},{160,128},{192,160},{224,1... | collective-permute-start | bytes 3145736 | tf_op jit(solution)/shard_map/ppermute | solution.py:118
  389.6 19.8 %collective-permute-start.25 = (bf16[2,128,2048]{2,1,0:T(8,128)(2,1)S(1)}, bf16[2,128,2048]{2,1,0:T(8,128)(2,1)}, u32[]{:S(2)}, u32[]{:S(2)}) collective-permute-start(bf16[2,128,2048]{2,1,0:T(8,128)(2,1)S(1)} %get-tuple-element.68), channel_id=1, source_target_pairs={{0,32},{32,64},{64,96},{96,128},{128,160},{160,192},{192,224},{224... | collective-permute-start | bytes 3145736 | tf_op jit(solution)/shard_map/ppermute | solution.py:118
  391.5 19.5 %collective-permute-start.26 = (bf16[2,128,2048]{2,1,0:T(8,128)(2,1)S(1)}, bf16[2,128,2048]{2,1,0:T(8,128)(2,1)S(1)}, u32[]{:S(2)}, u32[]{:S(2)}) collective-permute-start(bf16[2,128,2048]{2,1,0:T(8,128)(2,1)S(1)} %get-tuple-element.67), channel_id=1, source_target_pairs={{0,480},{32,0},{64,32},{96,64},{128,96},{160,128},{192,160},{224,1... | collective-permute-start | bytes 3145736 | tf_op jit(solution)/shard_map/ppermute | solution.py:118
  413.5 21.3 %collective-permute-start.27 = (bf16[2,128,2048]{2,1,0:T(8,128)(2,1)S(1)}, bf16[2,128,2048]{2,1,0:T(8,128)(2,1)}, u32[]{:S(2)}, u32[]{:S(2)}) collective-permute-start(bf16[2,128,2048]{2,1,0:T(8,128)(2,1)S(1)} %get-tuple-element.66), channel_id=1, source_target_pairs={{0,32},{32,64},{64,96},{96,128},{128,160},{160,192},{192,224},{224... | collective-permute-start | bytes 3145736 | tf_op jit(solution)/shard_map/ppermute | solution.py:118
  418.0 20.7 %collective-permute-start.28 = (bf16[2,128,2048]{2,1,0:T(8,128)(2,1)S(1)}, bf16[2,128,2048]{2,1,0:T(8,128)(2,1)S(1)}, u32[]{:S(2)}, u32[]{:S(2)}) collective-permute-start(bf16[2,128,2048]{2,1,0:T(8,128)(2,1)S(1)} %get-tuple-element.65), channel_id=1, source_target_pairs={{0,480},{32,0},{64,32},{96,64},{128,96},{160,128},{192,160},{224,1... | collective-permute-start | bytes 3145736 | tf_op jit(solution)/shard_map/ppermute | solution.py:118
  441.1 23.4 %collective-permute-start.29 = (bf16[2,128,2048]{2,1,0:T(8,128)(2,1)S(1)}, bf16[2,128,2048]{2,1,0:T(8,128)(2,1)}, u32[]{:S(2)}, u32[]{:S(2)}) collective-permute-start(bf16[2,128,2048]{2,1,0:T(8,128)(2,1)S(1)} %get-tuple-element.64), channel_id=1, source_target_pairs={{0,32},{32,64},{64,96},{96,128},{128,160},{160,192},{192,224},{224... | collective-permute-start | bytes 3145736 | tf_op jit(solution)/shard_map/ppermute | solution.py:118
  445.3 20.7 %collective-permute-start.30 = (bf16[2,128,2048]{2,1,0:T(8,128)(2,1)S(1)}, bf16[2,128,2048]{2,1,0:T(8,128)(2,1)S(1)}, u32[]{:S(2)}, u32[]{:S(2)}) collective-permute-start(bf16[2,128,2048]{2,1,0:T(8,128)(2,1)S(1)} %get-tuple-element.63), channel_id=1, source_target_pairs={{0,480},{32,0},{64,32},{96,64},{128,96},{160,128},{192,160},{224,1... | collective-permute-start | bytes 3145736 | tf_op jit(solution)/shard_map/ppermute | solution.py:118
  467.8 18.0 %collective-permute-start.31 = (bf16[2,128,2048]{2,1,0:T(8,128)(2,1)S(1)}, bf16[2,128,2048]{2,1,0:T(8,128)(2,1)}, u32[]{:S(2)}, u32[]{:S(2)}) collective-permute-start(bf16[2,128,2048]{2,1,0:T(8,128)(2,1)S(1)} %fusion.1), channel_id=1, source_target_pairs={{0,32},{32,64},{64,96},{96,128},{128,160},{160,192},{192,224},{224... | collective-permute-start | bytes 3145736 | tf_op jit(solution)/shard_map/ppermute | solution.py:118

commit v5 on v4

--- a/solution.py
+++ b/solution.py
@@ -112,6 +112,67 @@
     )(pair_slot, window_query, window_grad, *([blocks] * (2 * NBRS)))
 
 
+def gather_kernel(held_ref, out_ref, send_sem, recv_sem, local_sem):
+    groups = lax.axis_size("grp")
+    me = lax.axis_index("grp")
+    column = lax.axis_index("seq")
+    ahead = groups // 2
+    behind = groups - 1 - ahead
+    up = lax.rem(me + 1, groups)
+    down = lax.rem(me + groups - 1, groups)
+    barrier = pltpu.get_barrier_semaphore()
+    for neighbour in (up, down):
+        pl.semaphore_signal(
+            barrier, 1, device_id=(neighbour, column), device_id_type=pl.DeviceIdType.MESH
+        )
+    pl.semaphore_wait(barrier, 2)
+    local = pltpu.make_async_copy(held_ref, out_ref.at[0], local_sem)
+    local.start()
+    for step in range(1, ahead + 1):
+        copies = [
+            pltpu.make_async_remote_copy(
+                src_ref=held_ref if step == 1 else out_ref.at[groups + 1 - step],
+                dst_ref=out_ref.at[groups - step],
+                send_sem=send_sem.at[0, step - 1],
+                recv_sem=recv_sem.at[0, step - 1],
+                device_id=(up, column),
+                device_id_type=pl.DeviceIdType.MESH,
+            )
+        ]
+        if step <= behind:
+            copies.append(
+                pltpu.make_async_remote_copy(
+                    src_ref=held_ref if step == 1 else out_ref.at[step - 1],
+                    dst_ref=out_ref.at[step],
+                    send_sem=send_sem.at[1, step - 1],
+                    recv_sem=recv_sem.at[1, step - 1],
+                    device_id=(down, column),
+                    device_id_type=pl.DeviceIdType.MESH,
+                )
+            )
+        for copy in copies:
+            copy.start()
+        for copy in copies:
+            copy.wait()
+    local.wait()
+
+
+def ring_gather(held, groups):
+    ahead = groups // 2
+    return pl.pallas_call(
+        gather_kernel,
+        out_shape=jax.ShapeDtypeStruct((groups,) + held.shape, held.dtype),
+        in_specs=[pl.BlockSpec(memory_space=pl.ANY)],
+        out_specs=pl.BlockSpec(memory_space=pl.ANY),
+        scratch_shapes=[
+            pltpu.SemaphoreType.DMA((2, ahead)),
+            pltpu.SemaphoreType.DMA((2, ahead)),
+            pltpu.SemaphoreType.DMA(()),
+        ],
+        compiler_params=pltpu.CompilerParams(collective_id=0, has_side_effects=True),
+    )(held)
+
+
 def ring_step(array, axis, by):
     length = lax.axis_size(axis)
     pairs = [(i, (i + by) % length) for i in range(length)]
@@ -147,16 +208,7 @@
     rel_groups = (me + group_ids) % groups
     pair_slot = (owner_ids - me) % groups
     held = jnp.stack([neighbour_keys[0, 0], neighbour_values[0, 0]])
-    ahead_blocks, behind_blocks = [], []
-    going_up, going_down = held, held
-    for step in range(1, ahead + 1):
-        going_up = ring_step(going_up, "grp", 1)
-        if step <= behind:
-            going_down = ring_step(going_down, "grp", -1)
-            going_up, going_down = lax.optimization_barrier((going_up, going_down))
-            behind_blocks.append(going_down)
-        ahead_blocks.append(going_up)
-    all_blocks = jnp.stack([held] + behind_blocks + ahead_blocks[::-1], axis=0)
+    all_blocks = ring_gather(held, groups)
     grad_windows, pair_terms = span_attention(pair_slot, window_query, window_grad, all_blocks)
     grad_windows = grad_windows.reshape(1, span_count, span_len, row_width)
     slot_pair = jnp.sum(placement * jnp.arange(pair_count, dtype=jnp.int32)[None, :], axis=1)

time: 496 us -> 491 us (0.990)
  the two profiles are of different devices: /device:TPU:6 before, /device:TPU:32 now
where the time goes in v5:
time: 491 us; the launch traced here: 485 us
  Pallas kernels  261 us (53%)
  waiting for transfers between devices  104 us (21%)
  starting transfers between devices  47 us (10%)
  other arithmetic  33.6 us (7%)
  between operations  31.2 us (6%)
  local copies, waits for them, and re-layouts  7.85 us (2%)
    pallas_call x1, Pallas kernels, ring_gather(): pl.pallas_call(gather_kernel, out_shape=jax.ShapeDtypeStruct((groups,) +...  203 us
    ppermute x15, waiting for transfers between devices, ring_step(): return lax.ppermute(array, axis, pairs)  104 us
    pallas_call x1, Pallas kernels, span_attention(): pl.pallas_call(span_kernel, grid_spec=pltpu.PrefetchScalarGridSpec(num_sc...  57.7 us
    ppermute x15, starting transfers between devices, ring_step(): return lax.ppermute(array, axis, pairs)  44.4 us
    convert_element_type x6, other arithmetic, shards(): (down_arrived + terms(groups - behind + step)).astype(jnp.bfloat16)  13.3 us
    convert_element_type x7, other arithmetic, shards(): up_arrived = ring_step(up_sum, 'grp', 1).astype(jnp.float32)  10.2 us
  transfers between devices with their start and end apart: 17, of which 15 were waited for; matrix products, arithmetic and copies ran while one was open for 4% of the time, Pallas kernels for 42%

profile of v5, /device:TPU:32, one launch (start us, length us, event | category | flops | bytes accessed | tf_op | source)
XLA Modules:
  0.0 484.7 jit_solution(4432979529609007660)
XLA Ops:
  0.7 1.1 slice_bitcast_fusion.5
  1.8 1.3 collective-permute-start
  3.1 1.0 slice_bitcast_fusion.4
  4.1 1.3 collective-permute-start.1
  5.4 1.3 slice_bitcast_fusion.1
  6.7 0.2 slice_bitcast_fusion
  7.2 1.1 pad_maximum_fusion.2.held_ref
  8.3 0.7 gather_fusion
  8.9 0.5 and_select_fusion.1.slot_ref
  9.5 0.7 fusion.17
  12.8 202.9 %shard_map.76.refs_0_.refs_1_.refs_2_.refs_3_.refs_4_.refs_5_.refs_6_.refs_7_ = bf16[16,2,128,2048]{3,2,1,0:T(8,128)(2,1)} custom-call(bf16[2,128,2048]{2,1,0:T(8,128)(2,1)} %pad_maximum_fusion.2.held_ref), custom_call_target="tpu_custom_call" | custom-call | tf_op jit(solution)/shard_map/pallas_call | solution.py:162
  217.1 2.1 pad_maximum_fusion
  219.1 1.1 pad_maximum_fusion.1
  220.2 57.7 %shard_map.77 = (bf16[4,64,2048]{2,1,0:T(8,128)(2,1)}, bf16[16,2,128,2048]{3,2,1,0:T(8,128)(2,1)}) custom-call(s32[16]{0:T(128)} %and_select_fusion.1.slot_ref, bf16[4,64,2048]{2,1,0:T(8,128)(2,1)} %bitcast.81, bf16[4,64,2048]{2,1,0:T(8,128)(2,1)} %bitcast.82, ...), custom_call_target="tpu_custom_call" | custom-call | flops 4831838208 | bytes 54525952 | tf_op jit(solution)/shard_map/pallas_call | solution.py:95
  278.0 1.7 dynamic-slice_bitcast_fusion
  279.6 2.0 collective-permute-start.2
  281.6 3.9 collective-permute-start.3
  289.0 14.5 %collective-permute-done.2 = bf16[2,128,2048]{2,1,0:T(8,128)(2,1)} collective-permute-done((bf16[2,128,2048]{2,1,0:T(8,128)(2,1)S(1)}, bf16[2,128,2048]{2,1,0:T(8,128)(2,1)}, u32[]{:S(2)}, u32[]{:S(2)}) %collective-permute-start.2) | collective-permute-done | bytes 1048608 | tf_op jit(solution)/shard_map/ppermute | solution.py:179
  303.6 1.5 convert_element_type.191
  305.1 0.4 collective-permute-done.3
  305.4 0.2 convert_element_type.192
  305.7 2.2 fusion.12
  307.9 3.7 collective-permute-start.4
  311.6 2.1 collective-permute-start.5
  317.3 13.7 %collective-permute-done.4 = bf16[2,128,2048]{2,1,0:T(8,128)(2,1)} collective-permute-done((bf16[2,128,2048]{2,1,0:T(8,128)(2,1)S(1)}, bf16[2,128,2048]{2,1,0:T(8,128)(2,1)}, u32[]{:S(2)}, u32[]{:S(2)}) %collective-permute-start.4) | collective-permute-done | bytes 1048608 | tf_op jit(solution)/shard_map/ppermute | solution.py:179
  331.0 1.5 convert_element_type.196
  332.4 2.9 collective-permute-done.5
  335.6 2.2 fusion.10
  337.8 3.6 collective-permute-start.6
  341.5 2.2 collective-permute-start.7
  347.4 12.6 %collective-permute-done.6 = bf16[2,128,2048]{2,1,0:T(8,128)(2,1)} collective-permute-done((bf16[2,128,2048]{2,1,0:T(8,128)(2,1)S(1)}, bf16[2,128,2048]{2,1,0:T(8,128)(2,1)}, u32[]{:S(2)}, u32[]{:S(2)}) %collective-permute-start.6) | collective-permute-done | bytes 1048608 | tf_op jit(solution)/shard_map/ppermute | solution.py:179
  360.0 1.5 convert_element_type.204
  361.4 1.5 collective-permute-done.7
  363.2 2.2 fusion.8
  365.4 3.6 collective-permute-start.8
  369.0 2.3 collective-permute-start.9
  374.9 11.3 %collective-permute-done.8 = bf16[2,128,2048]{2,1,0:T(8,128)(2,1)} collective-permute-done((bf16[2,128,2048]{2,1,0:T(8,128)(2,1)S(1)}, bf16[2,128,2048]{2,1,0:T(8,128)(2,1)}, u32[]{:S(2)}, u32[]{:S(2)}) %collective-permute-start.8) | collective-permute-done | bytes 1048608 | tf_op jit(solution)/shard_map/ppermute | solution.py:179
  386.2 1.5 convert_element_type.212
  387.6 1.9 collective-permute-done.9
  389.8 2.2 fusion.6
  392.0 3.6 collective-permute-start.10
  395.6 2.3 collective-permute-start.11
  401.9 10.0 %collective-permute-done.10 = bf16[2,128,2048]{2,1,0:T(8,128)(2,1)} collective-permute-done((bf16[2,128,2048]{2,1,0:T(8,128)(2,1)S(1)}, bf16[2,128,2048]{2,1,0:T(8,128)(2,1)}, u32[]{:S(2)}, u32[]{:S(2)}) %collective-permute-start.10) | collective-permute-done | bytes 1048608 | tf_op jit(solution)/shard_map/ppermute | solution.py:179
  411.8 1.5 convert_element_type.220
  413.3 1.9 collective-permute-done.11
  415.2 0.2 convert_element_type.224
  415.5 2.2 fusion.4
  417.7 3.3 collective-permute-start.12
  421.1 2.5 collective-permute-start.13
  427.4 9.2 %collective-permute-done.12 = bf16[2,128,2048]{2,1,0:T(8,128)(2,1)} collective-permute-done((bf16[2,128,2048]{2,1,0:T(8,128)(2,1)S(1)}, bf16[2,128,2048]{2,1,0:T(8,128)(2,1)}, u32[]{:S(2)}, u32[]{:S(2)}) %collective-permute-start.12) | collective-permute-done | bytes 1048608 | tf_op jit(solution)/shard_map/ppermute | solution.py:179
  436.6 1.5 convert_element_type.228
  438.1 1.2 collective-permute-done.13
  439.5 2.2 fusion.2
  441.7 3.5 collective-permute-start.14
  445.2 2.3 collective-permute-start.15
  449.7 10.4 %collective-permute-done.14 = bf16[2,128,2048]{2,1,0:T(8,128)(2,1)} collective-permute-done((bf16[2,128,2048]{2,1,0:T(8,128)(2,1)S(1)}, bf16[2,128,2048]{2,1,0:T(8,128)(2,1)}, u32[]{:S(2)}, u32[]{:S(2)}) %collective-permute-start.14) | collective-permute-done | bytes 1048608 | tf_op jit(solution)/shard_map/ppermute | solution.py:179
  460.1 1.5 convert_element_type.236
  461.5 0.9 collective-permute-done.15
  462.5 0.2 convert_element_type.240
  462.7 1.6 fusion.1
  464.3 3.5 collective-permute-start.16
  469.7 12.0 %collective-permute-done.16 = bf16[2,128,2048]{2,1,0:T(8,128)(2,1)} collective-permute-done((bf16[2,128,2048]{2,1,0:T(8,128)(2,1)S(1)}, bf16[2,128,2048]{2,1,0:T(8,128)(2,1)}, u32[]{:S(2)}, u32[]{:S(2)}) %collective-permute-start.16) | collective-permute-done | bytes 1048608 | tf_op jit(solution)/shard_map/ppermute | solution.py:179
  481.7 2.0 fusion
  483.7 1.0 slice_bitcast_fusion.2
  (18 shorter events, 1.2 us)
Async XLA Ops:
  0.6 6.1 %copy-start = (bf16[1,256,2048]{2,1,0:T(8,128)(2,1)S(1)}, bf16[1,256,2048]{2,1,0:T(8,128)(2,1)}, u32[]{:S(2)}) copy-start(bf16[1,256,2048]{2,1,0:T(8,128)(2,1)} %param.6) | copy-start | bytes 3145732
  0.6 6.3 %copy-start.3 = (s32[1,4,4]{2,1,0:T(4,128)S(1)}, s32[1,4,4]{2,1,0:T(4,128)}, u32[]{:S(2)}) copy-start(s32[1,4,4]{2,1,0:T(4,128)} %param.9) | copy-start | bytes 196
  0.7 6.6 %copy-start.1 = (bf16[1,1,128,2048]{3,2,1,0:T(8,128)(2,1)S(1)}, bf16[1,1,128,2048]{3,2,1,0:T(8,128)(2,1)}, u32[]{:S(2)}) copy-start(bf16[1,1,128,2048]{3,2,1,0:T(8,128)(2,1)} %param.8) | copy-start | bytes 1572868
  0.7 6.6 %copy-start.2 = (bf16[1,1,128,2048]{3,2,1,0:T(8,128)(2,1)S(1)}, bf16[1,1,128,2048]{3,2,1,0:T(8,128)(2,1)}, u32[]{:S(2)}) copy-start(bf16[1,1,128,2048]{3,2,1,0:T(8,128)(2,1)} %param.7) | copy-start | bytes 1572868
  1.8 215.3 %collective-permute-start = (bf16[63,2048]{1,0:T(8,128)(2,1)S(1)}, bf16[63,2048]{1,0:T(8,128)(2,1)}, u32[]{:S(2)}, u32[]{:S(2)}) collective-permute-start(bf16[63,2048]{1,0:T(8,128)(2,1)S(1)} %slice_bitcast_fusion.5), channel_id=1, source_target_pairs={{1,0},{2,1},{3,2},{4,3},{5,4},{6,5},{7,6},{8,7},{9,8},{10,9},{11,1... | collective-permute-start | bytes 774152 | tf_op jit(solution)/shard_map/ppermute | solution.py:16
  4.1 215.1 %collective-permute-start.1 = (bf16[63,2048]{1,0:T(8,128)(2,1)S(1)}, bf16[63,2048]{1,0:T(8,128)(2,1)S(1)}, u32[]{:S(2)}, u32[]{:S(2)}) collective-permute-start(bf16[63,2048]{1,0:T(8,128)(2,1)S(1)} %slice_bitcast_fusion.4), channel_id=1, source_target_pairs={{1,0},{2,1},{3,2},{4,3},{5,4},{6,5},{7,6},{8,7},{9,8},{10,9},{11,1... | collective-permute-start | bytes 774152 | tf_op jit(solution)/shard_map/ppermute | solution.py:16
  279.6 23.9 %collective-permute-start.2 = (bf16[2,128,2048]{2,1,0:T(8,128)(2,1)S(1)}, bf16[2,128,2048]{2,1,0:T(8,128)(2,1)}, u32[]{:S(2)}, u32[]{:S(2)}) collective-permute-start(bf16[2,128,2048]{2,1,0:T(8,128)(2,1)S(1)} %get-tuple-element.48), channel_id=1, source_target_pairs={{0,32},{32,64},{64,96},{96,128},{128,160},{160,192},{192,224},{224... | collective-permute-start | bytes 3145736 | tf_op jit(solution)/shard_map/ppermute | solution.py:179
  281.6 23.8 %collective-permute-start.3 = (bf16[2,128,2048]{2,1,0:T(8,128)(2,1)S(1)}, bf16[2,128,2048]{2,1,0:T(8,128)(2,1)S(1)}, u32[]{:S(2)}, u32[]{:S(2)}) collective-permute-start(bf16[2,128,2048]{2,1,0:T(8,128)(2,1)S(1)} %get-tuple-element.47), channel_id=1, source_target_pairs={{0,480},{32,0},{64,32},{96,64},{128,96},{160,128},{192,160},{224,1... | collective-permute-start | bytes 3145736 | tf_op jit(solution)/shard_map/ppermute | solution.py:179
  307.9 23.1 %collective-permute-start.4 = (bf16[2,128,2048]{2,1,0:T(8,128)(2,1)S(1)}, bf16[2,128,2048]{2,1,0:T(8,128)(2,1)}, u32[]{:S(2)}, u32[]{:S(2)}) collective-permute-start(bf16[2,128,2048]{2,1,0:T(8,128)(2,1)S(1)} %get-tuple-element.46), channel_id=1, source_target_pairs={{0,32},{32,64},{64,96},{96,128},{128,160},{160,192},{192,224},{224... | collective-permute-start | bytes 3145736 | tf_op jit(solution)/shard_map/ppermute | solution.py:179
  311.6 23.8 %collective-permute-start.5 = (bf16[2,128,2048]{2,1,0:T(8,128)(2,1)S(1)}, bf16[2,128,2048]{2,1,0:T(8,128)(2,1)S(1)}, u32[]{:S(2)}, u32[]{:S(2)}) collective-permute-start(bf16[2,128,2048]{2,1,0:T(8,128)(2,1)S(1)} %get-tuple-element.45), channel_id=1, source_target_pairs={{0,480},{32,0},{64,32},{96,64},{128,96},{160,128},{192,160},{224,1... | collective-permute-start | bytes 3145736 | tf_op jit(solution)/shard_map/ppermute | solution.py:179
  337.8 22.1 %collective-permute-start.6 = (bf16[2,128,2048]{2,1,0:T(8,128)(2,1)S(1)}, bf16[2,128,2048]{2,1,0:T(8,128)(2,1)}, u32[]{:S(2)}, u32[]{:S(2)}) collective-permute-start(bf16[2,128,2048]{2,1,0:T(8,128)(2,1)S(1)} %get-tuple-element.44), channel_id=1, source_target_pairs={{0,32},{32,64},{64,96},{96,128},{128,160},{160,192},{192,224},{224... | collective-permute-start | bytes 3145736 | tf_op jit(solution)/shard_map/ppermute | solution.py:179
  341.5 21.5 %collective-permute-start.7 = (bf16[2,128,2048]{2,1,0:T(8,128)(2,1)S(1)}, bf16[2,128,2048]{2,1,0:T(8,128)(2,1)S(1)}, u32[]{:S(2)}, u32[]{:S(2)}) collective-permute-start(bf16[2,128,2048]{2,1,0:T(8,128)(2,1)S(1)} %get-tuple-element.43), channel_id=1, source_target_pairs={{0,480},{32,0},{64,32},{96,64},{128,96},{160,128},{192,160},{224,1... | collective-permute-start | bytes 3145736 | tf_op jit(solution)/shard_map/ppermute | solution.py:179
  365.4 20.8 %collective-permute-start.8 = (bf16[2,128,2048]{2,1,0:T(8,128)(2,1)S(1)}, bf16[2,128,2048]{2,1,0:T(8,128)(2,1)}, u32[]{:S(2)}, u32[]{:S(2)}) collective-permute-start(bf16[2,128,2048]{2,1,0:T(8,128)(2,1)S(1)} %get-tuple-element.42), channel_id=1, source_target_pairs={{0,32},{32,64},{64,96},{96,128},{128,160},{160,192},{192,224},{224... | collective-permute-start | bytes 3145736 | tf_op jit(solution)/shard_map/ppermute | solution.py:179
  369.0 20.5 %collective-permute-start.9 = (bf16[2,128,2048]{2,1,0:T(8,128)(2,1)S(1)}, bf16[2,128,2048]{2,1,0:T(8,128)(2,1)S(1)}, u32[]{:S(2)}, u32[]{:S(2)}) collective-permute-start(bf16[2,128,2048]{2,1,0:T(8,128)(2,1)S(1)} %get-tuple-element.41), channel_id=1, source_target_pairs={{0,480},{32,0},{64,32},{96,64},{128,96},{160,128},{192,160},{224,1... | collective-permute-start | bytes 3145736 | tf_op jit(solution)/shard_map/ppermute | solution.py:179
  392.0 19.8 %collective-permute-start.10 = (bf16[2,128,2048]{2,1,0:T(8,128)(2,1)S(1)}, bf16[2,128,2048]{2,1,0:T(8,128)(2,1)}, u32[]{:S(2)}, u32[]{:S(2)}) collective-permute-start(bf16[2,128,2048]{2,1,0:T(8,128)(2,1)S(1)} %get-tuple-element.40), channel_id=1, source_target_pairs={{0,32},{32,64},{64,96},{96,128},{128,160},{160,192},{192,224},{224... | collective-permute-start | bytes 3145736 | tf_op jit(solution)/shard_map/ppermute | solution.py:179
  395.6 19.6 %collective-permute-start.11 = (bf16[2,128,2048]{2,1,0:T(8,128)(2,1)S(1)}, bf16[2,128,2048]{2,1,0:T(8,128)(2,1)S(1)}, u32[]{:S(2)}, u32[]{:S(2)}) collective-permute-start(bf16[2,128,2048]{2,1,0:T(8,128)(2,1)S(1)} %get-tuple-element.39), channel_id=1, source_target_pairs={{0,480},{32,0},{64,32},{96,64},{128,96},{160,128},{192,160},{224,1... | collective-permute-start | bytes 3145736 | tf_op jit(solution)/shard_map/ppermute | solution.py:179
  417.7 18.9 %collective-permute-start.12 = (bf16[2,128,2048]{2,1,0:T(8,128)(2,1)S(1)}, bf16[2,128,2048]{2,1,0:T(8,128)(2,1)}, u32[]{:S(2)}, u32[]{:S(2)}) collective-permute-start(bf16[2,128,2048]{2,1,0:T(8,128)(2,1)S(1)} %get-tuple-element.38), channel_id=1, source_target_pairs={{0,32},{32,64},{64,96},{96,128},{128,160},{160,192},{192,224},{224... | collective-permute-start | bytes 3145736 | tf_op jit(solution)/shard_map/ppermute | solution.py:179
  421.1 18.2 %collective-permute-start.13 = (bf16[2,128,2048]{2,1,0:T(8,128)(2,1)S(1)}, bf16[2,128,2048]{2,1,0:T(8,128)(2,1)S(1)}, u32[]{:S(2)}, u32[]{:S(2)}) collective-permute-start(bf16[2,128,2048]{2,1,0:T(8,128)(2,1)S(1)} %get-tuple-element.37), channel_id=1, source_target_pairs={{0,480},{32,0},{64,32},{96,64},{128,96},{160,128},{192,160},{224,1... | collective-permute-start | bytes 3145736 | tf_op jit(solution)/shard_map/ppermute | solution.py:179
  441.7 18.3 %collective-permute-start.14 = (bf16[2,128,2048]{2,1,0:T(8,128)(2,1)S(1)}, bf16[2,128,2048]{2,1,0:T(8,128)(2,1)}, u32[]{:S(2)}, u32[]{:S(2)}) collective-permute-start(bf16[2,128,2048]{2,1,0:T(8,128)(2,1)S(1)} %get-tuple-element.36), channel_id=1, source_target_pairs={{0,32},{32,64},{64,96},{96,128},{128,160},{160,192},{192,224},{224... | collective-permute-start | bytes 3145736 | tf_op jit(solution)/shard_map/ppermute | solution.py:179
  445.2 17.2 %collective-permute-start.15 = (bf16[2,128,2048]{2,1,0:T(8,128)(2,1)S(1)}, bf16[2,128,2048]{2,1,0:T(8,128)(2,1)S(1)}, u32[]{:S(2)}, u32[]{:S(2)}) collective-permute-start(bf16[2,128,2048]{2,1,0:T(8,128)(2,1)S(1)} %get-tuple-element.35), channel_id=1, source_target_pairs={{0,480},{32,0},{64,32},{96,64},{128,96},{160,128},{192,160},{224,1... | collective-permute-start | bytes 3145736 | tf_op jit(solution)/shard_map/ppermute | solution.py:179
  464.3 17.4 %collective-permute-start.16 = (bf16[2,128,2048]{2,1,0:T(8,128)(2,1)S(1)}, bf16[2,128,2048]{2,1,0:T(8,128)(2,1)}, u32[]{:S(2)}, u32[]{:S(2)}) collective-permute-start(bf16[2,128,2048]{2,1,0:T(8,128)(2,1)S(1)} %fusion.1), channel_id=1, source_target_pairs={{0,32},{32,64},{64,96},{96,128},{128,160},{160,192},{192,224},{224... | collective-permute-start | bytes 3145736 | tf_op jit(solution)/shard_map/ppermute | solution.py:179

commit v6 on v5

--- a/solution.py
+++ b/solution.py
@@ -16,57 +16,61 @@
     return lax.ppermute(array, axis, pairs)
 
 
-def span_kernel(slot_ref, query_ref, grad_ref, *refs):
-    key_refs = refs[:NBRS]
-    value_refs = refs[NBRS : 2 * NBRS]
-    window_ref, term_ref = refs[2 * NBRS :]
+def span_kernel(slot_ref, query_ref, grad_ref, block_ref, window_ref, term_ref):
     scale = HEAD ** (-0.5)
-    query = query_ref[0]
-    grad = grad_ref[0]
-    keys = jnp.concatenate([ref[0, 0] for ref in key_refs], axis=0)
-    values = jnp.concatenate([ref[0, 0] for ref in value_refs], axis=0)
     contract_last = (((1,), (1,)), ((), ()))
-    scores = lax.dot_general(query, keys, contract_last, preferred_element_type=jnp.float32) * scale
-    grad_probs = lax.dot_general(grad, values, contract_last, preferred_element_type=jnp.float32)
-    maxes, totals, dots = [], [], []
-    for j in range(NBRS):
-        part = scores[:, j * HEAD : (j + 1) * HEAD]
-        row_max = jnp.max(part, axis=-1, keepdims=True)
-        exp_part = jnp.exp(part - row_max)
-        row_total = jnp.sum(exp_part, axis=-1, keepdims=True)
-        rounded = exp_part.astype(jnp.bfloat16).astype(jnp.float32)
-        dotted = jnp.sum(rounded * grad_probs[:, j * HEAD : (j + 1) * HEAD], axis=-1, keepdims=True)
-        maxes.append(row_max)
-        totals.append(row_total)
-        dots.append(dotted / row_total)
-    top = maxes[0]
-    for j in range(1, NBRS):
-        top = jnp.maximum(top, maxes[j])
-    weights = [totals[j] * jnp.exp(maxes[j] - top) for j in range(NBRS)]
-    weight_sum = weights[0] + weights[1] + weights[2] + weights[3]
-    weighted = weights[0] * dots[0] + weights[1] * dots[1] + weights[2] * dots[2] + weights[3] * dots[3]
-    log_total = top + jnp.log(weight_sum)
-    delta = weighted / weight_sum
-    probs = jnp.exp(scores - log_total)
-    grad_scores = (probs * (grad_probs - delta)).astype(jnp.bfloat16)
-    window = jnp.zeros(query.shape, jnp.float32)
-    for j in range(NBRS):
-        part = lax.dot_general(
-            grad_scores[:, j * HEAD : (j + 1) * HEAD],
-            keys[j * HEAD : (j + 1) * HEAD],
-            (((1,), (0,)), ((), ())),
-            preferred_element_type=jnp.float32,
-        )
-        window = window + (part * scale).astype(jnp.bfloat16).astype(jnp.float32)
-    window_ref[0] = window.astype(window_ref.dtype)
-    probs_t = probs.astype(jnp.bfloat16).astype(jnp.float32).T.astype(jnp.bfloat16)
-    scores_t = grad_scores.astype(jnp.float32).T.astype(jnp.bfloat16)
     plain = (((1,), (0,)), ((), ()))
-    value_term = lax.dot_general(probs_t, grad, plain, preferred_element_type=jnp.float32)
-    key_term = lax.dot_general(scores_t, query, plain, preferred_element_type=jnp.float32) * scale
-    for j in range(NBRS):
-        term_ref[j, 0] = key_term[j * HEAD : (j + 1) * HEAD].astype(term_ref.dtype)
-        term_ref[j, 1] = value_term[j * HEAD : (j + 1) * HEAD].astype(term_ref.dtype)
+    for span in range(query_ref.shape[0]):
+        query = query_ref[span]
+        grad = grad_ref[span]
+        slots = [slot_ref[span * NBRS + j] for j in range(NBRS)]
+        keys = jnp.concatenate([block_ref[slot, 0] for slot in slots], axis=0)
+        values = jnp.concatenate([block_ref[slot, 1] for slot in slots], axis=0)
+        scores = lax.dot_general(query, keys, contract_last, preferred_element_type=jnp.float32) * scale
+        grad_probs = lax.dot_general(grad, values, contract_last, preferred_element_type=jnp.float32)
+        maxes, totals, dots = [], [], []
+        for j in range(NBRS):
+            part = scores[:, j * HEAD : (j + 1) * HEAD]
+            row_max = jnp.max(part, axis=-1, keepdims=True)
+            exp_part = jnp.exp(part - row_max)
+            row_total = jnp.sum(exp_part, axis=-1, keepdims=True)
+            rounded = exp_part.astype(jnp.bfloat16).astype(jnp.float32)
+            dotted = jnp.sum(
+                rounded * grad_probs[:, j * HEAD : (j + 1) * HEAD], axis=-1, keepdims=True
+            )
+            maxes.append(row_max)
+            totals.append(row_total)
+            dots.append(dotted / row_total)
+        top = maxes[0]
+        for j in range(1, NBRS):
+            top = jnp.maximum(top, maxes[j])
+        weights = [totals[j] * jnp.exp(maxes[j] - top) for j in range(NBRS)]
+        weight_sum = weights[0]
+        weighted = weights[0] * dots[0]
+        for j in range(1, NBRS):
+            weight_sum = weight_sum + weights[j]
+            weighted = weighted + weights[j] * dots[j]
+        log_total = top + jnp.log(weight_sum)
+        delta = weighted / weight_sum
+        probs = jnp.exp(scores - log_total)
+        grad_scores = (probs * (grad_probs - delta)).astype(jnp.bfloat16)
+        window = jnp.zeros(query.shape, jnp.float32)
+        for j in range(NBRS):
+            part = lax.dot_general(
+                grad_scores[:, j * HEAD : (j + 1) * HEAD],
+                keys[j * HEAD : (j + 1) * HEAD],
+                plain,
+                preferred_element_type=jnp.float32,
+            )
+            window = window + (part * scale).astype(jnp.bfloat16).astype(jnp.float32)
+        window_ref[span] = window.astype(window_ref.dtype)
+        probs_t = probs.astype(jnp.bfloat16).astype(jnp.float32).T.astype(jnp.bfloat16)
+        scores_t = grad_scores.astype(jnp.float32).T.astype(jnp.bfloat16)
+        value_term = lax.dot_general(probs_t, grad, plain, preferred_element_type=jnp.float32)
+        key_term = lax.dot_general(scores_t, query, plain, preferred_element_type=jnp.float32) * scale
+        for j in range(NBRS):
+            term_ref[span * NBRS + j, 0] = key_term[j * HEAD : (j + 1) * HEAD].astype(term_ref.dtype)
+            term_ref[span * NBRS + j, 1] = value_term[j * HEAD : (j + 1) * HEAD].astype(term_ref.dtype)
 
 
 def span_attention(pair_slot, window_query, window_grad, blocks):
@@ -75,30 +79,27 @@
     head_count = row_width // HEAD
     pair_count = span_count * NBRS
 
-    def window_map(h, i, slots):
-        return (i, 0, h)
-
-    def block_map(j, kind):
-        return lambda h, i, slots: (slots[i * NBRS + j], kind, 0, h)
-
-    in_specs = [
-        pl.BlockSpec((1, span_len, HEAD), window_map),
-        pl.BlockSpec((1, span_len, HEAD), window_map),
-    ]
-    in_specs += [pl.BlockSpec((1, 1, block_len, HEAD), block_map(j, 0)) for j in range(NBRS)]
-    in_specs += [pl.BlockSpec((1, 1, block_len, HEAD), block_map(j, 1)) for j in range(NBRS)]
-    out_specs = [
-        pl.BlockSpec((1, span_len, HEAD), window_map),
-        pl.BlockSpec((NBRS, 2, block_len, HEAD), lambda h, i, slots: (i, 0, 0, h)),
-    ]
+    def window_map(h, slots):
+        return (0, 0, h)
+
+    def block_map(h, slots):
+        return (0, 0, 0, h)
+
     flops = 2 * span_len * block_len * HEAD * 9 * pair_count * head_count
     return pl.pallas_call(
         span_kernel,
         grid_spec=pltpu.PrefetchScalarGridSpec(
             num_scalar_prefetch=1,
-            grid=(head_count, span_count),
-            in_specs=in_specs,
-            out_specs=out_specs,
+            grid=(head_count,),
+            in_specs=[
+                pl.BlockSpec((span_count, span_len, HEAD), window_map),
+                pl.BlockSpec((span_count, span_len, HEAD), window_map),
+                pl.BlockSpec((slot_count, 2, block_len, HEAD), block_map),
+            ],
+            out_specs=[
+                pl.BlockSpec((span_count, span_len, HEAD), window_map),
+                pl.BlockSpec((pair_count, 2, block_len, HEAD), block_map),
+            ],
         ),
         out_shape=[
             jax.ShapeDtypeStruct((span_count, span_len, row_width), jnp.bfloat16),
@@ -107,9 +108,9 @@
         cost_estimate=pl.CostEstimate(
             flops=flops,
             transcendentals=2 * pair_count * span_len * block_len * head_count,
-            bytes_accessed=2 * (3 * blocks.size + 4 * window_query.size),
+            bytes_accessed=2 * (2 * blocks.size + 3 * window_query.size),
         ),
-    )(pair_slot, window_query, window_grad, *([blocks] * (2 * NBRS)))
+    )(pair_slot, window_query, window_grad, blocks)
 
 
 def gather_kernel(held_ref, out_ref, send_sem, recv_sem, local_sem):

time: 491 us -> 469 us (0.955)
  the two profiles are of different devices: /device:TPU:32 before, /device:TPU:6 now
where the time goes in v6:
time: 469 us; the launch traced here: 460 us
  Pallas kernels  236 us (50%)
  waiting for transfers between devices  91.2 us (19%)
  starting transfers between devices  60.3 us (13%)
  other arithmetic  33.6 us (7%)
  between operations  31.3 us (7%)
  local copies, waits for them, and re-layouts  7.85 us (2%)
    pallas_call x1, Pallas kernels, ring_gather(): pl.pallas_call(gather_kernel, out_shape=jax.ShapeDtypeStruct((groups,) +...  196 us
    ppermute x15, waiting for transfers between devices, ring_step(): return lax.ppermute(array, axis, pairs)  91.2 us
    ppermute x15, starting transfers between devices, ring_step(): return lax.ppermute(array, axis, pairs)  53.1 us
    pallas_call x1, Pallas kernels, span_attention(): pl.pallas_call(span_kernel, grid_spec=pltpu.PrefetchScalarGridSpec(num_sc...  40 us
    convert_element_type x6, other arithmetic, shards(): (down_arrived + terms(groups - behind + step)).astype(jnp.bfloat16)  13.3 us
    convert_element_type x7, other arithmetic, shards(): up_arrived = ring_step(up_sum, 'grp', 1).astype(jnp.float32)  10.2 us
  transfers between devices with their start and end apart: 17, of which 12 were waited for; matrix products, arithmetic and copies ran while one was open for 4% of the time, Pallas kernels for 43%

profile of v6, /device:TPU:6, one launch (start us, length us, event | category | flops | bytes accessed | tf_op | source)
XLA Modules:
  0.0 460.1 jit_solution(1305620822281294403)
XLA Ops:
  0.7 1.1 slice_bitcast_fusion.5
  1.8 4.6 %collective-permute-start = (bf16[63,2048]{1,0:T(8,128)(2,1)S(1)}, bf16[63,2048]{1,0:T(8,128)(2,1)}, u32[]{:S(2)}, u32[]{:S(2)}) collective-permute-start(bf16[63,2048]{1,0:T(8,128)(2,1)S(1)} %slice_bitcast_fusion.5), channel_id=1, source_target_pairs={{1,0},{2,1},{3,2},{4,3},{5,4},{6,5},{7,6},{8,7},{9,8},{10,9},{11,1... | collective-permute-start | bytes 774152 | tf_op jit(solution)/shard_map/ppermute | solution.py:16
  6.4 1.0 slice_bitcast_fusion.4
  7.4 2.6 collective-permute-start.1
  10.0 1.3 slice_bitcast_fusion.1
  11.4 0.2 slice_bitcast_fusion
  11.9 1.1 pad_maximum_fusion.2.held_ref
  12.9 0.7 gather_fusion
  13.6 0.5 and_select_fusion.1.slot_ref
  14.1 0.7 fusion.17
  17.5 195.9 %shard_map.76.block_ref = bf16[16,2,128,2048]{3,2,1,0:T(8,128)(2,1)} custom-call(bf16[2,128,2048]{2,1,0:T(8,128)(2,1)} %pad_maximum_fusion.2.held_ref), custom_call_target="tpu_custom_call" | custom-call | tf_op jit(solution)/shard_map/pallas_call | solution.py:163
  214.7 2.1 pad_maximum_fusion
  216.8 1.1 pad_maximum_fusion.1
  217.9 40.0 %shard_map.77 = (bf16[4,64,2048]{2,1,0:T(8,128)(2,1)}, bf16[16,2,128,2048]{3,2,1,0:T(8,128)(2,1)}) custom-call(s32[16]{0:T(128)} %and_select_fusion.1.slot_ref, bf16[4,64,2048]{2,1,0:T(8,128)(2,1)} %bitcast.81, bf16[4,64,2048]{2,1,0:T(8,128)(2,1)} %bitcast.82, bf16[16,2,128,2048]{3,2,1,0:T(8,128)(2,1)} %shard_map.76.block_ref), custom_call_target="tpu_custom_call" | custom-call | flops 4831838208 | bytes 36700160 | tf_op jit(solution)/shard_map/pallas_call | solution.py:89
  257.9 1.7 dynamic-slice_bitcast_fusion
  259.6 2.1 collective-permute-start.2
  261.8 4.9 %collective-permute-start.3 = (bf16[2,128,2048]{2,1,0:T(8,128)(2,1)S(1)}, bf16[2,128,2048]{2,1,0:T(8,128)(2,1)S(1)}, u32[]{:S(2)}, u32[]{:S(2)}) collective-permute-start(bf16[2,128,2048]{2,1,0:T(8,128)(2,1)S(1)} %get-tuple-element.47), channel_id=1, source_target_pairs={{0,480},{32,0},{64,32},{96,64},{128,96},{160,128},{192,160},{224,1... | collective-permute-start | bytes 3145736 | tf_op jit(solution)/shard_map/ppermute | solution.py:180
  270.2 13.4 %collective-permute-done.2 = bf16[2,128,2048]{2,1,0:T(8,128)(2,1)} collective-permute-done((bf16[2,128,2048]{2,1,0:T(8,128)(2,1)S(1)}, bf16[2,128,2048]{2,1,0:T(8,128)(2,1)}, u32[]{:S(2)}, u32[]{:S(2)}) %collective-permute-start.2) | collective-permute-done | bytes 1048608 | tf_op jit(solution)/shard_map/ppermute | solution.py:180
  283.6 1.5 convert_element_type.191
  285.1 0.2 convert_element_type.192
  285.3 2.2 fusion.12
  287.6 1.9 collective-permute-start.4
  289.5 5.2 %collective-permute-start.5 = (bf16[2,128,2048]{2,1,0:T(8,128)(2,1)S(1)}, bf16[2,128,2048]{2,1,0:T(8,128)(2,1)S(1)}, u32[]{:S(2)}, u32[]{:S(2)}) collective-permute-start(bf16[2,128,2048]{2,1,0:T(8,128)(2,1)S(1)} %get-tuple-element.45), channel_id=1, source_target_pairs={{0,480},{32,0},{64,32},{96,64},{128,96},{160,128},{192,160},{224,1... | collective-permute-start | bytes 3145736 | tf_op jit(solution)/shard_map/ppermute | solution.py:180
  298.2 12.5 %collective-permute-done.4 = bf16[2,128,2048]{2,1,0:T(8,128)(2,1)} collective-permute-done((bf16[2,128,2048]{2,1,0:T(8,128)(2,1)S(1)}, bf16[2,128,2048]{2,1,0:T(8,128)(2,1)}, u32[]{:S(2)}, u32[]{:S(2)}) %collective-permute-start.4) | collective-permute-done | bytes 1048608 | tf_op jit(solution)/shard_map/ppermute | solution.py:180
  310.7 1.5 convert_element_type.196
  312.2 0.2 convert_element_type.200
  312.4 2.2 fusion.10
  314.7 3.3 collective-permute-start.6
  318.0 3.8 collective-permute-start.7
  325.5 11.4 %collective-permute-done.6 = bf16[2,128,2048]{2,1,0:T(8,128)(2,1)} collective-permute-done((bf16[2,128,2048]{2,1,0:T(8,128)(2,1)S(1)}, bf16[2,128,2048]{2,1,0:T(8,128)(2,1)}, u32[]{:S(2)}, u32[]{:S(2)}) %collective-permute-start.6) | collective-permute-done | bytes 1048608 | tf_op jit(solution)/shard_map/ppermute | solution.py:180
  336.9 1.5 convert_element_type.204
  338.3 0.7 collective-permute-done.7
  339.0 0.2 convert_element_type.208
  339.2 2.2 fusion.8
  341.5 3.4 collective-permute-start.8
  344.8 3.7 collective-permute-start.9
  352.1 10.9 %collective-permute-done.8 = bf16[2,128,2048]{2,1,0:T(8,128)(2,1)} collective-permute-done((bf16[2,128,2048]{2,1,0:T(8,128)(2,1)S(1)}, bf16[2,128,2048]{2,1,0:T(8,128)(2,1)}, u32[]{:S(2)}, u32[]{:S(2)}) %collective-permute-start.8) | collective-permute-done | bytes 1048608 | tf_op jit(solution)/shard_map/ppermute | solution.py:180
  363.0 1.5 convert_element_type.212
  364.6 0.2 convert_element_type.216
  364.9 2.2 fusion.6
  367.1 3.6 collective-permute-start.10
  370.8 3.4 collective-permute-start.11
  378.1 9.5 %collective-permute-done.10 = bf16[2,128,2048]{2,1,0:T(8,128)(2,1)} collective-permute-done((bf16[2,128,2048]{2,1,0:T(8,128)(2,1)S(1)}, bf16[2,128,2048]{2,1,0:T(8,128)(2,1)}, u32[]{:S(2)}, u32[]{:S(2)}) %collective-permute-start.10) | collective-permute-done | bytes 1048608 | tf_op jit(solution)/shard_map/ppermute | solution.py:180
  387.7 1.5 convert_element_type.220
  389.1 0.5 collective-permute-done.11
  389.6 0.2 convert_element_type.224
  389.9 2.2 fusion.4
  392.1 3.6 collective-permute-start.12
  395.7 3.4 collective-permute-start.13
  403.0 8.4 %collective-permute-done.12 = bf16[2,128,2048]{2,1,0:T(8,128)(2,1)} collective-permute-done((bf16[2,128,2048]{2,1,0:T(8,128)(2,1)S(1)}, bf16[2,128,2048]{2,1,0:T(8,128)(2,1)}, u32[]{:S(2)}, u32[]{:S(2)}) %collective-permute-start.12) | collective-permute-done | bytes 1048608 | tf_op jit(solution)/shard_map/ppermute | solution.py:180
  411.5 1.5 convert_element_type.228
  412.9 0.8 collective-permute-done.13
  413.7 0.2 convert_element_type.232
  413.9 2.2 fusion.2
  416.2 3.6 collective-permute-start.14
  419.8 3.4 collective-permute-start.15
  425.3 10.2 %collective-permute-done.14 = bf16[2,128,2048]{2,1,0:T(8,128)(2,1)} collective-permute-done((bf16[2,128,2048]{2,1,0:T(8,128)(2,1)S(1)}, bf16[2,128,2048]{2,1,0:T(8,128)(2,1)}, u32[]{:S(2)}, u32[]{:S(2)}) %collective-permute-start.14) | collective-permute-done | bytes 1048608 | tf_op jit(solution)/shard_map/ppermute | solution.py:180
  435.5 1.5 convert_element_type.236
  436.9 0.2 convert_element_type.240
  437.2 1.6 fusion.1
  438.7 3.6 collective-permute-start.16
  444.2 12.8 %collective-permute-done.16 = bf16[2,128,2048]{2,1,0:T(8,128)(2,1)} collective-permute-done((bf16[2,128,2048]{2,1,0:T(8,128)(2,1)S(1)}, bf16[2,128,2048]{2,1,0:T(8,128)(2,1)}, u32[]{:S(2)}, u32[]{:S(2)}) %collective-permute-start.16) | collective-permute-done | bytes 1048608 | tf_op jit(solution)/shard_map/ppermute | solution.py:180
  457.1 2.0 fusion
  459.1 1.0 slice_bitcast_fusion.2
  (18 shorter events, 0.4 us)
Async XLA Ops:
  0.6 10.7 %copy-start = (bf16[1,256,2048]{2,1,0:T(8,128)(2,1)S(1)}, bf16[1,256,2048]{2,1,0:T(8,128)(2,1)}, u32[]{:S(2)}) copy-start(bf16[1,256,2048]{2,1,0:T(8,128)(2,1)} %param.6) | copy-start | bytes 3145732
  0.6 11.0 %copy-start.3 = (s32[1,4,4]{2,1,0:T(4,128)S(1)}, s32[1,4,4]{2,1,0:T(4,128)}, u32[]{:S(2)}) copy-start(s32[1,4,4]{2,1,0:T(4,128)} %param.9) | copy-start | bytes 196
  0.7 11.2 %copy-start.1 = (bf16[1,1,128,2048]{3,2,1,0:T(8,128)(2,1)S(1)}, bf16[1,1,128,2048]{3,2,1,0:T(8,128)(2,1)}, u32[]{:S(2)}) copy-start(bf16[1,1,128,2048]{3,2,1,0:T(8,128)(2,1)} %param.8) | copy-start | bytes 1572868
  0.7 11.2 %copy-start.2 = (bf16[1,1,128,2048]{3,2,1,0:T(8,128)(2,1)S(1)}, bf16[1,1,128,2048]{3,2,1,0:T(8,128)(2,1)}, u32[]{:S(2)}) copy-start(bf16[1,1,128,2048]{3,2,1,0:T(8,128)(2,1)} %param.7) | copy-start | bytes 1572868
  1.8 212.9 %collective-permute-start = (bf16[63,2048]{1,0:T(8,128)(2,1)S(1)}, bf16[63,2048]{1,0:T(8,128)(2,1)}, u32[]{:S(2)}, u32[]{:S(2)}) collective-permute-start(bf16[63,2048]{1,0:T(8,128)(2,1)S(1)} %slice_bitcast_fusion.5), channel_id=1, source_target_pairs={{1,0},{2,1},{3,2},{4,3},{5,4},{6,5},{7,6},{8,7},{9,8},{10,9},{11,1... | collective-permute-start | bytes 774152 | tf_op jit(solution)/shard_map/ppermute | solution.py:16
  7.4 209.4 %collective-permute-start.1 = (bf16[63,2048]{1,0:T(8,128)(2,1)S(1)}, bf16[63,2048]{1,0:T(8,128)(2,1)S(1)}, u32[]{:S(2)}, u32[]{:S(2)}) collective-permute-start(bf16[63,2048]{1,0:T(8,128)(2,1)S(1)} %slice_bitcast_fusion.4), channel_id=1, source_target_pairs={{1,0},{2,1},{3,2},{4,3},{5,4},{6,5},{7,6},{8,7},{9,8},{10,9},{11,1... | collective-permute-start | bytes 774152 | tf_op jit(solution)/shard_map/ppermute | solution.py:16
  259.6 24.0 %collective-permute-start.2 = (bf16[2,128,2048]{2,1,0:T(8,128)(2,1)S(1)}, bf16[2,128,2048]{2,1,0:T(8,128)(2,1)}, u32[]{:S(2)}, u32[]{:S(2)}) collective-permute-start(bf16[2,128,2048]{2,1,0:T(8,128)(2,1)S(1)} %get-tuple-element.48), channel_id=1, source_target_pairs={{0,32},{32,64},{64,96},{96,128},{128,160},{160,192},{192,224},{224... | collective-permute-start | bytes 3145736 | tf_op jit(solution)/shard_map/ppermute | solution.py:180
  261.8 23.3 %collective-permute-start.3 = (bf16[2,128,2048]{2,1,0:T(8,128)(2,1)S(1)}, bf16[2,128,2048]{2,1,0:T(8,128)(2,1)S(1)}, u32[]{:S(2)}, u32[]{:S(2)}) collective-permute-start(bf16[2,128,2048]{2,1,0:T(8,128)(2,1)S(1)} %get-tuple-element.47), channel_id=1, source_target_pairs={{0,480},{32,0},{64,32},{96,64},{128,96},{160,128},{192,160},{224,1... | collective-permute-start | bytes 3145736 | tf_op jit(solution)/shard_map/ppermute | solution.py:180
  287.6 23.1 %collective-permute-start.4 = (bf16[2,128,2048]{2,1,0:T(8,128)(2,1)S(1)}, bf16[2,128,2048]{2,1,0:T(8,128)(2,1)}, u32[]{:S(2)}, u32[]{:S(2)}) collective-permute-start(bf16[2,128,2048]{2,1,0:T(8,128)(2,1)S(1)} %get-tuple-element.46), channel_id=1, source_target_pairs={{0,32},{32,64},{64,96},{96,128},{128,160},{160,192},{192,224},{224... | collective-permute-start | bytes 3145736 | tf_op jit(solution)/shard_map/ppermute | solution.py:180
  289.5 22.7 %collective-permute-start.5 = (bf16[2,128,2048]{2,1,0:T(8,128)(2,1)S(1)}, bf16[2,128,2048]{2,1,0:T(8,128)(2,1)S(1)}, u32[]{:S(2)}, u32[]{:S(2)}) collective-permute-start(bf16[2,128,2048]{2,1,0:T(8,128)(2,1)S(1)} %get-tuple-element.45), channel_id=1, source_target_pairs={{0,480},{32,0},{64,32},{96,64},{128,96},{160,128},{192,160},{224,1... | collective-permute-start | bytes 3145736 | tf_op jit(solution)/shard_map/ppermute | solution.py:180
  314.7 22.2 %collective-permute-start.6 = (bf16[2,128,2048]{2,1,0:T(8,128)(2,1)S(1)}, bf16[2,128,2048]{2,1,0:T(8,128)(2,1)}, u32[]{:S(2)}, u32[]{:S(2)}) collective-permute-start(bf16[2,128,2048]{2,1,0:T(8,128)(2,1)S(1)} %get-tuple-element.44), channel_id=1, source_target_pairs={{0,32},{32,64},{64,96},{96,128},{128,160},{160,192},{192,224},{224... | collective-permute-start | bytes 3145736 | tf_op jit(solution)/shard_map/ppermute | solution.py:180
  318.0 21.1 %collective-permute-start.7 = (bf16[2,128,2048]{2,1,0:T(8,128)(2,1)S(1)}, bf16[2,128,2048]{2,1,0:T(8,128)(2,1)S(1)}, u32[]{:S(2)}, u32[]{:S(2)}) collective-permute-start(bf16[2,128,2048]{2,1,0:T(8,128)(2,1)S(1)} %get-tuple-element.43), channel_id=1, source_target_pairs={{0,480},{32,0},{64,32},{96,64},{128,96},{160,128},{192,160},{224,1... | collective-permute-start | bytes 3145736 | tf_op jit(solution)/shard_map/ppermute | solution.py:180
  341.5 21.6 %collective-permute-start.8 = (bf16[2,128,2048]{2,1,0:T(8,128)(2,1)S(1)}, bf16[2,128,2048]{2,1,0:T(8,128)(2,1)}, u32[]{:S(2)}, u32[]{:S(2)}) collective-permute-start(bf16[2,128,2048]{2,1,0:T(8,128)(2,1)S(1)} %get-tuple-element.42), channel_id=1, source_target_pairs={{0,32},{32,64},{64,96},{96,128},{128,160},{160,192},{192,224},{224... | collective-permute-start | bytes 3145736 | tf_op jit(solution)/shard_map/ppermute | solution.py:180
  344.8 19.8 %collective-permute-start.9 = (bf16[2,128,2048]{2,1,0:T(8,128)(2,1)S(1)}, bf16[2,128,2048]{2,1,0:T(8,128)(2,1)S(1)}, u32[]{:S(2)}, u32[]{:S(2)}) collective-permute-start(bf16[2,128,2048]{2,1,0:T(8,128)(2,1)S(1)} %get-tuple-element.41), channel_id=1, source_target_pairs={{0,480},{32,0},{64,32},{96,64},{128,96},{160,128},{192,160},{224,1... | collective-permute-start | bytes 3145736 | tf_op jit(solution)/shard_map/ppermute | solution.py:180
  367.1 20.6 %collective-permute-start.10 = (bf16[2,128,2048]{2,1,0:T(8,128)(2,1)S(1)}, bf16[2,128,2048]{2,1,0:T(8,128)(2,1)}, u32[]{:S(2)}, u32[]{:S(2)}) collective-permute-start(bf16[2,128,2048]{2,1,0:T(8,128)(2,1)S(1)} %get-tuple-element.40), channel_id=1, source_target_pairs={{0,32},{32,64},{64,96},{96,128},{128,160},{160,192},{192,224},{224... | collective-permute-start | bytes 3145736 | tf_op jit(solution)/shard_map/ppermute | solution.py:180
  370.8 18.9 %collective-permute-start.11 = (bf16[2,128,2048]{2,1,0:T(8,128)(2,1)S(1)}, bf16[2,128,2048]{2,1,0:T(8,128)(2,1)S(1)}, u32[]{:S(2)}, u32[]{:S(2)}) collective-permute-start(bf16[2,128,2048]{2,1,0:T(8,128)(2,1)S(1)} %get-tuple-element.39), channel_id=1, source_target_pairs={{0,480},{32,0},{64,32},{96,64},{128,96},{160,128},{192,160},{224,1... | collective-permute-start | bytes 3145736 | tf_op jit(solution)/shard_map/ppermute | solution.py:180
  392.1 19.4 %collective-permute-start.12 = (bf16[2,128,2048]{2,1,0:T(8,128)(2,1)S(1)}, bf16[2,128,2048]{2,1,0:T(8,128)(2,1)}, u32[]{:S(2)}, u32[]{:S(2)}) collective-permute-start(bf16[2,128,2048]{2,1,0:T(8,128)(2,1)S(1)} %get-tuple-element.38), channel_id=1, source_target_pairs={{0,32},{32,64},{64,96},{96,128},{128,160},{160,192},{192,224},{224... | collective-permute-start | bytes 3145736 | tf_op jit(solution)/shard_map/ppermute | solution.py:180
  395.7 17.9 %collective-permute-start.13 = (bf16[2,128,2048]{2,1,0:T(8,128)(2,1)S(1)}, bf16[2,128,2048]{2,1,0:T(8,128)(2,1)S(1)}, u32[]{:S(2)}, u32[]{:S(2)}) collective-permute-start(bf16[2,128,2048]{2,1,0:T(8,128)(2,1)S(1)} %get-tuple-element.37), channel_id=1, source_target_pairs={{0,480},{32,0},{64,32},{96,64},{128,96},{160,128},{192,160},{224,1... | collective-permute-start | bytes 3145736 | tf_op jit(solution)/shard_map/ppermute | solution.py:180
  416.2 19.3 %collective-permute-start.14 = (bf16[2,128,2048]{2,1,0:T(8,128)(2,1)S(1)}, bf16[2,128,2048]{2,1,0:T(8,128)(2,1)}, u32[]{:S(2)}, u32[]{:S(2)}) collective-permute-start(bf16[2,128,2048]{2,1,0:T(8,128)(2,1)S(1)} %get-tuple-element.36), channel_id=1, source_target_pairs={{0,32},{32,64},{64,96},{96,128},{128,160},{160,192},{192,224},{224... | collective-permute-start | bytes 3145736 | tf_op jit(solution)/shard_map/ppermute | solution.py:180
  419.8 17.1 %collective-permute-start.15 = (bf16[2,128,2048]{2,1,0:T(8,128)(2,1)S(1)}, bf16[2,128,2048]{2,1,0:T(8,128)(2,1)S(1)}, u32[]{:S(2)}, u32[]{:S(2)}) collective-permute-start(bf16[2,128,2048]{2,1,0:T(8,128)(2,1)S(1)} %get-tuple-element.35), channel_id=1, source_target_pairs={{0,480},{32,0},{64,32},{96,64},{128,96},{160,128},{192,160},{224,1... | collective-permute-start | bytes 3145736 | tf_op jit(solution)/shard_map/ppermute | solution.py:180
  438.7 18.3 %collective-permute-start.16 = (bf16[2,128,2048]{2,1,0:T(8,128)(2,1)S(1)}, bf16[2,128,2048]{2,1,0:T(8,128)(2,1)}, u32[]{:S(2)}, u32[]{:S(2)}) collective-permute-start(bf16[2,128,2048]{2,1,0:T(8,128)(2,1)S(1)} %fusion.1), channel_id=1, source_target_pairs={{0,32},{32,64},{64,96},{96,128},{128,160},{160,192},{192,224},{224... | collective-permute-start | bytes 3145736 | tf_op jit(solution)/shard_map/ppermute | solution.py:180

commit v7 on v6

--- a/solution.py
+++ b/solution.py
@@ -129,32 +129,36 @@
     pl.semaphore_wait(barrier, 2)
     local = pltpu.make_async_copy(held_ref, out_ref.at[0], local_sem)
     local.start()
+    rows = held_ref.shape[1] // 2
+    parts = [(kind, half) for kind in range(2) for half in range(2)]
+    pending, started = {}, []
     for step in range(1, ahead + 1):
-        copies = [
-            pltpu.make_async_remote_copy(
-                src_ref=held_ref if step == 1 else out_ref.at[groups + 1 - step],
-                dst_ref=out_ref.at[groups - step],
-                send_sem=send_sem.at[0, step - 1],
-                recv_sem=recv_sem.at[0, step - 1],
-                device_id=(up, column),
-                device_id_type=pl.DeviceIdType.MESH,
-            )
-        ]
-        if step <= behind:
-            copies.append(
-                pltpu.make_async_remote_copy(
-                    src_ref=held_ref if step == 1 else out_ref.at[step - 1],
-                    dst_ref=out_ref.at[step],
-                    send_sem=send_sem.at[1, step - 1],
-                    recv_sem=recv_sem.at[1, step - 1],
-                    device_id=(down, column),
+        for part, (kind, half) in enumerate(parts):
+            span = pl.ds(half * rows, rows)
+            for direction in (0, 1):
+                if direction == 1 and step > behind:
+                    continue
+                if direction == 0:
+                    source, target, device = groups + 1 - step, groups - step, up
+                else:
+                    source, target, device = step - 1, step, down
+                if step > 1:
+                    pending.pop((direction, part)).wait_recv()
+                copy = pltpu.make_async_remote_copy(
+                    src_ref=held_ref.at[kind, span] if step == 1 else out_ref.at[source, kind, span],
+                    dst_ref=out_ref.at[target, kind, span],
+                    send_sem=send_sem.at[direction, step - 1, part],
+                    recv_sem=recv_sem.at[direction, step - 1, part],
+                    device_id=(device, column),
                     device_id_type=pl.DeviceIdType.MESH,
                 )
-            )
-        for copy in copies:
-            copy.start()
-        for copy in copies:
-            copy.wait()
+                copy.start()
+                pending[(direction, part)] = copy
+                started.append(copy)
+    for copy in pending.values():
+        copy.wait_recv()
+    for copy in started:
+        copy.wait_send()
     local.wait()
 
 
@@ -166,8 +170,8 @@
         in_specs=[pl.BlockSpec(memory_space=pl.ANY)],
         out_specs=pl.BlockSpec(memory_space=pl.ANY),
         scratch_shapes=[
-            pltpu.SemaphoreType.DMA((2, ahead)),
-            pltpu.SemaphoreType.DMA((2, ahead)),
+            pltpu.SemaphoreType.DMA((2, ahead, 4)),
+            pltpu.SemaphoreType.DMA((2, ahead, 4)),
             pltpu.SemaphoreType.DMA(()),
         ],
         compiler_params=pltpu.CompilerParams(collective_id=0, has_side_effects=True),

time: 469 us -> 487 us (1.038)
  waiting for transfers between devices: 91.2 us -> 113 us
    ppermute x15, waiting for transfers between devices: 91.2 us -> 113 us  [ring_step(): return lax.ppermute(array, axis, pairs)]
  transfers between devices with their start and end apart: 17 -> 17, of which waited for: 12 -> 9; matrix products, arithmetic and copies ran while one was open for 4% -> 4% of each run, Pallas kernels for 43% -> 40%
where the time goes in v7:
time: 487 us; the launch traced here: 479 us
  Pallas kernels  233 us (48%)
  waiting for transfers between devices  113 us (23%)
  starting transfers between devices  59.9 us (12%)
  other arithmetic  33.6 us (7%)
  between operations  31.3 us (6%)
  local copies, waits for them, and re-layouts  7.85 us (2%)
    pallas_call x1, Pallas kernels, ring_gather(): pl.pallas_call(gather_kernel, out_shape=jax.ShapeDtypeStruct((groups,) +...  193 us
    ppermute x15, waiting for transfers between devices, ring_step(): return lax.ppermute(array, axis, pairs)  113 us
    ppermute x15, starting transfers between devices, ring_step(): return lax.ppermute(array, axis, pairs)  52.7 us
    pallas_call x1, Pallas kernels, span_attention(): pl.pallas_call(span_kernel, grid_spec=pltpu.PrefetchScalarGridSpec(num_sc...  40 us
    convert_element_type x6, other arithmetic, shards(): (down_arrived + terms(groups - behind + step)).astype(jnp.bfloat16)  13.3 us
    convert_element_type x7, other arithmetic, shards(): up_arrived = ring_step(up_sum, 'grp', 1).astype(jnp.float32)  10.2 us
  transfers between devices with their start and end apart: 17, of which 9 were waited for; matrix products, arithmetic and copies ran while one was open for 4% of the time, Pallas kernels for 40%

profile of v7, /device:TPU:6, one launch (start us, length us, event | category | flops | bytes accessed | tf_op | source)
XLA Modules:
  0.0 479.1 jit_solution(263518286966492928)
XLA Ops:
  0.7 1.1 slice_bitcast_fusion.5
  1.8 4.6 collective-permute-start
  6.4 1.0 slice_bitcast_fusion.4
  7.4 2.6 collective-permute-start.1
  10.0 1.3 slice_bitcast_fusion.1
  11.4 0.2 slice_bitcast_fusion
  11.6 0.1 reshape_squeeze.3
  11.7 0.1 select_reduce_fusion
  11.9 1.1 pad_maximum_fusion.2.held_ref
  12.9 0.7 gather_fusion
  13.6 0.5 and_select_fusion.1.slot_ref
  14.1 0.7 fusion.17
  17.5 192.9 %shard_map.76.block_ref = bf16[16,2,128,2048]{3,2,1,0:T(8,128)(2,1)} custom-call(bf16[2,128,2048]{2,1,0:T(8,128)(2,1)} %pad_maximum_fusion.2.held_ref), custom_call_target="tpu_custom_call" | custom-call | tf_op jit(solution)/shard_map/pallas_call | solution.py:167
  211.7 2.1 pad_maximum_fusion
  213.8 1.1 pad_maximum_fusion.1
  214.9 40.0 %shard_map.77 = (bf16[4,64,2048]{2,1,0:T(8,128)(2,1)}, bf16[16,2,128,2048]{3,2,1,0:T(8,128)(2,1)}) custom-call(s32[16]{0:T(128)} %and_select_fusion.1.slot_ref, bf16[4,64,2048]{2,1,0:T(8,128)(2,1)} %bitcast.81, bf16[4,64,2048]{2,1,0:T(8,128)(2,1)} %bitcast.82, bf16[16,2,128,2048]{3,2,1,0:T(8,128)(2,1)} %shard_map.76.block_ref), custom_call_target="tpu_custom_call" | custom-call | flops 4831838208 | bytes 36700160 | tf_op jit(solution)/shard_map/pallas_call | solution.py:89
  254.9 1.7 dynamic-slice_bitcast_fusion
  256.6 2.9 collective-permute-start.2
  259.5 4.1 collective-permute-start.3
  267.2 16.6 %collective-permute-done.2 = bf16[2,128,2048]{2,1,0:T(8,128)(2,1)} collective-permute-done((bf16[2,128,2048]{2,1,0:T(8,128)(2,1)S(1)}, bf16[2,128,2048]{2,1,0:T(8,128)(2,1)}, u32[]{:S(2)}, u32[]{:S(2)}) %collective-permute-start.2) | collective-permute-done | bytes 1048608 | tf_op jit(solution)/shard_map/ppermute | solution.py:184
  283.9 1.5 convert_element_type.191
  285.3 0.2 convert_element_type.192
  285.6 2.2 fusion.12
  287.8 2.1 collective-permute-start.4
  289.9 5.1 %collective-permute-start.5 = (bf16[2,128,2048]{2,1,0:T(8,128)(2,1)S(1)}, bf16[2,128,2048]{2,1,0:T(8,128)(2,1)S(1)}, u32[]{:S(2)}, u32[]{:S(2)}) collective-permute-start(bf16[2,128,2048]{2,1,0:T(8,128)(2,1)S(1)} %get-tuple-element.45), channel_id=1, source_target_pairs={{0,480},{32,0},{64,32},{96,64},{128,96},{160,128},{192,160},{224,1... | collective-permute-start | bytes 3145736 | tf_op jit(solution)/shard_map/ppermute | solution.py:184
  298.5 15.7 %collective-permute-done.4 = bf16[2,128,2048]{2,1,0:T(8,128)(2,1)} collective-permute-done((bf16[2,128,2048]{2,1,0:T(8,128)(2,1)S(1)}, bf16[2,128,2048]{2,1,0:T(8,128)(2,1)}, u32[]{:S(2)}, u32[]{:S(2)}) %collective-permute-start.4) | collective-permute-done | bytes 1048608 | tf_op jit(solution)/shard_map/ppermute | solution.py:184
  314.2 1.5 convert_element_type.196
  315.7 0.2 convert_element_type.200
  315.9 2.2 fusion.10
  318.1 1.9 collective-permute-start.6
  320.0 5.2 %collective-permute-start.7 = (bf16[2,128,2048]{2,1,0:T(8,128)(2,1)S(1)}, bf16[2,128,2048]{2,1,0:T(8,128)(2,1)S(1)}, u32[]{:S(2)}, u32[]{:S(2)}) collective-permute-start(bf16[2,128,2048]{2,1,0:T(8,128)(2,1)S(1)} %get-tuple-element.43), channel_id=1, source_target_pairs={{0,480},{32,0},{64,32},{96,64},{128,96},{160,128},{192,160},{224,1... | collective-permute-start | bytes 3145736 | tf_op jit(solution)/shard_map/ppermute | solution.py:184
  328.9 14.6 %collective-permute-done.6 = bf16[2,128,2048]{2,1,0:T(8,128)(2,1)} collective-permute-done((bf16[2,128,2048]{2,1,0:T(8,128)(2,1)S(1)}, bf16[2,128,2048]{2,1,0:T(8,128)(2,1)}, u32[]{:S(2)}, u32[]{:S(2)}) %collective-permute-start.6) | collective-permute-done | bytes 1048608 | tf_op jit(solution)/shard_map/ppermute | solution.py:184
  343.6 1.5 convert_element_type.204
  345.1 0.2 convert_element_type.208
  345.3 2.2 fusion.8
  347.5 1.9 collective-permute-start.8
  349.4 5.2 %collective-permute-start.9 = (bf16[2,128,2048]{2,1,0:T(8,128)(2,1)S(1)}, bf16[2,128,2048]{2,1,0:T(8,128)(2,1)S(1)}, u32[]{:S(2)}, u32[]{:S(2)}) collective-permute-start(bf16[2,128,2048]{2,1,0:T(8,128)(2,1)S(1)} %get-tuple-element.41), channel_id=1, source_target_pairs={{0,480},{32,0},{64,32},{96,64},{128,96},{160,128},{192,160},{224,1... | collective-permute-start | bytes 3145736 | tf_op jit(solution)/shard_map/ppermute | solution.py:184
  358.2 13.8 %collective-permute-done.8 = bf16[2,128,2048]{2,1,0:T(8,128)(2,1)} collective-permute-done((bf16[2,128,2048]{2,1,0:T(8,128)(2,1)S(1)}, bf16[2,128,2048]{2,1,0:T(8,128)(2,1)}, u32[]{:S(2)}, u32[]{:S(2)}) %collective-permute-start.8) | collective-permute-done | bytes 1048608 | tf_op jit(solution)/shard_map/ppermute | solution.py:184
  372.0 1.5 convert_element_type.212
  373.5 0.2 convert_element_type.216
  373.8 2.2 fusion.6
  376.0 3.3 collective-permute-start.10
  379.3 3.8 collective-permute-start.11
  387.1 12.5 %collective-permute-done.10 = bf16[2,128,2048]{2,1,0:T(8,128)(2,1)} collective-permute-done((bf16[2,128,2048]{2,1,0:T(8,128)(2,1)S(1)}, bf16[2,128,2048]{2,1,0:T(8,128)(2,1)}, u32[]{:S(2)}, u32[]{:S(2)}) %collective-permute-start.10) | collective-permute-done | bytes 1048608 | tf_op jit(solution)/shard_map/ppermute | solution.py:184
  399.6 1.5 convert_element_type.220
  401.1 0.1 collective-permute-done.11
  401.1 0.2 convert_element_type.224
  401.4 2.2 fusion.4
  403.6 3.6 collective-permute-start.12
  407.2 3.5 collective-permute-start.13
  414.6 11.7 %collective-permute-done.12 = bf16[2,128,2048]{2,1,0:T(8,128)(2,1)} collective-permute-done((bf16[2,128,2048]{2,1,0:T(8,128)(2,1)S(1)}, bf16[2,128,2048]{2,1,0:T(8,128)(2,1)}, u32[]{:S(2)}, u32[]{:S(2)}) %collective-permute-start.12) | collective-permute-done | bytes 1048608 | tf_op jit(solution)/shard_map/ppermute | solution.py:184
  426.2 1.5 convert_element_type.228
  427.7 0.2 convert_element_type.232
  428.0 2.2 fusion.2
  430.2 3.2 collective-permute-start.14
  433.4 3.9 collective-permute-start.15
  439.4 12.6 %collective-permute-done.14 = bf16[2,128,2048]{2,1,0:T(8,128)(2,1)} collective-permute-done((bf16[2,128,2048]{2,1,0:T(8,128)(2,1)S(1)}, bf16[2,128,2048]{2,1,0:T(8,128)(2,1)}, u32[]{:S(2)}, u32[]{:S(2)}) %collective-permute-start.14) | collective-permute-done | bytes 1048608 | tf_op jit(solution)/shard_map/ppermute | solution.py:184
  451.9 1.5 convert_element_type.236
  453.4 0.2 convert_element_type.240
  453.7 1.6 fusion.1
  455.2 3.0 collective-permute-start.16
  460.2 15.9 %collective-permute-done.16 = bf16[2,128,2048]{2,1,0:T(8,128)(2,1)} collective-permute-done((bf16[2,128,2048]{2,1,0:T(8,128)(2,1)S(1)}, bf16[2,128,2048]{2,1,0:T(8,128)(2,1)}, u32[]{:S(2)}, u32[]{:S(2)}) %collective-permute-start.16) | collective-permute-done | bytes 1048608 | tf_op jit(solution)/shard_map/ppermute | solution.py:184
  476.1 2.0 fusion
  478.1 1.0 slice_bitcast_fusion.2
  (18 shorter events, 0.1 us)
Async XLA Ops:
  0.6 10.7 %copy-start = (bf16[1,256,2048]{2,1,0:T(8,128)(2,1)S(1)}, bf16[1,256,2048]{2,1,0:T(8,128)(2,1)}, u32[]{:S(2)}) copy-start(bf16[1,256,2048]{2,1,0:T(8,128)(2,1)} %param.6) | copy-start | bytes 3145732
  0.6 11.0 %copy-start.3 = (s32[1,4,4]{2,1,0:T(4,128)S(1)}, s32[1,4,4]{2,1,0:T(4,128)}, u32[]{:S(2)}) copy-start(s32[1,4,4]{2,1,0:T(4,128)} %param.9) | copy-start | bytes 196
  0.7 11.2 %copy-start.1 = (bf16[1,1,128,2048]{3,2,1,0:T(8,128)(2,1)S(1)}, bf16[1,1,128,2048]{3,2,1,0:T(8,128)(2,1)}, u32[]{:S(2)}) copy-start(bf16[1,1,128,2048]{3,2,1,0:T(8,128)(2,1)} %param.8) | copy-start | bytes 1572868
  0.7 11.2 %copy-start.2 = (bf16[1,1,128,2048]{3,2,1,0:T(8,128)(2,1)S(1)}, bf16[1,1,128,2048]{3,2,1,0:T(8,128)(2,1)}, u32[]{:S(2)}) copy-start(bf16[1,1,128,2048]{3,2,1,0:T(8,128)(2,1)} %param.7) | copy-start | bytes 1572868
  1.8 209.9 %collective-permute-start = (bf16[63,2048]{1,0:T(8,128)(2,1)S(1)}, bf16[63,2048]{1,0:T(8,128)(2,1)}, u32[]{:S(2)}, u32[]{:S(2)}) collective-permute-start(bf16[63,2048]{1,0:T(8,128)(2,1)S(1)} %slice_bitcast_fusion.5), channel_id=1, source_target_pairs={{1,0},{2,1},{3,2},{4,3},{5,4},{6,5},{7,6},{8,7},{9,8},{10,9},{11,1... | collective-permute-start | bytes 774152 | tf_op jit(solution)/shard_map/ppermute | solution.py:16
  7.4 206.4 %collective-permute-start.1 = (bf16[63,2048]{1,0:T(8,128)(2,1)S(1)}, bf16[63,2048]{1,0:T(8,128)(2,1)S(1)}, u32[]{:S(2)}, u32[]{:S(2)}) collective-permute-start(bf16[63,2048]{1,0:T(8,128)(2,1)S(1)} %slice_bitcast_fusion.4), channel_id=1, source_target_pairs={{1,0},{2,1},{3,2},{4,3},{5,4},{6,5},{7,6},{8,7},{9,8},{10,9},{11,1... | collective-permute-start | bytes 774152 | tf_op jit(solution)/shard_map/ppermute | solution.py:16
  256.6 27.2 %collective-permute-start.2 = (bf16[2,128,2048]{2,1,0:T(8,128)(2,1)S(1)}, bf16[2,128,2048]{2,1,0:T(8,128)(2,1)}, u32[]{:S(2)}, u32[]{:S(2)}) collective-permute-start(bf16[2,128,2048]{2,1,0:T(8,128)(2,1)S(1)} %get-tuple-element.48), channel_id=1, source_target_pairs={{0,32},{32,64},{64,96},{96,128},{128,160},{160,192},{192,224},{224... | collective-permute-start | bytes 3145736 | tf_op jit(solution)/shard_map/ppermute | solution.py:184
  259.5 25.8 %collective-permute-start.3 = (bf16[2,128,2048]{2,1,0:T(8,128)(2,1)S(1)}, bf16[2,128,2048]{2,1,0:T(8,128)(2,1)S(1)}, u32[]{:S(2)}, u32[]{:S(2)}) collective-permute-start(bf16[2,128,2048]{2,1,0:T(8,128)(2,1)S(1)} %get-tuple-element.47), channel_id=1, source_target_pairs={{0,480},{32,0},{64,32},{96,64},{128,96},{160,128},{192,160},{224,1... | collective-permute-start | bytes 3145736 | tf_op jit(solution)/shard_map/ppermute | solution.py:184
  287.8 26.4 %collective-permute-start.4 = (bf16[2,128,2048]{2,1,0:T(8,128)(2,1)S(1)}, bf16[2,128,2048]{2,1,0:T(8,128)(2,1)}, u32[]{:S(2)}, u32[]{:S(2)}) collective-permute-start(bf16[2,128,2048]{2,1,0:T(8,128)(2,1)S(1)} %get-tuple-element.46), channel_id=1, source_target_pairs={{0,32},{32,64},{64,96},{96,128},{128,160},{160,192},{192,224},{224... | collective-permute-start | bytes 3145736 | tf_op jit(solution)/shard_map/ppermute | solution.py:184
  289.9 25.8 %collective-permute-start.5 = (bf16[2,128,2048]{2,1,0:T(8,128)(2,1)S(1)}, bf16[2,128,2048]{2,1,0:T(8,128)(2,1)S(1)}, u32[]{:S(2)}, u32[]{:S(2)}) collective-permute-start(bf16[2,128,2048]{2,1,0:T(8,128)(2,1)S(1)} %get-tuple-element.45), channel_id=1, source_target_pairs={{0,480},{32,0},{64,32},{96,64},{128,96},{160,128},{192,160},{224,1... | collective-permute-start | bytes 3145736 | tf_op jit(solution)/shard_map/ppermute | solution.py:184
  318.1 25.5 %collective-permute-start.6 = (bf16[2,128,2048]{2,1,0:T(8,128)(2,1)S(1)}, bf16[2,128,2048]{2,1,0:T(8,128)(2,1)}, u32[]{:S(2)}, u32[]{:S(2)}) collective-permute-start(bf16[2,128,2048]{2,1,0:T(8,128)(2,1)S(1)} %get-tuple-element.44), channel_id=1, source_target_pairs={{0,32},{32,64},{64,96},{96,128},{128,160},{160,192},{192,224},{224... | collective-permute-start | bytes 3145736 | tf_op jit(solution)/shard_map/ppermute | solution.py:184
  320.0 25.0 %collective-permute-start.7 = (bf16[2,128,2048]{2,1,0:T(8,128)(2,1)S(1)}, bf16[2,128,2048]{2,1,0:T(8,128)(2,1)S(1)}, u32[]{:S(2)}, u32[]{:S(2)}) collective-permute-start(bf16[2,128,2048]{2,1,0:T(8,128)(2,1)S(1)} %get-tuple-element.43), channel_id=1, source_target_pairs={{0,480},{32,0},{64,32},{96,64},{128,96},{160,128},{192,160},{224,1... | collective-permute-start | bytes 3145736 | tf_op jit(solution)/shard_map/ppermute | solution.py:184
  347.5 24.5 %collective-permute-start.8 = (bf16[2,128,2048]{2,1,0:T(8,128)(2,1)S(1)}, bf16[2,128,2048]{2,1,0:T(8,128)(2,1)}, u32[]{:S(2)}, u32[]{:S(2)}) collective-permute-start(bf16[2,128,2048]{2,1,0:T(8,128)(2,1)S(1)} %get-tuple-element.42), channel_id=1, source_target_pairs={{0,32},{32,64},{64,96},{96,128},{128,160},{160,192},{192,224},{224... | collective-permute-start | bytes 3145736 | tf_op jit(solution)/shard_map/ppermute | solution.py:184
  349.4 24.1 %collective-permute-start.9 = (bf16[2,128,2048]{2,1,0:T(8,128)(2,1)S(1)}, bf16[2,128,2048]{2,1,0:T(8,128)(2,1)S(1)}, u32[]{:S(2)}, u32[]{:S(2)}) collective-permute-start(bf16[2,128,2048]{2,1,0:T(8,128)(2,1)S(1)} %get-tuple-element.41), channel_id=1, source_target_pairs={{0,480},{32,0},{64,32},{96,64},{128,96},{160,128},{192,160},{224,1... | collective-permute-start | bytes 3145736 | tf_op jit(solution)/shard_map/ppermute | solution.py:184
  376.0 23.6 %collective-permute-start.10 = (bf16[2,128,2048]{2,1,0:T(8,128)(2,1)S(1)}, bf16[2,128,2048]{2,1,0:T(8,128)(2,1)}, u32[]{:S(2)}, u32[]{:S(2)}) collective-permute-start(bf16[2,128,2048]{2,1,0:T(8,128)(2,1)S(1)} %get-tuple-element.40), channel_id=1, source_target_pairs={{0,32},{32,64},{64,96},{96,128},{128,160},{160,192},{192,224},{224... | collective-permute-start | bytes 3145736 | tf_op jit(solution)/shard_map/ppermute | solution.py:184
  379.3 21.8 %collective-permute-start.11 = (bf16[2,128,2048]{2,1,0:T(8,128)(2,1)S(1)}, bf16[2,128,2048]{2,1,0:T(8,128)(2,1)S(1)}, u32[]{:S(2)}, u32[]{:S(2)}) collective-permute-start(bf16[2,128,2048]{2,1,0:T(8,128)(2,1)S(1)} %get-tuple-element.39), channel_id=1, source_target_pairs={{0,480},{32,0},{64,32},{96,64},{128,96},{160,128},{192,160},{224,1... | collective-permute-start | bytes 3145736 | tf_op jit(solution)/shard_map/ppermute | solution.py:184
  403.6 22.6 %collective-permute-start.12 = (bf16[2,128,2048]{2,1,0:T(8,128)(2,1)S(1)}, bf16[2,128,2048]{2,1,0:T(8,128)(2,1)}, u32[]{:S(2)}, u32[]{:S(2)}) collective-permute-start(bf16[2,128,2048]{2,1,0:T(8,128)(2,1)S(1)} %get-tuple-element.38), channel_id=1, source_target_pairs={{0,32},{32,64},{64,96},{96,128},{128,160},{160,192},{192,224},{224... | collective-permute-start | bytes 3145736 | tf_op jit(solution)/shard_map/ppermute | solution.py:184
  407.2 20.5 %collective-permute-start.13 = (bf16[2,128,2048]{2,1,0:T(8,128)(2,1)S(1)}, bf16[2,128,2048]{2,1,0:T(8,128)(2,1)S(1)}, u32[]{:S(2)}, u32[]{:S(2)}) collective-permute-start(bf16[2,128,2048]{2,1,0:T(8,128)(2,1)S(1)} %get-tuple-element.37), channel_id=1, source_target_pairs={{0,480},{32,0},{64,32},{96,64},{128,96},{160,128},{192,160},{224,1... | collective-permute-start | bytes 3145736 | tf_op jit(solution)/shard_map/ppermute | solution.py:184
  430.2 21.8 %collective-permute-start.14 = (bf16[2,128,2048]{2,1,0:T(8,128)(2,1)S(1)}, bf16[2,128,2048]{2,1,0:T(8,128)(2,1)}, u32[]{:S(2)}, u32[]{:S(2)}) collective-permute-start(bf16[2,128,2048]{2,1,0:T(8,128)(2,1)S(1)} %get-tuple-element.36), channel_id=1, source_target_pairs={{0,32},{32,64},{64,96},{96,128},{128,160},{160,192},{192,224},{224... | collective-permute-start | bytes 3145736 | tf_op jit(solution)/shard_map/ppermute | solution.py:184
  433.4 20.0 %collective-permute-start.15 = (bf16[2,128,2048]{2,1,0:T(8,128)(2,1)S(1)}, bf16[2,128,2048]{2,1,0:T(8,128)(2,1)S(1)}, u32[]{:S(2)}, u32[]{:S(2)}) collective-permute-start(bf16[2,128,2048]{2,1,0:T(8,128)(2,1)S(1)} %get-tuple-element.35), channel_id=1, source_target_pairs={{0,480},{32,0},{64,32},{96,64},{128,96},{160,128},{192,160},{224,1... | collective-permute-start | bytes 3145736 | tf_op jit(solution)/shard_map/ppermute | solution.py:184
  455.2 20.9 %collective-permute-start.16 = (bf16[2,128,2048]{2,1,0:T(8,128)(2,1)S(1)}, bf16[2,128,2048]{2,1,0:T(8,128)(2,1)}, u32[]{:S(2)}, u32[]{:S(2)}) collective-permute-start(bf16[2,128,2048]{2,1,0:T(8,128)(2,1)S(1)} %fusion.1), channel_id=1, source_target_pairs={{0,32},{32,64},{64,96},{96,128},{128,160},{160,192},{192,224},{224... | collective-permute-start | bytes 3145736 | tf_op jit(solution)/shard_map/ppermute | solution.py:184

commit v8 on v6

--- a/solution.py
+++ b/solution.py
@@ -113,7 +113,7 @@
     )(pair_slot, window_query, window_grad, blocks)
 
 
-def gather_kernel(held_ref, out_ref, send_sem, recv_sem, local_sem):
+def gather_kernel(key_ref, value_ref, out_ref, send_sem, recv_sem, local_sem):
     groups = lax.axis_size("grp")
     me = lax.axis_index("grp")
     column = lax.axis_index("seq")
@@ -127,51 +127,56 @@
             barrier, 1, device_id=(neighbour, column), device_id_type=pl.DeviceIdType.MESH
         )
     pl.semaphore_wait(barrier, 2)
-    local = pltpu.make_async_copy(held_ref, out_ref.at[0], local_sem)
-    local.start()
+    own = (key_ref.at[0, 0], value_ref.at[0, 0])
+    locals_ = [
+        pltpu.make_async_copy(own[kind], out_ref.at[0, kind], local_sem.at[kind]) for kind in range(2)
+    ]
+    for copy in locals_:
+        copy.start()
     for step in range(1, ahead + 1):
-        copies = [
-            pltpu.make_async_remote_copy(
-                src_ref=held_ref if step == 1 else out_ref.at[groups + 1 - step],
-                dst_ref=out_ref.at[groups - step],
-                send_sem=send_sem.at[0, step - 1],
-                recv_sem=recv_sem.at[0, step - 1],
-                device_id=(up, column),
-                device_id_type=pl.DeviceIdType.MESH,
-            )
-        ]
+        routes = [(0, groups + 1 - step, groups - step, up)]
         if step <= behind:
-            copies.append(
-                pltpu.make_async_remote_copy(
-                    src_ref=held_ref if step == 1 else out_ref.at[step - 1],
-                    dst_ref=out_ref.at[step],
-                    send_sem=send_sem.at[1, step - 1],
-                    recv_sem=recv_sem.at[1, step - 1],
-                    device_id=(down, column),
-                    device_id_type=pl.DeviceIdType.MESH,
+            routes.append((1, step - 1, step, down))
+        copies = []
+        for direction, source, target, device in routes:
+            if step == 1:
+                pieces = [(own[kind], out_ref.at[target, kind], kind) for kind in range(2)]
+            else:
+                pieces = [(out_ref.at[source], out_ref.at[target], 0)]
+            for src, dst, part in pieces:
+                copies.append(
+                    pltpu.make_async_remote_copy(
+                        src_ref=src,
+                        dst_ref=dst,
+                        send_sem=send_sem.at[direction, step - 1, part],
+                        recv_sem=recv_sem.at[direction, step - 1, part],
+                        device_id=(device, column),
+                        device_id_type=pl.DeviceIdType.MESH,
+                    )
                 )
-            )
         for copy in copies:
             copy.start()
         for copy in copies:
             copy.wait()
-    local.wait()
-
-
-def ring_gather(held, groups):
+    for copy in locals_:
+        copy.wait()
+
+
+def ring_gather(keys, values, groups):
     ahead = groups // 2
+    block_shape = keys.shape[2:]
     return pl.pallas_call(
         gather_kernel,
-        out_shape=jax.ShapeDtypeStruct((groups,) + held.shape, held.dtype),
-        in_specs=[pl.BlockSpec(memory_space=pl.ANY)],
+        out_shape=jax.ShapeDtypeStruct((groups, 2) + block_shape, keys.dtype),
+        in_specs=[pl.BlockSpec(memory_space=pl.ANY), pl.BlockSpec(memory_space=pl.ANY)],
         out_specs=pl.BlockSpec(memory_space=pl.ANY),
         scratch_shapes=[
-            pltpu.SemaphoreType.DMA((2, ahead)),
-            pltpu.SemaphoreType.DMA((2, ahead)),
-            pltpu.SemaphoreType.DMA(()),
+            pltpu.SemaphoreType.DMA((2, ahead, 2)),
+            pltpu.SemaphoreType.DMA((2, ahead, 2)),
+            pltpu.SemaphoreType.DMA((2,)),
         ],
         compiler_params=pltpu.CompilerParams(collective_id=0, has_side_effects=True),
-    )(held)
+    )(keys, values)
 
 
 def ring_step(array, axis, by):
@@ -208,8 +213,7 @@
     placement = (owner_ids[None, :] == group_ids[:, None]).astype(jnp.int32)
     rel_groups = (me + group_ids) % groups
     pair_slot = (owner_ids - me) % groups
-    held = jnp.stack([neighbour_keys[0, 0], neighbour_values[0, 0]])
-    all_blocks = ring_gather(held, groups)
+    all_blocks = ring_gather(neighbour_keys, neighbour_values, groups)
     grad_windows, pair_terms = span_attention(pair_slot, window_query, window_grad, all_blocks)
     grad_windows = grad_windows.reshape(1, span_count, span_len, row_width)
     slot_pair = jnp.sum(placement * jnp.arange(pair_count, dtype=jnp.int32)[None, :], axis=1)

time: 469 us -> 467 us (level)
  transfers between devices with their start and end apart: 17 -> 17, of which waited for: 12 -> 12; matrix products, arithmetic and copies ran while one was open for 4% -> 3% of each run, Pallas kernels for 43% -> 43%
where the time goes in v8:
time: 467 us; the launch traced here: 458 us
  Pallas kernels  236 us (51%)
  waiting for transfers between devices  90.8 us (19%)
  starting transfers between devices  60.3 us (13%)
  other arithmetic  31.6 us (7%)
  between operations  31.3 us (7%)
  local copies, waits for them, and re-layouts  7.77 us (2%)
    pallas_call x1, Pallas kernels, ring_gather(): pl.pallas_call(gather_kernel, out_shape=jax.ShapeDtypeStruct((groups, 2)...  196 us
    ppermute x15, waiting for transfers between devices, ring_step(): return lax.ppermute(array, axis, pairs)  90.8 us
    ppermute x15, starting transfers between devices, ring_step(): return lax.ppermute(array, axis, pairs)  53.1 us
    pallas_call x1, Pallas kernels, span_attention(): pl.pallas_call(span_kernel, grid_spec=pltpu.PrefetchScalarGridSpec(num_sc...  40 us
    convert_element_type x6, other arithmetic, shards(): (down_arrived + terms(groups - behind + step)).astype(jnp.bfloat16)  13.3 us
    convert_element_type x7, other arithmetic, shards(): up_arrived = ring_step(up_sum, 'grp', 1).astype(jnp.float32)  10.2 us
  transfers between devices with their start and end apart: 17, of which 12 were waited for; matrix products, arithmetic and copies ran while one was open for 3% of the time, Pallas kernels for 43%

profile of v8, /device:TPU:6, one launch (start us, length us, event | category | flops | bytes accessed | tf_op | source)
XLA Modules:
  0.0 458.0 jit_solution(13288733904047351056)
XLA Ops:
  0.7 1.1 slice_bitcast_fusion.5
  1.7 4.6 %collective-permute-start = (bf16[63,2048]{1,0:T(8,128)(2,1)S(1)}, bf16[63,2048]{1,0:T(8,128)(2,1)S(1)}, u32[]{:S(2)}, u32[]{:S(2)}) collective-permute-start(bf16[63,2048]{1,0:T(8,128)(2,1)S(1)} %slice_bitcast_fusion.5), channel_id=1, source_target_pairs={{1,0},{2,1},{3,2},{4,3},{5,4},{6,5},{7,6},{8,7},{9,8},{10,9},{11,1... | collective-permute-start | bytes 774152 | tf_op jit(solution)/shard_map/ppermute | solution.py:16
  6.3 1.0 slice_bitcast_fusion.4
  7.3 2.6 collective-permute-start.1
  9.9 1.3 slice_bitcast_fusion.1
  11.3 0.2 slice_bitcast_fusion
  11.8 0.7 gather_fusion
  12.4 0.5 and_select_fusion.1.slot_ref
  12.9 0.7 fusion.17
  16.1 196.2 %shard_map.76.block_ref = bf16[16,2,128,2048]{3,2,1,0:T(8,128)(2,1)} custom-call(bf16[1,1,128,2048]{3,2,1,0:T(8,128)(2,1)} %key_ref.1, bf16[1,1,128,2048]{3,2,1,0:T(8,128)(2,1)} %value_ref.1), custom_call_target="tpu_custom_call" | custom-call | tf_op jit(solution)/shard_map/pallas_call | solution.py:168
  213.5 1.1 pad_maximum_fusion
  214.7 1.1 pad_maximum_fusion.1
  215.8 40.0 %shard_map.77 = (bf16[4,64,2048]{2,1,0:T(8,128)(2,1)}, bf16[16,2,128,2048]{3,2,1,0:T(8,128)(2,1)}) custom-call(s32[16]{0:T(128)} %and_select_fusion.1.slot_ref, bf16[4,64,2048]{2,1,0:T(8,128)(2,1)} %bitcast.79, bf16[4,64,2048]{2,1,0:T(8,128)(2,1)} %bitcast.80, bf16[16,2,128,2048]{3,2,1,0:T(8,128)(2,1)} %shard_map.76.block_ref), custom_call_target="tpu_custom_call" | custom-call | flops 4831838208 | bytes 36700160 | tf_op jit(solution)/shard_map/pallas_call | solution.py:89
  255.8 1.7 dynamic-slice_bitcast_fusion
  257.5 2.1 collective-permute-start.2
  259.6 4.9 %collective-permute-start.3 = (bf16[2,128,2048]{2,1,0:T(8,128)(2,1)S(1)}, bf16[2,128,2048]{2,1,0:T(8,128)(2,1)S(1)}, u32[]{:S(2)}, u32[]{:S(2)}) collective-permute-start(bf16[2,128,2048]{2,1,0:T(8,128)(2,1)S(1)} %get-tuple-element.47), channel_id=1, source_target_pairs={{0,480},{32,0},{64,32},{96,64},{128,96},{160,128},{192,160},{224,1... | collective-permute-start | bytes 3145736 | tf_op jit(solution)/shard_map/ppermute | solution.py:185
  268.1 13.4 %collective-permute-done.2 = bf16[2,128,2048]{2,1,0:T(8,128)(2,1)} collective-permute-done((bf16[2,128,2048]{2,1,0:T(8,128)(2,1)S(1)}, bf16[2,128,2048]{2,1,0:T(8,128)(2,1)}, u32[]{:S(2)}, u32[]{:S(2)}) %collective-permute-start.2) | collective-permute-done | bytes 1048608 | tf_op jit(solution)/shard_map/ppermute | solution.py:185
  281.5 1.5 convert_element_type.191
  283.0 0.2 convert_element_type.192
  283.2 2.2 fusion.12
  285.4 1.9 collective-permute-start.4
  287.4 5.2 %collective-permute-start.5 = (bf16[2,128,2048]{2,1,0:T(8,128)(2,1)S(1)}, bf16[2,128,2048]{2,1,0:T(8,128)(2,1)S(1)}, u32[]{:S(2)}, u32[]{:S(2)}) collective-permute-start(bf16[2,128,2048]{2,1,0:T(8,128)(2,1)S(1)} %get-tuple-element.45), channel_id=1, source_target_pairs={{0,480},{32,0},{64,32},{96,64},{128,96},{160,128},{192,160},{224,1... | collective-permute-start | bytes 3145736 | tf_op jit(solution)/shard_map/ppermute | solution.py:185
  296.2 12.3 %collective-permute-done.4 = bf16[2,128,2048]{2,1,0:T(8,128)(2,1)} collective-permute-done((bf16[2,128,2048]{2,1,0:T(8,128)(2,1)S(1)}, bf16[2,128,2048]{2,1,0:T(8,128)(2,1)}, u32[]{:S(2)}, u32[]{:S(2)}) %collective-permute-start.4) | collective-permute-done | bytes 1048608 | tf_op jit(solution)/shard_map/ppermute | solution.py:185
  308.6 1.5 convert_element_type.196
  310.0 0.2 convert_element_type.200
  310.3 2.2 fusion.10
  312.5 3.3 collective-permute-start.6
  315.8 3.8 collective-permute-start.7
  323.2 11.5 %collective-permute-done.6 = bf16[2,128,2048]{2,1,0:T(8,128)(2,1)} collective-permute-done((bf16[2,128,2048]{2,1,0:T(8,128)(2,1)S(1)}, bf16[2,128,2048]{2,1,0:T(8,128)(2,1)}, u32[]{:S(2)}, u32[]{:S(2)}) %collective-permute-start.6) | collective-permute-done | bytes 1048608 | tf_op jit(solution)/shard_map/ppermute | solution.py:185
  334.7 1.5 convert_element_type.204
  336.2 0.7 collective-permute-done.7
  336.9 0.2 convert_element_type.208
  337.1 2.2 fusion.8
  339.3 3.4 collective-permute-start.8
  342.7 3.7 collective-permute-start.9
  350.4 10.5 %collective-permute-done.8 = bf16[2,128,2048]{2,1,0:T(8,128)(2,1)} collective-permute-done((bf16[2,128,2048]{2,1,0:T(8,128)(2,1)S(1)}, bf16[2,128,2048]{2,1,0:T(8,128)(2,1)}, u32[]{:S(2)}, u32[]{:S(2)}) %collective-permute-start.8) | collective-permute-done | bytes 1048608 | tf_op jit(solution)/shard_map/ppermute | solution.py:185
  360.9 1.5 convert_element_type.212
  362.4 0.1 collective-permute-done.9
  362.5 0.2 convert_element_type.216
  362.7 2.2 fusion.6
  365.0 3.6 collective-permute-start.10
  368.6 3.4 collective-permute-start.11
  375.9 9.6 %collective-permute-done.10 = bf16[2,128,2048]{2,1,0:T(8,128)(2,1)} collective-permute-done((bf16[2,128,2048]{2,1,0:T(8,128)(2,1)S(1)}, bf16[2,128,2048]{2,1,0:T(8,128)(2,1)}, u32[]{:S(2)}, u32[]{:S(2)}) %collective-permute-start.10) | collective-permute-done | bytes 1048608 | tf_op jit(solution)/shard_map/ppermute | solution.py:185
  385.5 1.5 convert_element_type.220
  387.0 0.5 collective-permute-done.11
  387.5 0.2 convert_element_type.224
  387.7 2.2 fusion.4
  390.0 3.6 collective-permute-start.12
  393.6 3.4 collective-permute-start.13
  400.9 8.4 %collective-permute-done.12 = bf16[2,128,2048]{2,1,0:T(8,128)(2,1)} collective-permute-done((bf16[2,128,2048]{2,1,0:T(8,128)(2,1)S(1)}, bf16[2,128,2048]{2,1,0:T(8,128)(2,1)}, u32[]{:S(2)}, u32[]{:S(2)}) %collective-permute-start.12) | collective-permute-done | bytes 1048608 | tf_op jit(solution)/shard_map/ppermute | solution.py:185
  409.3 1.5 convert_element_type.228
  410.8 0.8 collective-permute-done.13
  411.6 0.2 convert_element_type.232
  411.8 2.2 fusion.2
  414.0 3.6 collective-permute-start.14
  417.7 3.4 collective-permute-start.15
  423.2 10.2 %collective-permute-done.14 = bf16[2,128,2048]{2,1,0:T(8,128)(2,1)} collective-permute-done((bf16[2,128,2048]{2,1,0:T(8,128)(2,1)S(1)}, bf16[2,128,2048]{2,1,0:T(8,128)(2,1)}, u32[]{:S(2)}, u32[]{:S(2)}) %collective-permute-start.14) | collective-permute-done | bytes 1048608 | tf_op jit(solution)/shard_map/ppermute | solution.py:185
  433.3 1.5 convert_element_type.236
  434.8 0.2 convert_element_type.240
  435.0 1.6 fusion.1
  436.6 3.6 collective-permute-start.16
  442.1 12.8 %collective-permute-done.16 = bf16[2,128,2048]{2,1,0:T(8,128)(2,1)} collective-permute-done((bf16[2,128,2048]{2,1,0:T(8,128)(2,1)S(1)}, bf16[2,128,2048]{2,1,0:T(8,128)(2,1)}, u32[]{:S(2)}, u32[]{:S(2)}) %collective-permute-start.16) | collective-permute-done | bytes 1048608 | tf_op jit(solution)/shard_map/ppermute | solution.py:185
  454.9 2.0 fusion
  456.9 1.0 slice_bitcast_fusion.2
  (13 shorter events, 0.2 us)
Async XLA Ops:
  0.6 10.6 %copy-start = (bf16[1,256,2048]{2,1,0:T(8,128)(2,1)S(1)}, bf16[1,256,2048]{2,1,0:T(8,128)(2,1)}, u32[]{:S(2)}) copy-start(bf16[1,256,2048]{2,1,0:T(8,128)(2,1)} %param.6) | copy-start | bytes 3145732
  0.6 10.9 %copy-start.1 = (s32[1,4,4]{2,1,0:T(4,128)S(1)}, s32[1,4,4]{2,1,0:T(4,128)}, u32[]{:S(2)}) copy-start(s32[1,4,4]{2,1,0:T(4,128)} %param.9) | copy-start | bytes 196
  1.7 211.8 %collective-permute-start = (bf16[63,2048]{1,0:T(8,128)(2,1)S(1)}, bf16[63,2048]{1,0:T(8,128)(2,1)S(1)}, u32[]{:S(2)}, u32[]{:S(2)}) collective-permute-start(bf16[63,2048]{1,0:T(8,128)(2,1)S(1)} %slice_bitcast_fusion.5), channel_id=1, source_target_pairs={{1,0},{2,1},{3,2},{4,3},{5,4},{6,5},{7,6},{8,7},{9,8},{10,9},{11,1... | collective-permute-start | bytes 774152 | tf_op jit(solution)/shard_map/ppermute | solution.py:16
  7.3 207.3 %collective-permute-start.1 = (bf16[63,2048]{1,0:T(8,128)(2,1)S(1)}, bf16[63,2048]{1,0:T(8,128)(2,1)S(1)}, u32[]{:S(2)}, u32[]{:S(2)}) collective-permute-start(bf16[63,2048]{1,0:T(8,128)(2,1)S(1)} %slice_bitcast_fusion.4), channel_id=1, source_target_pairs={{1,0},{2,1},{3,2},{4,3},{5,4},{6,5},{7,6},{8,7},{9,8},{10,9},{11,1... | collective-permute-start | bytes 774152 | tf_op jit(solution)/shard_map/ppermute | solution.py:16
  257.5 24.0 %collective-permute-start.2 = (bf16[2,128,2048]{2,1,0:T(8,128)(2,1)S(1)}, bf16[2,128,2048]{2,1,0:T(8,128)(2,1)}, u32[]{:S(2)}, u32[]{:S(2)}) collective-permute-start(bf16[2,128,2048]{2,1,0:T(8,128)(2,1)S(1)} %get-tuple-element.48), channel_id=1, source_target_pairs={{0,32},{32,64},{64,96},{96,128},{128,160},{160,192},{192,224},{224... | collective-permute-start | bytes 3145736 | tf_op jit(solution)/shard_map/ppermute | solution.py:185
  259.6 23.3 %collective-permute-start.3 = (bf16[2,128,2048]{2,1,0:T(8,128)(2,1)S(1)}, bf16[2,128,2048]{2,1,0:T(8,128)(2,1)S(1)}, u32[]{:S(2)}, u32[]{:S(2)}) collective-permute-start(bf16[2,128,2048]{2,1,0:T(8,128)(2,1)S(1)} %get-tuple-element.47), channel_id=1, source_target_pairs={{0,480},{32,0},{64,32},{96,64},{128,96},{160,128},{192,160},{224,1... | collective-permute-start | bytes 3145736 | tf_op jit(solution)/shard_map/ppermute | solution.py:185
  285.4 23.1 %collective-permute-start.4 = (bf16[2,128,2048]{2,1,0:T(8,128)(2,1)S(1)}, bf16[2,128,2048]{2,1,0:T(8,128)(2,1)}, u32[]{:S(2)}, u32[]{:S(2)}) collective-permute-start(bf16[2,128,2048]{2,1,0:T(8,128)(2,1)S(1)} %get-tuple-element.46), channel_id=1, source_target_pairs={{0,32},{32,64},{64,96},{96,128},{128,160},{160,192},{192,224},{224... | collective-permute-start | bytes 3145736 | tf_op jit(solution)/shard_map/ppermute | solution.py:185
  287.4 22.7 %collective-permute-start.5 = (bf16[2,128,2048]{2,1,0:T(8,128)(2,1)S(1)}, bf16[2,128,2048]{2,1,0:T(8,128)(2,1)S(1)}, u32[]{:S(2)}, u32[]{:S(2)}) collective-permute-start(bf16[2,128,2048]{2,1,0:T(8,128)(2,1)S(1)} %get-tuple-element.45), channel_id=1, source_target_pairs={{0,480},{32,0},{64,32},{96,64},{128,96},{160,128},{192,160},{224,1... | collective-permute-start | bytes 3145736 | tf_op jit(solution)/shard_map/ppermute | solution.py:185
  312.5 22.2 %collective-permute-start.6 = (bf16[2,128,2048]{2,1,0:T(8,128)(2,1)S(1)}, bf16[2,128,2048]{2,1,0:T(8,128)(2,1)}, u32[]{:S(2)}, u32[]{:S(2)}) collective-permute-start(bf16[2,128,2048]{2,1,0:T(8,128)(2,1)S(1)} %get-tuple-element.44), channel_id=1, source_target_pairs={{0,32},{32,64},{64,96},{96,128},{128,160},{160,192},{192,224},{224... | collective-permute-start | bytes 3145736 | tf_op jit(solution)/shard_map/ppermute | solution.py:185
  315.8 21.1 %collective-permute-start.7 = (bf16[2,128,2048]{2,1,0:T(8,128)(2,1)S(1)}, bf16[2,128,2048]{2,1,0:T(8,128)(2,1)S(1)}, u32[]{:S(2)}, u32[]{:S(2)}) collective-permute-start(bf16[2,128,2048]{2,1,0:T(8,128)(2,1)S(1)} %get-tuple-element.43), channel_id=1, source_target_pairs={{0,480},{32,0},{64,32},{96,64},{128,96},{160,128},{192,160},{224,1... | collective-permute-start | bytes 3145736 | tf_op jit(solution)/shard_map/ppermute | solution.py:185
  339.3 21.6 %collective-permute-start.8 = (bf16[2,128,2048]{2,1,0:T(8,128)(2,1)S(1)}, bf16[2,128,2048]{2,1,0:T(8,128)(2,1)}, u32[]{:S(2)}, u32[]{:S(2)}) collective-permute-start(bf16[2,128,2048]{2,1,0:T(8,128)(2,1)S(1)} %get-tuple-element.42), channel_id=1, source_target_pairs={{0,32},{32,64},{64,96},{96,128},{128,160},{160,192},{192,224},{224... | collective-permute-start | bytes 3145736 | tf_op jit(solution)/shard_map/ppermute | solution.py:185
  342.7 19.8 %collective-permute-start.9 = (bf16[2,128,2048]{2,1,0:T(8,128)(2,1)S(1)}, bf16[2,128,2048]{2,1,0:T(8,128)(2,1)S(1)}, u32[]{:S(2)}, u32[]{:S(2)}) collective-permute-start(bf16[2,128,2048]{2,1,0:T(8,128)(2,1)S(1)} %get-tuple-element.41), channel_id=1, source_target_pairs={{0,480},{32,0},{64,32},{96,64},{128,96},{160,128},{192,160},{224,1... | collective-permute-start | bytes 3145736 | tf_op jit(solution)/shard_map/ppermute | solution.py:185
  365.0 20.6 %collective-permute-start.10 = (bf16[2,128,2048]{2,1,0:T(8,128)(2,1)S(1)}, bf16[2,128,2048]{2,1,0:T(8,128)(2,1)}, u32[]{:S(2)}, u32[]{:S(2)}) collective-permute-start(bf16[2,128,2048]{2,1,0:T(8,128)(2,1)S(1)} %get-tuple-element.40), channel_id=1, source_target_pairs={{0,32},{32,64},{64,96},{96,128},{128,160},{160,192},{192,224},{224... | collective-permute-start | bytes 3145736 | tf_op jit(solution)/shard_map/ppermute | solution.py:185
  368.6 18.9 %collective-permute-start.11 = (bf16[2,128,2048]{2,1,0:T(8,128)(2,1)S(1)}, bf16[2,128,2048]{2,1,0:T(8,128)(2,1)S(1)}, u32[]{:S(2)}, u32[]{:S(2)}) collective-permute-start(bf16[2,128,2048]{2,1,0:T(8,128)(2,1)S(1)} %get-tuple-element.39), channel_id=1, source_target_pairs={{0,480},{32,0},{64,32},{96,64},{128,96},{160,128},{192,160},{224,1... | collective-permute-start | bytes 3145736 | tf_op jit(solution)/shard_map/ppermute | solution.py:185
  390.0 19.4 %collective-permute-start.12 = (bf16[2,128,2048]{2,1,0:T(8,128)(2,1)S(1)}, bf16[2,128,2048]{2,1,0:T(8,128)(2,1)}, u32[]{:S(2)}, u32[]{:S(2)}) collective-permute-start(bf16[2,128,2048]{2,1,0:T(8,128)(2,1)S(1)} %get-tuple-element.38), channel_id=1, source_target_pairs={{0,32},{32,64},{64,96},{96,128},{128,160},{160,192},{192,224},{224... | collective-permute-start | bytes 3145736 | tf_op jit(solution)/shard_map/ppermute | solution.py:185
  393.6 17.9 %collective-permute-start.13 = (bf16[2,128,2048]{2,1,0:T(8,128)(2,1)S(1)}, bf16[2,128,2048]{2,1,0:T(8,128)(2,1)S(1)}, u32[]{:S(2)}, u32[]{:S(2)}) collective-permute-start(bf16[2,128,2048]{2,1,0:T(8,128)(2,1)S(1)} %get-tuple-element.37), channel_id=1, source_target_pairs={{0,480},{32,0},{64,32},{96,64},{128,96},{160,128},{192,160},{224,1... | collective-permute-start | bytes 3145736 | tf_op jit(solution)/shard_map/ppermute | solution.py:185
  414.0 19.3 %collective-permute-start.14 = (bf16[2,128,2048]{2,1,0:T(8,128)(2,1)S(1)}, bf16[2,128,2048]{2,1,0:T(8,128)(2,1)}, u32[]{:S(2)}, u32[]{:S(2)}) collective-permute-start(bf16[2,128,2048]{2,1,0:T(8,128)(2,1)S(1)} %get-tuple-element.36), channel_id=1, source_target_pairs={{0,32},{32,64},{64,96},{96,128},{128,160},{160,192},{192,224},{224... | collective-permute-start | bytes 3145736 | tf_op jit(solution)/shard_map/ppermute | solution.py:185
  417.7 17.1 %collective-permute-start.15 = (bf16[2,128,2048]{2,1,0:T(8,128)(2,1)S(1)}, bf16[2,128,2048]{2,1,0:T(8,128)(2,1)S(1)}, u32[]{:S(2)}, u32[]{:S(2)}) collective-permute-start(bf16[2,128,2048]{2,1,0:T(8,128)(2,1)S(1)} %get-tuple-element.35), channel_id=1, source_target_pairs={{0,480},{32,0},{64,32},{96,64},{128,96},{160,128},{192,160},{224,1... | collective-permute-start | bytes 3145736 | tf_op jit(solution)/shard_map/ppermute | solution.py:185
  436.6 18.3 %collective-permute-start.16 = (bf16[2,128,2048]{2,1,0:T(8,128)(2,1)S(1)}, bf16[2,128,2048]{2,1,0:T(8,128)(2,1)}, u32[]{:S(2)}, u32[]{:S(2)}) collective-permute-start(bf16[2,128,2048]{2,1,0:T(8,128)(2,1)S(1)} %fusion.1), channel_id=1, source_target_pairs={{0,32},{32,64},{64,96},{96,128},{128,160},{160,192},{192,224},{224... | collective-permute-start | bytes 3145736 | tf_op jit(solution)/shard_map/ppermute | solution.py:185

commit v9 on v8

--- a/solution.py
+++ b/solution.py
@@ -69,8 +69,8 @@
         value_term = lax.dot_general(probs_t, grad, plain, preferred_element_type=jnp.float32)
         key_term = lax.dot_general(scores_t, query, plain, preferred_element_type=jnp.float32) * scale
         for j in range(NBRS):
-            term_ref[span * NBRS + j, 0] = key_term[j * HEAD : (j + 1) * HEAD].astype(term_ref.dtype)
-            term_ref[span * NBRS + j, 1] = value_term[j * HEAD : (j + 1) * HEAD].astype(term_ref.dtype)
+            term_ref[slots[j], 0] = key_term[j * HEAD : (j + 1) * HEAD].astype(term_ref.dtype)
+            term_ref[slots[j], 1] = value_term[j * HEAD : (j + 1) * HEAD].astype(term_ref.dtype)
 
 
 def span_attention(pair_slot, window_query, window_grad, blocks):
@@ -179,6 +179,102 @@
     )(keys, values)
 
 
+def add_rows(target, first, second):
+    rows = 16
+
+    def body(index, carry):
+        part = pl.ds(pl.multiple_of(index * rows, rows), rows)
+        for kind in range(target.shape[0]):
+            total = first[kind, part].astype(jnp.float32) + second[kind, part].astype(jnp.float32)
+            target[kind, part] = total.astype(target.dtype)
+        return carry
+
+    lax.fori_loop(0, target.shape[1] // rows, body, 0)
+
+
+def reduce_kernel(term_ref, out_ref, own, recv_up, recv_down, send_up, send_down, local_sem, send_sem, recv_sem):
+    groups = lax.axis_size("grp")
+    me = lax.axis_index("grp")
+    column = lax.axis_index("seq")
+    ahead = groups // 2
+    behind = groups - 1 - ahead
+    up = lax.rem(me + 1, groups)
+    down = lax.rem(me + groups - 1, groups)
+    barrier = pltpu.get_barrier_semaphore()
+    for neighbour in (up, down):
+        pl.semaphore_signal(
+            barrier, 1, device_id=(neighbour, column), device_id_type=pl.DeviceIdType.MESH
+        )
+    pl.semaphore_wait(barrier, 2)
+    load = pltpu.make_async_copy(term_ref, own, local_sem)
+    load.start()
+    for step in range(1, ahead + 1):
+        if step == 2:
+            load.wait()
+        routes = [(0, up, recv_up, send_up, term_ref.at[ahead], ahead - step + 1)]
+        if step <= behind:
+            routes.append((1, down, recv_down, send_down, term_ref.at[groups - behind], groups - behind + step - 1))
+        copies = []
+        for direction, device, recv, send, first, slot in routes:
+            if step == 1:
+                source = first
+            else:
+                add_rows(send.at[step - 2], recv.at[step - 2], own.at[slot])
+                source = send.at[step - 2]
+            copies.append(
+                pltpu.make_async_remote_copy(
+                    src_ref=source,
+                    dst_ref=recv.at[step - 1],
+                    send_sem=send_sem.at[direction, step - 1],
+                    recv_sem=recv_sem.at[direction, step - 1],
+                    device_id=(device, column),
+                    device_id_type=pl.DeviceIdType.MESH,
+                )
+            )
+            copies[-1].start()
+        for copy in copies:
+            copy.wait()
+    rows = 16
+
+    def body(index, carry):
+        part = pl.ds(pl.multiple_of(index * rows, rows), rows)
+        for kind in range(out_ref.shape[0]):
+            total = (
+                recv_up[ahead - 1, kind, part].astype(jnp.float32)
+                + recv_down[behind - 1, kind, part].astype(jnp.float32)
+                + own[0, kind, part].astype(jnp.float32)
+            )
+            out_ref[kind, part] = total.astype(out_ref.dtype)
+        return carry
+
+    lax.fori_loop(0, out_ref.shape[1] // rows, body, 0)
+
+
+def ring_reduce(terms, groups):
+    ahead = groups // 2
+    behind = groups - 1 - ahead
+    block = terms.shape[1:]
+    return pl.pallas_call(
+        reduce_kernel,
+        out_shape=jax.ShapeDtypeStruct(block, terms.dtype),
+        in_specs=[pl.BlockSpec(memory_space=pl.ANY)],
+        out_specs=pl.BlockSpec(memory_space=pltpu.VMEM),
+        scratch_shapes=[
+            pltpu.VMEM(terms.shape, terms.dtype),
+            pltpu.VMEM((ahead,) + block, terms.dtype),
+            pltpu.VMEM((behind,) + block, terms.dtype),
+            pltpu.VMEM((ahead - 1,) + block, terms.dtype),
+            pltpu.VMEM((behind - 1,) + block, terms.dtype),
+            pltpu.SemaphoreType.DMA(()),
+            pltpu.SemaphoreType.DMA((2, ahead)),
+            pltpu.SemaphoreType.DMA((2, ahead)),
+        ],
+        compiler_params=pltpu.CompilerParams(
+            collective_id=1, has_side_effects=True, vmem_limit_bytes=60 * 1024 * 1024
+        ),
+    )(terms)
+
+
 def ring_step(array, axis, by):
     length = lax.axis_size(axis)
     pairs = [(i, (i + by) % length) for i in range(length)]
@@ -216,24 +312,7 @@
     all_blocks = ring_gather(neighbour_keys, neighbour_values, groups)
     grad_windows, pair_terms = span_attention(pair_slot, window_query, window_grad, all_blocks)
     grad_windows = grad_windows.reshape(1, span_count, span_len, row_width)
-    slot_pair = jnp.sum(placement * jnp.arange(pair_count, dtype=jnp.int32)[None, :], axis=1)
-    slot_pair = slot_pair[rel_groups]
-
-    def terms(slot):
-        return lax.dynamic_index_in_dim(pair_terms, slot_pair[slot], axis=0, keepdims=False)
-
-    up_sum = terms(ahead)
-    down_sum = terms(groups - behind)
-    for step in range(1, ahead + 1):
-        up_arrived = ring_step(up_sum, "grp", 1).astype(jnp.float32)
-        if step <= behind:
-            down_arrived = ring_step(down_sum, "grp", -1).astype(jnp.float32)
-            up_arrived, down_arrived = lax.optimization_barrier((up_arrived, down_arrived))
-        if step < ahead:
-            up_sum = (up_arrived + terms(ahead - step)).astype(jnp.bfloat16)
-        if step < behind:
-            down_sum = (down_arrived + terms(groups - behind + step)).astype(jnp.bfloat16)
-    total = up_arrived + down_arrived + terms(0).astype(jnp.float32)
+    total = ring_reduce(pair_terms, groups)
     grad_keys = total[0].astype(jnp.bfloat16).reshape(1, 1, neighbour_len, row_width)
     grad_values = total[1].astype(jnp.bfloat16).reshape(1, 1, neighbour_len, row_width)
     return (grad_windows, grad_keys, grad_values)

time: 467 us -> 438 us (0.938); the launches traced: 458 us -> 435 us
  Pallas kernels: 236 us -> 418 us
  waiting for transfers between devices: 90.8 us -> 0.01 us
  starting transfers between devices: 60.3 us -> 7.21 us
  between operations: 31.3 us -> 0.74 us
  other arithmetic: 31.6 us -> 2.75 us
    pallas_call x0 -> x1, Pallas kernels: none -> 182 us  [ring_reduce(): pl.pallas_call(reduce_kernel, out_shape=jax.ShapeDtypeStruct(block, terms...]
    ppermute x15 -> x0, waiting for transfers between devices: 90.8 us -> none  [ring_step(): return lax.ppermute(array, axis, pairs)]
    ppermute x15 -> x0, starting transfers between devices: 53.1 us -> none  [ring_step(): return lax.ppermute(array, axis, pairs)]
    convert_element_type x21 -> x0, other arithmetic: 26.7 us -> none  [the longest x6 13.3 us: shards(): (down_arrived + terms(groups - behind + step)).astype(jnp.bfloat16)]
  transfers between devices with their start and end apart: 17 -> 2, of which waited for: 12 -> 0; matrix products, arithmetic and copies ran while one was open for 3% -> 1% of each run, Pallas kernels for 43% -> 45%
where the time goes in v9:
time: 438 us; the launch traced here: 435 us
  Pallas kernels  418 us (95%)
  starting transfers between devices  7.21 us (2%)
  local copies, waits for them, and re-layouts  5.93 us (1%)
    pallas_call x1, Pallas kernels, ring_gather(): pl.pallas_call(gather_kernel, out_shape=jax.ShapeDtypeStruct((groups, 2)...  196 us
    pallas_call x1, Pallas kernels, ring_reduce(): pl.pallas_call(reduce_kernel, out_shape=jax.ShapeDtypeStruct(block, terms...  182 us
    pallas_call x1, Pallas kernels, span_attention(): pl.pallas_call(span_kernel, grid_spec=pltpu.PrefetchScalarGridSpec(num_sc...  40.1 us
  transfers between devices with their start and end apart: 2, of which 0 were waited for; matrix products, arithmetic and copies ran while one was open for 1% of the time, Pallas kernels for 45%

profile of v9, /device:TPU:6, one launch (start us, length us, event | category | flops | bytes accessed | tf_op | source)
XLA Modules:
  0.0 434.9 jit_solution(17462183366458968608)
XLA Ops:
  0.6 0.0 copy-start
  0.6 0.0 copy-start.1
  0.7 1.1 slice_bitcast_fusion.4
  1.7 4.6 %collective-permute-start.1 = (bf16[63,2048]{1,0:T(8,128)(2,1)S(1)}, bf16[63,2048]{1,0:T(8,128)(2,1)S(1)}, u32[]{:S(2)}, u32[]{:S(2)}) collective-permute-start(bf16[63,2048]{1,0:T(8,128)(2,1)S(1)} %slice_bitcast_fusion.4), channel_id=1, source_target_pairs={{1,0},{2,1},{3,2},{4,3},{5,4},{6,5},{7,6},{8,7},{9,8},{10,9},{11,1... | collective-permute-start | bytes 774152 | tf_op jit(solution)/shard_map/ppermute | solution.py:16
  6.3 1.0 slice_bitcast_fusion.5
  7.3 2.6 collective-permute-start
  9.9 1.3 slice_bitcast_fusion.1
  11.3 0.0 copy-done
  11.3 0.2 slice_bitcast_fusion
  11.5 0.0 copy-done.1
  11.5 0.1 sub.11
  11.6 0.5 and_select_fusion.slot_ref
  12.1 196.2 %shard_map.76.block_ref = bf16[16,2,128,2048]{3,2,1,0:T(8,128)(2,1)} custom-call(bf16[1,1,128,2048]{3,2,1,0:T(8,128)(2,1)} %key_ref.1, bf16[1,1,128,2048]{3,2,1,0:T(8,128)(2,1)} %value_ref.1), custom_call_target="tpu_custom_call" | custom-call | tf_op jit(solution)/shard_map/pallas_call | solution.py:168
  208.4 0.0 collective-permute-done
  208.4 1.1 pad_maximum_fusion
  209.5 0.0 collective-permute-done.1
  209.5 1.1 pad_maximum_fusion.1
  210.6 40.1 %shard_map.77 = (bf16[4,64,2048]{2,1,0:T(8,128)(2,1)}, bf16[16,2,128,2048]{3,2,1,0:T(8,128)(2,1)}) custom-call(s32[16]{0:T(128)} %and_select_fusion.slot_ref, bf16[4,64,2048]{2,1,0:T(8,128)(2,1)} %bitcast.15, bf16[4,64,2048]{2,1,0:T(8,128)(2,1)} %bitcast.16, bf16[16,2,128,2048]{3,2,1,0:T(8,128)(2,1)} %shard_map.76.block_ref), custom_call_target="tpu_custom_call" | custom-call | flops 4831838208 | bytes 36700160 | tf_op jit(solution)/shard_map/pallas_call | solution.py:89
  250.6 181.9 %shard_map.78 = bf16[2,128,2048]{2,1,0:T(8,128)(2,1)} custom-call(bf16[16,2,128,2048]{3,2,1,0:T(8,128)(2,1)} %get-tuple-element.6.term_ref), custom_call_target="tpu_custom_call" | custom-call | tf_op jit(solution)/shard_map/pallas_call | solution.py:257
  432.6 2.3 slice_bitcast_fusion.2
  (1 shorter events, 0.0 us)
Async XLA Ops:
  0.6 10.6 %copy-start = (bf16[1,256,2048]{2,1,0:T(8,128)(2,1)S(1)}, bf16[1,256,2048]{2,1,0:T(8,128)(2,1)}, u32[]{:S(2)}) copy-start(bf16[1,256,2048]{2,1,0:T(8,128)(2,1)} %param.6) | copy-start | bytes 3145732
  0.6 10.8 %copy-start.1 = (s32[1,4,4]{2,1,0:T(4,128)S(1)}, s32[1,4,4]{2,1,0:T(4,128)}, u32[]{:S(2)}) copy-start(s32[1,4,4]{2,1,0:T(4,128)} %param.9) | copy-start | bytes 196
  1.7 207.7 %collective-permute-start.1 = (bf16[63,2048]{1,0:T(8,128)(2,1)S(1)}, bf16[63,2048]{1,0:T(8,128)(2,1)S(1)}, u32[]{:S(2)}, u32[]{:S(2)}) collective-permute-start(bf16[63,2048]{1,0:T(8,128)(2,1)S(1)} %slice_bitcast_fusion.4), channel_id=1, source_target_pairs={{1,0},{2,1},{3,2},{4,3},{5,4},{6,5},{7,6},{8,7},{9,8},{10,9},{11,1... | collective-permute-start | bytes 774152 | tf_op jit(solution)/shard_map/ppermute | solution.py:16
  7.3 201.0 %collective-permute-start = (bf16[63,2048]{1,0:T(8,128)(2,1)S(1)}, bf16[63,2048]{1,0:T(8,128)(2,1)S(1)}, u32[]{:S(2)}, u32[]{:S(2)}) collective-permute-start(bf16[63,2048]{1,0:T(8,128)(2,1)S(1)} %slice_bitcast_fusion.5), channel_id=1, source_target_pairs={{1,0},{2,1},{3,2},{4,3},{5,4},{6,5},{7,6},{8,7},{9,8},{10,9},{11,1... | collective-permute-start | bytes 774152 | tf_op jit(solution)/shard_map/ppermute | solution.py:16

commit v10 on v9

--- a/solution.py
+++ b/solution.py
@@ -133,31 +133,36 @@
     ]
     for copy in locals_:
         copy.start()
+    rows = key_ref.shape[2] // 2
+    parts = [(kind, half) for kind in range(2) for half in range(2)]
+    pending, started = {}, []
     for step in range(1, ahead + 1):
-        routes = [(0, groups + 1 - step, groups - step, up)]
-        if step <= behind:
-            routes.append((1, step - 1, step, down))
-        copies = []
-        for direction, source, target, device in routes:
-            if step == 1:
-                pieces = [(own[kind], out_ref.at[target, kind], kind) for kind in range(2)]
-            else:
-                pieces = [(out_ref.at[source], out_ref.at[target], 0)]
-            for src, dst, part in pieces:
-                copies.append(
-                    pltpu.make_async_remote_copy(
-                        src_ref=src,
-                        dst_ref=dst,
-                        send_sem=send_sem.at[direction, step - 1, part],
-                        recv_sem=recv_sem.at[direction, step - 1, part],
-                        device_id=(device, column),
-                        device_id_type=pl.DeviceIdType.MESH,
-                    )
+        for part, (kind, half) in enumerate(parts):
+            span = pl.ds(half * rows, rows)
+            for direction in (0, 1):
+                if direction == 1 and step > behind:
+                    continue
+                if direction == 0:
+                    source, target, device = groups + 1 - step, groups - step, up
+                else:
+                    source, target, device = step - 1, step, down
+                if step > 1:
+                    pending.pop((direction, part)).wait_recv()
+                copy = pltpu.make_async_remote_copy(
+                    src_ref=own[kind].at[span] if step == 1 else out_ref.at[source, kind, span],
+                    dst_ref=out_ref.at[target, kind, span],
+                    send_sem=send_sem.at[direction, step - 1, part],
+                    recv_sem=recv_sem.at[direction, step - 1, part],
+                    device_id=(device, column),
+                    device_id_type=pl.DeviceIdType.MESH,
                 )
-        for copy in copies:
-            copy.start()
-        for copy in copies:
-            copy.wait()
+                copy.start()
+                pending[(direction, part)] = copy
+                started.append(copy)
+    for copy in pending.values():
+        copy.wait_recv()
+    for copy in started:
+        copy.wait_send()
     for copy in locals_:
         copy.wait()
 
@@ -171,8 +176,8 @@
         in_specs=[pl.BlockSpec(memory_space=pl.ANY), pl.BlockSpec(memory_space=pl.ANY)],
         out_specs=pl.BlockSpec(memory_space=pl.ANY),
         scratch_shapes=[
-            pltpu.SemaphoreType.DMA((2, ahead, 2)),
-            pltpu.SemaphoreType.DMA((2, ahead, 2)),
+            pltpu.SemaphoreType.DMA((2, ahead, 4)),
+            pltpu.SemaphoreType.DMA((2, ahead, 4)),
             pltpu.SemaphoreType.DMA((2,)),
         ],
         compiler_params=pltpu.CompilerParams(collective_id=0, has_side_effects=True),

time: 438 us -> 438 us (level)
    pallas_call x1, Pallas kernels: 182 us -> 186 us  [ring_reduce(): pl.pallas_call(reduce_kernel, out_shape=jax.ShapeDtypeStruct(block, terms...]
  transfers between devices with their start and end apart: 2 -> 2, of which waited for: 0 -> 0; matrix products, arithmetic and copies ran while one was open for 1% -> 1% of each run, Pallas kernels for 45% -> 44%
where the time goes in v10:
time: 438 us; the launch traced here: 436 us
  Pallas kernels  419 us (96%)
  starting transfers between devices  7.21 us (2%)
  local copies, waits for them, and re-layouts  5.93 us (1%)
    pallas_call x1, Pallas kernels, ring_gather(): pl.pallas_call(gather_kernel, out_shape=jax.ShapeDtypeStruct((groups, 2)...  193 us
    pallas_call x1, Pallas kernels, ring_reduce(): pl.pallas_call(reduce_kernel, out_shape=jax.ShapeDtypeStruct(block, terms...  186 us
    pallas_call x1, Pallas kernels, span_attention(): pl.pallas_call(span_kernel, grid_spec=pltpu.PrefetchScalarGridSpec(num_sc...  40.1 us
  transfers between devices with their start and end apart: 2, of which 0 were waited for; matrix products, arithmetic and copies ran while one was open for 1% of the time, Pallas kernels for 44%

profile of v10, /device:TPU:6, one launch (start us, length us, event | category | flops | bytes accessed | tf_op | source)
XLA Modules:
  0.0 436.0 jit_solution(1156612532467703398)
XLA Ops:
  0.6 0.0 copy-start
  0.6 0.0 copy-start.1
  0.7 1.1 slice_bitcast_fusion.4
  1.7 4.6 %collective-permute-start.1 = (bf16[63,2048]{1,0:T(8,128)(2,1)S(1)}, bf16[63,2048]{1,0:T(8,128)(2,1)S(1)}, u32[]{:S(2)}, u32[]{:S(2)}) collective-permute-start(bf16[63,2048]{1,0:T(8,128)(2,1)S(1)} %slice_bitcast_fusion.4), channel_id=1, source_target_pairs={{1,0},{2,1},{3,2},{4,3},{5,4},{6,5},{7,6},{8,7},{9,8},{10,9},{11,1... | collective-permute-start | bytes 774152 | tf_op jit(solution)/shard_map/ppermute | solution.py:16
  6.3 1.0 slice_bitcast_fusion.5
  7.3 2.6 collective-permute-start
  9.9 1.3 slice_bitcast_fusion.1
  11.3 0.0 copy-done
  11.3 0.2 slice_bitcast_fusion
  11.5 0.0 copy-done.1
  11.5 0.1 sub.11
  11.6 0.5 and_select_fusion.slot_ref
  12.1 193.0 %shard_map.76.block_ref = bf16[16,2,128,2048]{3,2,1,0:T(8,128)(2,1)} custom-call(bf16[1,1,128,2048]{3,2,1,0:T(8,128)(2,1)} %key_ref.1, bf16[1,1,128,2048]{3,2,1,0:T(8,128)(2,1)} %value_ref.1), custom_call_target="tpu_custom_call" | custom-call | tf_op jit(solution)/shard_map/pallas_call | solution.py:173
  205.1 0.0 collective-permute-done
  205.1 1.1 pad_maximum_fusion
  206.2 0.0 collective-permute-done.1
  206.2 1.1 pad_maximum_fusion.1
  207.3 40.1 %shard_map.77 = (bf16[4,64,2048]{2,1,0:T(8,128)(2,1)}, bf16[16,2,128,2048]{3,2,1,0:T(8,128)(2,1)}) custom-call(s32[16]{0:T(128)} %and_select_fusion.slot_ref, bf16[4,64,2048]{2,1,0:T(8,128)(2,1)} %bitcast.15, bf16[4,64,2048]{2,1,0:T(8,128)(2,1)} %bitcast.16, bf16[16,2,128,2048]{3,2,1,0:T(8,128)(2,1)} %shard_map.76.block_ref), custom_call_target="tpu_custom_call" | custom-call | flops 4831838208 | bytes 36700160 | tf_op jit(solution)/shard_map/pallas_call | solution.py:89
  247.4 186.4 %shard_map.78 = bf16[2,128,2048]{2,1,0:T(8,128)(2,1)} custom-call(bf16[16,2,128,2048]{3,2,1,0:T(8,128)(2,1)} %get-tuple-element.6.term_ref), custom_call_target="tpu_custom_call" | custom-call | tf_op jit(solution)/shard_map/pallas_call | solution.py:262
  433.7 2.3 slice_bitcast_fusion.2
  (1 shorter events, 0.0 us)
Async XLA Ops:
  0.6 10.6 %copy-start = (bf16[1,256,2048]{2,1,0:T(8,128)(2,1)S(1)}, bf16[1,256,2048]{2,1,0:T(8,128)(2,1)}, u32[]{:S(2)}) copy-start(bf16[1,256,2048]{2,1,0:T(8,128)(2,1)} %param.6) | copy-start | bytes 3145732
  0.6 10.8 %copy-start.1 = (s32[1,4,4]{2,1,0:T(4,128)S(1)}, s32[1,4,4]{2,1,0:T(4,128)}, u32[]{:S(2)}) copy-start(s32[1,4,4]{2,1,0:T(4,128)} %param.9) | copy-start | bytes 196
  1.7 204.5 %collective-permute-start.1 = (bf16[63,2048]{1,0:T(8,128)(2,1)S(1)}, bf16[63,2048]{1,0:T(8,128)(2,1)S(1)}, u32[]{:S(2)}, u32[]{:S(2)}) collective-permute-start(bf16[63,2048]{1,0:T(8,128)(2,1)S(1)} %slice_bitcast_fusion.4), channel_id=1, source_target_pairs={{1,0},{2,1},{3,2},{4,3},{5,4},{6,5},{7,6},{8,7},{9,8},{10,9},{11,1... | collective-permute-start | bytes 774152 | tf_op jit(solution)/shard_map/ppermute | solution.py:16
  7.3 197.8 %collective-permute-start = (bf16[63,2048]{1,0:T(8,128)(2,1)S(1)}, bf16[63,2048]{1,0:T(8,128)(2,1)S(1)}, u32[]{:S(2)}, u32[]{:S(2)}) collective-permute-start(bf16[63,2048]{1,0:T(8,128)(2,1)S(1)} %slice_bitcast_fusion.5), channel_id=1, source_target_pairs={{1,0},{2,1},{3,2},{4,3},{5,4},{6,5},{7,6},{8,7},{9,8},{10,9},{11,1... | collective-permute-start | bytes 774152 | tf_op jit(solution)/shard_map/ppermute | solution.py:16

commit v11 on v9

--- a/solution.py
+++ b/solution.py
@@ -64,10 +64,14 @@
             )
             window = window + (part * scale).astype(jnp.bfloat16).astype(jnp.float32)
         window_ref[span] = window.astype(window_ref.dtype)
-        probs_t = probs.astype(jnp.bfloat16).astype(jnp.float32).T.astype(jnp.bfloat16)
-        scores_t = grad_scores.astype(jnp.float32).T.astype(jnp.bfloat16)
-        value_term = lax.dot_general(probs_t, grad, plain, preferred_element_type=jnp.float32)
-        key_term = lax.dot_general(scores_t, query, plain, preferred_element_type=jnp.float32) * scale
+        contract_first = (((0,), (0,)), ((), ()))
+        value_term = lax.dot_general(
+            probs.astype(jnp.bfloat16), grad, contract_first, preferred_element_type=jnp.float32
+        )
+        key_term = (
+            lax.dot_general(grad_scores, query, contract_first, preferred_element_type=jnp.float32)
+            * scale
+        )
         for j in range(NBRS):
             term_ref[slots[j], 0] = key_term[j * HEAD : (j + 1) * HEAD].astype(term_ref.dtype)
             term_ref[slots[j], 1] = value_term[j * HEAD : (j + 1) * HEAD].astype(term_ref.dtype)

time: 438 us -> 436 us (level)
  no operation moved by 1% of the time
where the time goes in v11:
time: 436 us; the launch traced here: 434 us
  Pallas kernels  417 us (96%)
  starting transfers between devices  7.21 us (2%)
  local copies, waits for them, and re-layouts  5.93 us (1%)
    pallas_call x1, Pallas kernels, ring_gather(): pl.pallas_call(gather_kernel, out_shape=jax.ShapeDtypeStruct((groups, 2)...  196 us
    pallas_call x1, Pallas kernels, ring_reduce(): pl.pallas_call(reduce_kernel, out_shape=jax.ShapeDtypeStruct(block, terms...  182 us
    pallas_call x1, Pallas kernels, span_attention(): pl.pallas_call(span_kernel, grid_spec=pltpu.PrefetchScalarGridSpec(num_sc...  38.7 us
  transfers between devices with their start and end apart: 2, of which 0 were waited for; matrix products, arithmetic and copies ran while one was open for 1% of the time, Pallas kernels for 45%

profile of v11, /device:TPU:6, one launch (start us, length us, event | category | flops | bytes accessed | tf_op | source)
XLA Modules:
  0.0 433.5 jit_solution(657015807750277253)
XLA Ops:
  0.6 0.0 copy-start
  0.6 0.0 copy-start.1
  0.7 1.1 slice_bitcast_fusion.4
  1.7 4.6 %collective-permute-start.1 = (bf16[63,2048]{1,0:T(8,128)(2,1)S(1)}, bf16[63,2048]{1,0:T(8,128)(2,1)S(1)}, u32[]{:S(2)}, u32[]{:S(2)}) collective-permute-start(bf16[63,2048]{1,0:T(8,128)(2,1)S(1)} %slice_bitcast_fusion.4), channel_id=1, source_target_pairs={{1,0},{2,1},{3,2},{4,3},{5,4},{6,5},{7,6},{8,7},{9,8},{10,9},{11,1... | collective-permute-start | bytes 774152 | tf_op jit(solution)/shard_map/ppermute | solution.py:16
  6.3 1.0 slice_bitcast_fusion.5
  7.3 2.6 collective-permute-start
  9.9 1.3 slice_bitcast_fusion.1
  11.3 0.0 copy-done
  11.3 0.2 slice_bitcast_fusion
  11.5 0.0 copy-done.1
  11.5 0.1 sub.11
  11.6 0.5 and_select_fusion.slot_ref
  12.1 196.2 %shard_map.76.block_ref = bf16[16,2,128,2048]{3,2,1,0:T(8,128)(2,1)} custom-call(bf16[1,1,128,2048]{3,2,1,0:T(8,128)(2,1)} %key_ref.1, bf16[1,1,128,2048]{3,2,1,0:T(8,128)(2,1)} %value_ref.1), custom_call_target="tpu_custom_call" | custom-call | tf_op jit(solution)/shard_map/pallas_call | solution.py:172
  208.4 0.0 collective-permute-done
  208.4 1.1 pad_maximum_fusion
  209.5 0.0 collective-permute-done.1
  209.5 1.1 pad_maximum_fusion.1
  210.6 38.7 %shard_map.77 = (bf16[4,64,2048]{2,1,0:T(8,128)(2,1)}, bf16[16,2,128,2048]{3,2,1,0:T(8,128)(2,1)}) custom-call(s32[16]{0:T(128)} %and_select_fusion.slot_ref, bf16[4,64,2048]{2,1,0:T(8,128)(2,1)} %bitcast.15, bf16[4,64,2048]{2,1,0:T(8,128)(2,1)} %bitcast.16, bf16[16,2,128,2048]{3,2,1,0:T(8,128)(2,1)} %shard_map.76.block_ref), custom_call_target="tpu_custom_call" | custom-call | flops 4831838208 | bytes 36700160 | tf_op jit(solution)/shard_map/pallas_call | solution.py:93
  249.3 181.9 %shard_map.78 = bf16[2,128,2048]{2,1,0:T(8,128)(2,1)} custom-call(bf16[16,2,128,2048]{3,2,1,0:T(8,128)(2,1)} %get-tuple-element.6.term_ref), custom_call_target="tpu_custom_call" | custom-call | tf_op jit(solution)/shard_map/pallas_call | solution.py:261
  431.2 2.3 slice_bitcast_fusion.2
  (1 shorter events, 0.0 us)
Async XLA Ops:
  0.6 10.6 %copy-start = (bf16[1,256,2048]{2,1,0:T(8,128)(2,1)S(1)}, bf16[1,256,2048]{2,1,0:T(8,128)(2,1)}, u32[]{:S(2)}) copy-start(bf16[1,256,2048]{2,1,0:T(8,128)(2,1)} %param.6) | copy-start | bytes 3145732
  0.6 10.8 %copy-start.1 = (s32[1,4,4]{2,1,0:T(4,128)S(1)}, s32[1,4,4]{2,1,0:T(4,128)}, u32[]{:S(2)}) copy-start(s32[1,4,4]{2,1,0:T(4,128)} %param.9) | copy-start | bytes 196
  1.7 207.7 %collective-permute-start.1 = (bf16[63,2048]{1,0:T(8,128)(2,1)S(1)}, bf16[63,2048]{1,0:T(8,128)(2,1)S(1)}, u32[]{:S(2)}, u32[]{:S(2)}) collective-permute-start(bf16[63,2048]{1,0:T(8,128)(2,1)S(1)} %slice_bitcast_fusion.4), channel_id=1, source_target_pairs={{1,0},{2,1},{3,2},{4,3},{5,4},{6,5},{7,6},{8,7},{9,8},{10,9},{11,1... | collective-permute-start | bytes 774152 | tf_op jit(solution)/shard_map/ppermute | solution.py:16
  7.3 201.0 %collective-permute-start = (bf16[63,2048]{1,0:T(8,128)(2,1)S(1)}, bf16[63,2048]{1,0:T(8,128)(2,1)S(1)}, u32[]{:S(2)}, u32[]{:S(2)}) collective-permute-start(bf16[63,2048]{1,0:T(8,128)(2,1)S(1)} %slice_bitcast_fusion.5), channel_id=1, source_target_pairs={{1,0},{2,1},{3,2},{4,3},{5,4},{6,5},{7,6},{8,7},{9,8},{10,9},{11,1... | collective-permute-start | bytes 774152 | tf_op jit(solution)/shard_map/ppermute | solution.py:16

commit v12 on v11

--- a/solution.py
+++ b/solution.py
@@ -173,13 +173,15 @@
         gather_kernel,
         out_shape=jax.ShapeDtypeStruct((groups, 2) + block_shape, keys.dtype),
         in_specs=[pl.BlockSpec(memory_space=pl.ANY), pl.BlockSpec(memory_space=pl.ANY)],
-        out_specs=pl.BlockSpec(memory_space=pl.ANY),
+        out_specs=pl.BlockSpec(memory_space=pltpu.VMEM),
         scratch_shapes=[
             pltpu.SemaphoreType.DMA((2, ahead, 2)),
             pltpu.SemaphoreType.DMA((2, ahead, 2)),
             pltpu.SemaphoreType.DMA((2,)),
         ],
-        compiler_params=pltpu.CompilerParams(collective_id=0, has_side_effects=True),
+        compiler_params=pltpu.CompilerParams(
+            collective_id=0, has_side_effects=True, vmem_limit_bytes=60 * 1024 * 1024
+        ),
     )(keys, values)
 
 

time: 436 us -> 440 us (level)
  Pallas kernels: 417 us -> 422 us
    pallas_call x1, Pallas kernels: 196 us -> 201 us  [ring_gather(): pl.pallas_call(gather_kernel, out_shape=jax.ShapeDtypeStruct((groups, 2)...]
  transfers between devices with their start and end apart: 2 -> 2, of which waited for: 0 -> 0; matrix products, arithmetic and copies ran while one was open for 1% -> 1% of each run, Pallas kernels for 45% -> 46%
where the time goes in v12:
time: 440 us; the launch traced here: 439 us
  Pallas kernels  422 us (96%)
  starting transfers between devices  7.21 us (2%)
  local copies, waits for them, and re-layouts  5.93 us (1%)
    pallas_call x1, Pallas kernels, ring_gather(): pl.pallas_call(gather_kernel, out_shape=jax.ShapeDtypeStruct((groups, 2)...  201 us
    pallas_call x1, Pallas kernels, ring_reduce(): pl.pallas_call(reduce_kernel, out_shape=jax.ShapeDtypeStruct(block, terms...  182 us
    pallas_call x1, Pallas kernels, span_attention(): pl.pallas_call(span_kernel, grid_spec=pltpu.PrefetchScalarGridSpec(num_sc...  38.7 us
  transfers between devices with their start and end apart: 2, of which 0 were waited for; matrix products, arithmetic and copies ran while one was open for 1% of the time, Pallas kernels for 46%

profile of v12, /device:TPU:6, one launch (start us, length us, event | category | flops | bytes accessed | tf_op | source)
XLA Modules:
  0.0 438.8 jit_solution(4974422056264461428)
XLA Ops:
  0.6 0.0 copy-start
  0.6 0.0 copy-start.1
  0.7 1.1 slice_bitcast_fusion.4
  1.7 4.6 %collective-permute-start.1 = (bf16[63,2048]{1,0:T(8,128)(2,1)S(1)}, bf16[63,2048]{1,0:T(8,128)(2,1)S(1)}, u32[]{:S(2)}, u32[]{:S(2)}) collective-permute-start(bf16[63,2048]{1,0:T(8,128)(2,1)S(1)} %slice_bitcast_fusion.4), channel_id=1, source_target_pairs={{1,0},{2,1},{3,2},{4,3},{5,4},{6,5},{7,6},{8,7},{9,8},{10,9},{11,1... | collective-permute-start | bytes 774152 | tf_op jit(solution)/shard_map/ppermute | solution.py:16
  6.3 1.0 slice_bitcast_fusion.5
  7.3 2.6 collective-permute-start
  9.9 1.3 slice_bitcast_fusion.1
  11.3 0.0 copy-done
  11.3 0.2 slice_bitcast_fusion
  11.5 0.0 copy-done.1
  11.5 0.1 sub.11
  11.6 0.5 and_select_fusion.slot_ref
  12.1 200.9 %shard_map.76.block_ref = bf16[16,2,128,2048]{3,2,1,0:T(8,128)(2,1)} custom-call(bf16[1,1,128,2048]{3,2,1,0:T(8,128)(2,1)} %key_ref.1, bf16[1,1,128,2048]{3,2,1,0:T(8,128)(2,1)} %value_ref.1), custom_call_target="tpu_custom_call" | custom-call | tf_op jit(solution)/shard_map/pallas_call | solution.py:172
  213.1 0.0 collective-permute-done
  213.1 1.1 pad_maximum_fusion
  214.2 0.0 collective-permute-done.1
  214.2 1.1 pad_maximum_fusion.1
  215.3 38.7 %shard_map.77 = (bf16[4,64,2048]{2,1,0:T(8,128)(2,1)}, bf16[16,2,128,2048]{3,2,1,0:T(8,128)(2,1)}) custom-call(s32[16]{0:T(128)} %and_select_fusion.slot_ref, bf16[4,64,2048]{2,1,0:T(8,128)(2,1)} %bitcast.15, bf16[4,64,2048]{2,1,0:T(8,128)(2,1)} %bitcast.16, bf16[16,2,128,2048]{3,2,1,0:T(8,128)(2,1)} %shard_map.76.block_ref), custom_call_target="tpu_custom_call" | custom-call | flops 4831838208 | bytes 36700160 | tf_op jit(solution)/shard_map/pallas_call | solution.py:93
  254.0 182.5 %shard_map.78 = bf16[2,128,2048]{2,1,0:T(8,128)(2,1)} custom-call(bf16[16,2,128,2048]{3,2,1,0:T(8,128)(2,1)} %get-tuple-element.6.term_ref), custom_call_target="tpu_custom_call" | custom-call | tf_op jit(solution)/shard_map/pallas_call | solution.py:263
  436.5 2.3 slice_bitcast_fusion.2
  (1 shorter events, 0.0 us)
Async XLA Ops:
  0.6 10.6 %copy-start = (bf16[1,256,2048]{2,1,0:T(8,128)(2,1)S(1)}, bf16[1,256,2048]{2,1,0:T(8,128)(2,1)}, u32[]{:S(2)}) copy-start(bf16[1,256,2048]{2,1,0:T(8,128)(2,1)} %param.6) | copy-start | bytes 3145732
  0.6 10.8 %copy-start.1 = (s32[1,4,4]{2,1,0:T(4,128)S(1)}, s32[1,4,4]{2,1,0:T(4,128)}, u32[]{:S(2)}) copy-start(s32[1,4,4]{2,1,0:T(4,128)} %param.9) | copy-start | bytes 196
  1.7 212.4 %collective-permute-start.1 = (bf16[63,2048]{1,0:T(8,128)(2,1)S(1)}, bf16[63,2048]{1,0:T(8,128)(2,1)S(1)}, u32[]{:S(2)}, u32[]{:S(2)}) collective-permute-start(bf16[63,2048]{1,0:T(8,128)(2,1)S(1)} %slice_bitcast_fusion.4), channel_id=1, source_target_pairs={{1,0},{2,1},{3,2},{4,3},{5,4},{6,5},{7,6},{8,7},{9,8},{10,9},{11,1... | collective-permute-start | bytes 774152 | tf_op jit(solution)/shard_map/ppermute | solution.py:16
  7.3 205.7 %collective-permute-start = (bf16[63,2048]{1,0:T(8,128)(2,1)S(1)}, bf16[63,2048]{1,0:T(8,128)(2,1)S(1)}, u32[]{:S(2)}, u32[]{:S(2)}) collective-permute-start(bf16[63,2048]{1,0:T(8,128)(2,1)S(1)} %slice_bitcast_fusion.5), channel_id=1, source_target_pairs={{1,0},{2,1},{3,2},{4,3},{5,4},{6,5},{7,6},{8,7},{9,8},{10,9},{11,1... | collective-permute-start | bytes 774152 | tf_op jit(solution)/shard_map/ppermute | solution.py:16

commit v13 on v11

--- a/solution.py
+++ b/solution.py
@@ -17,15 +17,21 @@
 
 
 def span_kernel(slot_ref, query_ref, grad_ref, block_ref, window_ref, term_ref):
+    for head in range(query_ref.shape[-1] // HEAD):
+        cols = pl.ds(head * HEAD, HEAD)
+        head_kernel(slot_ref, query_ref, grad_ref, block_ref, window_ref, term_ref, cols)
+
+
+def head_kernel(slot_ref, query_ref, grad_ref, block_ref, window_ref, term_ref, cols):
     scale = HEAD ** (-0.5)
     contract_last = (((1,), (1,)), ((), ()))
     plain = (((1,), (0,)), ((), ()))
     for span in range(query_ref.shape[0]):
-        query = query_ref[span]
-        grad = grad_ref[span]
+        query = query_ref[span, :, cols]
+        grad = grad_ref[span, :, cols]
         slots = [slot_ref[span * NBRS + j] for j in range(NBRS)]
-        keys = jnp.concatenate([block_ref[slot, 0] for slot in slots], axis=0)
-        values = jnp.concatenate([block_ref[slot, 1] for slot in slots], axis=0)
+        keys = jnp.concatenate([block_ref[slot, 0, :, cols] for slot in slots], axis=0)
+        values = jnp.concatenate([block_ref[slot, 1, :, cols] for slot in slots], axis=0)
         scores = lax.dot_general(query, keys, contract_last, preferred_element_type=jnp.float32) * scale
         grad_probs = lax.dot_general(grad, values, contract_last, preferred_element_type=jnp.float32)
         maxes, totals, dots = [], [], []
@@ -63,7 +69,7 @@
                 preferred_element_type=jnp.float32,
             )
             window = window + (part * scale).astype(jnp.bfloat16).astype(jnp.float32)
-        window_ref[span] = window.astype(window_ref.dtype)
+        window_ref[span, :, cols] = window.astype(window_ref.dtype)
         contract_first = (((0,), (0,)), ((), ()))
         value_term = lax.dot_general(
             probs.astype(jnp.bfloat16), grad, contract_first, preferred_element_type=jnp.float32
@@ -73,14 +79,15 @@
             * scale
         )
         for j in range(NBRS):
-            term_ref[slots[j], 0] = key_term[j * HEAD : (j + 1) * HEAD].astype(term_ref.dtype)
-            term_ref[slots[j], 1] = value_term[j * HEAD : (j + 1) * HEAD].astype(term_ref.dtype)
+            term_ref[slots[j], 0, :, cols] = key_term[j * HEAD : (j + 1) * HEAD].astype(term_ref.dtype)
+            term_ref[slots[j], 1, :, cols] = value_term[j * HEAD : (j + 1) * HEAD].astype(term_ref.dtype)
 
 
 def span_attention(pair_slot, window_query, window_grad, blocks):
     span_count, span_len, row_width = window_query.shape
     slot_count, _, block_len, _ = blocks.shape
     head_count = row_width // HEAD
+    width = 2 * HEAD
     pair_count = span_count * NBRS
 
     def window_map(h, slots):
@@ -94,15 +101,15 @@
         span_kernel,
         grid_spec=pltpu.PrefetchScalarGridSpec(
             num_scalar_prefetch=1,
-            grid=(head_count,),
+            grid=(row_width // width,),
             in_specs=[
-                pl.BlockSpec((span_count, span_len, HEAD), window_map),
-                pl.BlockSpec((span_count, span_len, HEAD), window_map),
-                pl.BlockSpec((slot_count, 2, block_len, HEAD), block_map),
+                pl.BlockSpec((span_count, span_len, width), window_map),
+                pl.BlockSpec((span_count, span_len, width), window_map),
+                pl.BlockSpec((slot_count, 2, block_len, width), block_map),
             ],
             out_specs=[
-                pl.BlockSpec((span_count, span_len, HEAD), window_map),
-                pl.BlockSpec((pair_count, 2, block_len, HEAD), block_map),
+                pl.BlockSpec((span_count, span_len, width), window_map),
+                pl.BlockSpec((pair_count, 2, block_len, width), block_map),
             ],
         ),
         out_shape=[

time: 436 us -> 436 us (level)
  no operation moved by 1% of the time
where the time goes in v13:
time: 436 us; the launch traced here: 433 us
  Pallas kernels  417 us (96%)
  starting transfers between devices  7.21 us (2%)
  local copies, waits for them, and re-layouts  5.93 us (1%)
    pallas_call x1, Pallas kernels, ring_gather(): pl.pallas_call(gather_kernel, out_shape=jax.ShapeDtypeStruct((groups, 2)...  196 us
    pallas_call x1, Pallas kernels, ring_reduce(): pl.pallas_call(reduce_kernel, out_shape=jax.ShapeDtypeStruct(block, terms...  182 us
    pallas_call x1, Pallas kernels, span_attention(): pl.pallas_call(span_kernel, grid_spec=pltpu.PrefetchScalarGridSpec(num_sc...  38.4 us
  transfers between devices with their start and end apart: 2, of which 0 were waited for; matrix products, arithmetic and copies ran while one was open for 1% of the time, Pallas kernels for 45%

profile of v13, /device:TPU:6, one launch (start us, length us, event | category | flops | bytes accessed | tf_op | source)
XLA Modules:
  0.0 433.2 jit_solution(7565502690958971435)
XLA Ops:
  0.6 0.0 copy-start
  0.6 0.0 copy-start.1
  0.7 1.1 slice_bitcast_fusion.4
  1.7 4.6 %collective-permute-start.1 = (bf16[63,2048]{1,0:T(8,128)(2,1)S(1)}, bf16[63,2048]{1,0:T(8,128)(2,1)S(1)}, u32[]{:S(2)}, u32[]{:S(2)}) collective-permute-start(bf16[63,2048]{1,0:T(8,128)(2,1)S(1)} %slice_bitcast_fusion.4), channel_id=1, source_target_pairs={{1,0},{2,1},{3,2},{4,3},{5,4},{6,5},{7,6},{8,7},{9,8},{10,9},{11,1... | collective-permute-start | bytes 774152 | tf_op jit(solution)/shard_map/ppermute | solution.py:16
  6.3 1.0 slice_bitcast_fusion.5
  7.3 2.6 collective-permute-start
  9.9 1.3 slice_bitcast_fusion.1
  11.3 0.0 copy-done
  11.3 0.2 slice_bitcast_fusion
  11.5 0.0 copy-done.1
  11.5 0.1 sub.11
  11.6 0.5 and_select_fusion.slot_ref
  12.1 196.2 %shard_map.76.block_ref = bf16[16,2,128,2048]{3,2,1,0:T(8,128)(2,1)} custom-call(bf16[1,1,128,2048]{3,2,1,0:T(8,128)(2,1)} %key_ref.1, bf16[1,1,128,2048]{3,2,1,0:T(8,128)(2,1)} %value_ref.1), custom_call_target="tpu_custom_call" | custom-call | tf_op jit(solution)/shard_map/pallas_call | solution.py:179
  208.4 0.0 collective-permute-done
  208.4 1.1 pad_maximum_fusion
  209.5 0.0 collective-permute-done.1
  209.5 1.1 pad_maximum_fusion.1
  210.6 38.4 %shard_map.77 = (bf16[4,64,2048]{2,1,0:T(8,128)(2,1)}, bf16[16,2,128,2048]{3,2,1,0:T(8,128)(2,1)}) custom-call(s32[16]{0:T(128)} %and_select_fusion.slot_ref, bf16[4,64,2048]{2,1,0:T(8,128)(2,1)} %bitcast.15, bf16[4,64,2048]{2,1,0:T(8,128)(2,1)} %bitcast.16, bf16[16,2,128,2048]{3,2,1,0:T(8,128)(2,1)} %shard_map.76.block_ref), custom_call_target="tpu_custom_call" | custom-call | flops 4831838208 | bytes 36700160 | tf_op jit(solution)/shard_map/pallas_call | solution.py:100
  249.0 181.9 %shard_map.78 = bf16[2,128,2048]{2,1,0:T(8,128)(2,1)} custom-call(bf16[16,2,128,2048]{3,2,1,0:T(8,128)(2,1)} %get-tuple-element.6.term_ref), custom_call_target="tpu_custom_call" | custom-call | tf_op jit(solution)/shard_map/pallas_call | solution.py:268
  430.9 2.3 slice_bitcast_fusion.2
  (1 shorter events, 0.0 us)
Async XLA Ops:
  0.6 10.6 %copy-start = (bf16[1,256,2048]{2,1,0:T(8,128)(2,1)S(1)}, bf16[1,256,2048]{2,1,0:T(8,128)(2,1)}, u32[]{:S(2)}) copy-start(bf16[1,256,2048]{2,1,0:T(8,128)(2,1)} %param.6) | copy-start | bytes 3145732
  0.6 10.8 %copy-start.1 = (s32[1,4,4]{2,1,0:T(4,128)S(1)}, s32[1,4,4]{2,1,0:T(4,128)}, u32[]{:S(2)}) copy-start(s32[1,4,4]{2,1,0:T(4,128)} %param.9) | copy-start | bytes 196
  1.7 207.7 %collective-permute-start.1 = (bf16[63,2048]{1,0:T(8,128)(2,1)S(1)}, bf16[63,2048]{1,0:T(8,128)(2,1)S(1)}, u32[]{:S(2)}, u32[]{:S(2)}) collective-permute-start(bf16[63,2048]{1,0:T(8,128)(2,1)S(1)} %slice_bitcast_fusion.4), channel_id=1, source_target_pairs={{1,0},{2,1},{3,2},{4,3},{5,4},{6,5},{7,6},{8,7},{9,8},{10,9},{11,1... | collective-permute-start | bytes 774152 | tf_op jit(solution)/shard_map/ppermute | solution.py:16
  7.3 201.0 %collective-permute-start = (bf16[63,2048]{1,0:T(8,128)(2,1)S(1)}, bf16[63,2048]{1,0:T(8,128)(2,1)S(1)}, u32[]{:S(2)}, u32[]{:S(2)}) collective-permute-start(bf16[63,2048]{1,0:T(8,128)(2,1)S(1)} %slice_bitcast_fusion.5), channel_id=1, source_target_pairs={{1,0},{2,1},{3,2},{4,3},{5,4},{6,5},{7,6},{8,7},{9,8},{10,9},{11,1... | collective-permute-start | bytes 774152 | tf_op jit(solution)/shard_map/ppermute | solution.py:16
